TPU v7x, 256 devices: a whole 4x4x8 slice. The times are simulated.
256 devices in a mesh: vert: 16 (over x, z_hi), tm: 16 (over y, z_lo, core).
Axes of the slice: x: 4, y: 4, z: 8 (z_hi: 4, z_lo: 2; z = z_hi * 2 + z_lo), core: 2. Of those that a mesh axis runs over, the one named last changes fastest.
Arguments:
- source: bfloat16 [20480, 2048], P('vert', 'tm'), may hold values from -6 to 6
- band_taps: bfloat16 [2, 2, 65], replicated, may hold values from -0.75 to 0.75
- smooth_taps: bfloat16 [2, 65], replicated, may hold values from 0.0009 to 0.031
- parcel_ids: int32 [3, 20480], P(None, 'vert'), may hold values from 0 to 999, as said below
Outputs:
- envelope_coupling: float32 [16, 2, 1504, 1504], P('tm', None, 'vert')
Inputs may be any that keep to these rules, and one draw needn't show every extreme that they name: `parcel_ids`: row r = 0, 1, 2 gives each vertex's parcel in the atlas of 100, 400 or 1000 parcels (values below that count); every parcel of each atlas has at least one vertex.
All inputs are finite; a program needn't handle non-finite values.
Results may differ from a plain program's by a relative error of at most 0.0053.
Values may be sent and summed in bfloat16 or wider, within the bound.
A program may use at most 64 MiB of HBM per device.

v0:
```python
from functools import partial
import math

import jax
import jax.numpy as jnp
from jax import lax
from jax.sharding import PartitionSpec as P

P1 = 100
P2 = 400
P3 = 1000
BANDS = 2
TAPS = 65
HALF = 32
LAG = 64
LAG_STEP = 1
NLAG = 129


EPSILON = 1e-05


def extended_2(cells, sides, width):
    for axis, dim in sides:
        count = lax.axis_size(axis)
        ends = count - 1
        head = lax.slice_in_dim(cells, 0, width, axis=dim)
        tail = lax.slice_in_dim(cells, cells.shape[dim] - width, cells.shape[dim], axis=dim)
        cells = jnp.concatenate(
            [
                lax.ppermute(tail, axis, [(i, (i + 1) % count) for i in range(ends)]),
                cells,
                lax.ppermute(head, axis, [((i + 1) % count, i) for i in range(ends)]),
            ],
            axis=dim,
        )
    return cells


def toeplitz_band(taps, n_out, n_in):
    period = jnp.concatenate([taps, jnp.zeros((n_in + 1 - taps.shape[0],), taps.dtype)])
    return jnp.tile(period, n_out)[: n_out * n_in].reshape(n_out, n_in)


def resolution_of(parcel):
    first = (parcel >= P1).astype(jnp.int32)
    second = (parcel >= P1 + P2).astype(jnp.int32)
    third = (parcel >= P1 + P2 + P3).astype(jnp.int32)
    return first + second + third


def centered_rows(extended, length):
    level_mean = jnp.mean(extended[:, :, LAG : LAG + length], axis=2, keepdims=True)
    centered = (extended - level_mean).astype(jnp.bfloat16)
    middle = centered[:, :, LAG : LAG + length]
    middle_wide = middle.astype(jnp.float32)
    spread = lax.rsqrt(jnp.mean(middle_wide * middle_wide, axis=2) + EPSILON)
    return (centered, middle, spread)


def make_fold(own_middle, own_spread, owner_start, par_dev, t_dev):
    kernel = own_middle.transpose(1, 0, 2).reshape(BANDS * par_dev, 1, t_dev)
    own_level = resolution_of(owner_start + lax.iota(jnp.int32, par_dev))

    def block_value(visiting, first):
        vis_middle = visiting[:, :, LAG : LAG + t_dev].astype(jnp.float32)
        vis_spread = lax.rsqrt(jnp.mean(vis_middle * vis_middle, axis=2) + EPSILON)
        inner = lax.conv_general_dilated(
            visiting,
            kernel,
            (LAG_STEP,),
            "VALID",
            dimension_numbers=("NCH", "OIH", "NCH"),
            feature_group_count=BANDS,
            preferred_element_type=jnp.float32,
        )
        inner = inner.reshape(par_dev, BANDS, par_dev, NLAG)
        energy = jnp.sum(inner * inner, axis=3).transpose(1, 2, 0)
        scale = own_spread.T[:, :, None] * vis_spread.T[:, None, :] / t_dev
        vis_level = resolution_of(first + lax.iota(jnp.int32, par_dev))
        same = ((own_level[:, None] == vis_level[None, :]) & (own_level[:, None] < 3)).astype(
            jnp.float32
        )
        return energy * scale * scale * same[None] / NLAG

    def guarded(visiting, first):
        result = block_value(visiting, first)
        return result

    def fold_rows(carry, piece, start):
        count = piece.shape[0] // par_dev

        def add_block(block_idx, total):
            first = block_idx * par_dev
            visiting = lax.dynamic_slice_in_dim(piece, block_idx * par_dev, par_dev, 0)
            slot = first // par_dev
            zero = jnp.int32(0)
            return lax.dynamic_update_slice(
                total, guarded(visiting, first)[None], (slot, zero, zero, zero)
            )

        return lax.fori_loop(0, count, add_block, carry)

    return fold_rows


def local(source, band_taps, smooth_taps, parcel_ids):
    vert_dev, t_dev = source.shape
    owners = lax.axis_size("vert")
    total_par = (P1 + P2 + P3 + owners - 1) // owners * owners
    par_dev = total_par // owners
    n_mid = t_dev + 2 * HALF
    n_in = t_dev + 4 * HALF
    first_rows = jax.vmap(partial(toeplitz_band, n_out=n_mid, n_in=n_in))(
        band_taps.reshape(2 * BANDS, TAPS)
    )
    first_mat = first_rows.transpose(2, 0, 1).reshape(n_in, 2 * BANDS * n_mid)
    second_rows = jax.vmap(partial(toeplitz_band, n_out=t_dev, n_in=n_mid))(smooth_taps)
    second_mat = second_rows.transpose(0, 2, 1)
    widened = extended_2(source, (("tm", 1),), 2 * HALF)
    block_rows = math.gcd(vert_dev, 128)

    def filter_block(block):
        wave = jnp.dot(block, first_mat, preferred_element_type=jnp.float32).reshape(
            block_rows, 2, BANDS, n_mid
        )
        power = (wave[:, 0] * wave[:, 0] + wave[:, 1] * wave[:, 1]).astype(jnp.bfloat16)
        return jnp.einsum(
            "vbu,but->vbt", power, second_mat, preferred_element_type=jnp.float32
        ).astype(jnp.bfloat16)

    envelope = lax.map(filter_block, widened.reshape(vert_dev // block_rows, block_rows, n_in))
    flat_env = envelope.reshape(vert_dev, BANDS * t_dev)
    offsets = jnp.array([0, P1, P1 + P2], dtype=jnp.int32)
    global_ids = parcel_ids + offsets[:, None]
    owner_start = lax.axis_index("vert") * par_dev
    empty = jnp.zeros((owners, BANDS, par_dev, par_dev), jnp.float32)

    def one_block(block_idx):
        wanted = block_idx * par_dev + lax.iota(jnp.int32, par_dev)
        hits = jnp.sum(
            (global_ids[:, None, :] == wanted[None, :, None]).astype(jnp.bfloat16), axis=0
        )
        return jnp.dot(hits, flat_env, preferred_element_type=jnp.float32)

    pooled = lax.map(
        one_block, jnp.arange(par_dev * lax.axis_size("vert") // par_dev, dtype=jnp.int32)
    )
    own_sums = lax.psum_scatter(
        pooled.reshape(par_dev * lax.axis_size("vert"), BANDS * t_dev),
        "vert",
        scatter_dimension=0,
        tiled=True,
    )
    own_env = own_sums.reshape(par_dev, BANDS, t_dev)
    own_ext = extended_2(own_env, (("tm", 2),), LAG)
    centered, own_middle, own_spread = centered_rows(own_ext, t_dev)
    fold_rows = make_fold(own_middle, own_spread, owner_start, par_dev, t_dev)
    blocks = fold_rows(empty, lax.all_gather(centered, "vert", axis=0, tiled=True), jnp.int32(0))
    coupling = blocks.transpose(1, 2, 0, 3).reshape(BANDS, par_dev, total_par)
    return coupling[None]


def solution(mesh):
    return jax.shard_map(
        local,
        mesh=mesh,
        in_specs=(P("vert", "tm"), P(), P(), P(None, "vert")),
        out_specs=P("tm", None, "vert", None),
        check_vma=False,
    )
```

profile of v0, /device:TPU:8, one launch (start us, length us, event | category | flops | bytes accessed | tf_op | source)
XLA Modules:
  0.0 327.7 jit_solution(10390628284923040536)
XLA Ops:
  6.5 2.0 fusion.27
  8.5 1.9 collective-permute-start
  10.4 4.5 %collective-permute-start.1 = (bf16[1280,64]{1,0:T(8,128)(2,1)S(1)}, bf16[1280,64]{1,0:T(8,128)(2,1)}, u32[]{:S(2)}, u32[]{:S(2)}) collective-permute-start(bf16[1280,64]{1,0:T(8,128)(2,1)S(1)} %get-tuple-element.349), channel_id=1, source_target_pairs={{1,0},{2,1},{3,2},{4,3},{5,4},{6,5},{7,6},{8,7},{9,8},{10,9},{11,1... | collective-permute-start | bytes 491528 | tf_op jit(solution)/shard_map/ppermute | solution.py:33
  18.6 1.4 collective-permute-done.1
  20.0 1.5 pad_maximum_fusion
  21.5 12.1 %while.38 = (s32[]{:T(128)}, bf16[10,128,2,128]{3,2,1,0:T(2,128)(2,1)}, bf16[10,128,256]{2,1,0:T(8,128)(2,1)S(1)}, bf16[256,768]{0,1:T(8,128)(2,1)S(1)}, bf16[2,192,128]{2,1,0:T(8,128)(2,1)S(1)}, /*index=5*/s32[]{:T(128)}) while((s32[]{:T(128)}, bf16[10,128,2,128]{3,2,1,0:T(2,128)(2,1)}, bf16[10,128,256]{2,1,0:T(8,128)(2,1)S(1)}, ...), condition=%wide.region_1.2_spmd, body=%wide.region_0.1_spmd.sunk | while | flops 63143936 | bytes 1540681 | solution.py:132
  33.6 1.2 copy.58
  34.8 27.9 %while.39 = (s32[]{:T(128)}, f32[16,94,256]{2,1,0:T(8,128)S(1)}, s32[3,1280]{1,0:T(4,128)S(1)}, s32[16]{0:T(128)S(1)}, bf16[1280,256]{1,0:T(8,128)(2,1)S(1)}, /*index=5*/s32[]{:T(128)}, s32[1]{0:T(128)}) while((s32[]{:T(128)}, f32[16,94,256]{2,1,0:T(8,128)S(1)}, s32[3,1280]{1,0:T(4,128)S(1)}, s32[16]{0:T(128)S(1)}, ...), condition=%wide.region_4.5_spmd, body=%wide.region_2.4_spmd.sunk | while | flops 62566496 | bytes 1256285 | solution.py:146
  62.9 63.4 %fusion.2 = f32[96,256]{1,0:T(8,128)S(1)} fusion(f32[1504,256]{1,0:T(8,128)S(1)} %reshape.143), kind=kCustom, calls=%all-reduce-scatter | all-reduce-scatter fusion | flops 393217 | bytes 1639424
  126.3 4.2 %collective-permute-start.4 = (f32[30,256]{1,0:T(8,128)S(1)}, f32[30,256]{1,0:T(8,128)S(1)}, u32[]{:S(2)}, u32[]{:S(2)}) collective-permute-start(f32[30,256]{1,0:T(8,128)S(1)} %slice.55), channel_id=1, source_target_pairs={{0,16},{16,32},{32,48},{48,64},{64,80},{80,96},{96,112},{112,128},... | collective-permute-start | bytes 92168
  132.6 1.9 collective-permute-start.2
  134.5 4.7 %collective-permute-start.3 = (f32[94,2,64]{2,1,0:T(2,128)S(1)}, f32[94,2,64]{2,1,0:T(2,128)S(1)}, u32[]{:S(2)}, u32[]{:S(2)}) collective-permute-start(f32[94,2,64]{2,1,0:T(2,128)S(1)} %get-tuple-element.351), channel_id=1, source_target_pairs={{1,0},{2,1},{3,2},{4,3},{5,4},{6,5},{7,6},{8,7},{9,8},{10,9},{11,1... | collective-permute-start | bytes 144392 | tf_op jit(solution)/shard_map/ppermute | solution.py:33
  139.4 1.8 collective-permute-done.3
  141.2 1.1 fusion.26
  142.3 1.0 slice_bitcast_fusion
  143.6 1.1 multiply_reduce_fusion.2
  145.4 51.5 %all-gather.2.cloned.1.call-done = bf16[1504,2,256]{2,1,0:T(2,128)(2,1)} async-done(((bf16[94,2,256]{2,1,0:T(2,128)(2,1)}), bf16[1504,2,256]{2,1,0:T(2,128)(2,1)}) %all-gather.2.cloned.1.call-update) | async-done | bytes 1540112 | tf_op jit(solution)/shard_map/all_gather | solution.py:159
  196.9 1.3 broadcast_in_dim.52
  198.3 117.5 %while.40 = (s32[]{:T(128)}, f32[16,2,94,94]{3,2,1,0:T(8,128)}, bf16[1504,2,256]{2,1,0:T(2,128)(2,1)}, bf16[188,1,128]{0,2,1:T(8,128)(2,1)S(1)}, f32[94,2]{0,1:T...) while((s32[]{:T(128)}, f32[16,2,94,94]{3,2,1,0:T(8,128)}, ...), condition=%wide.region_11.12_spmd.clone, body=%wide.region_8.11_spmd.clone.sunk | while | flops 1172045696 | bytes 1180199 | solution.py:102
  198.3 1.0 constant_dynamic-slice_fusion.3
  199.4 4.9 %multiply_reduce_fusion.5 = f32[94,188]{1,0:T(8,128)S(1)} fusion(bf16[94,2,256]{0,1,2:T(2,128)(2,1)S(1)} %copy.64, s32[188]{0:T(256)S(1)} %get-tuple-element.532, bf16[188,128]{0,1:T(8,128)(2,1)S(1)} %bitcast.104), kind=kOutput, calls=%fused_computation.18.clone.1 | convolution fusion | flops 1171838208 | bytes 215824 | tf_op jit(solution)/shard_map/while/body/eval_jaxpr/conv_general_dilated | solution.py:68
  205.6 1.0 constant_dynamic-slice_fusion.3
  206.7 4.9 %multiply_reduce_fusion.5 = f32[94,188]{1,0:T(8,128)S(1)} fusion(bf16[94,2,256]{0,1,2:T(2,128)(2,1)S(1)} %copy.64, s32[188]{0:T(256)S(1)} %get-tuple-element.532, bf16[188,128]{0,1:T(8,128)(2,1)S(1)} %bitcast.104), kind=kOutput, calls=%fused_computation.18.clone.1 | convolution fusion | flops 1171838208 | bytes 215824 | tf_op jit(solution)/shard_map/while/body/eval_jaxpr/conv_general_dilated | solution.py:68
  213.0 1.0 constant_dynamic-slice_fusion.3
  214.1 4.9 %multiply_reduce_fusion.5 = f32[94,188]{1,0:T(8,128)S(1)} fusion(bf16[94,2,256]{0,1,2:T(2,128)(2,1)S(1)} %copy.64, s32[188]{0:T(256)S(1)} %get-tuple-element.532, bf16[188,128]{0,1:T(8,128)(2,1)S(1)} %bitcast.104), kind=kOutput, calls=%fused_computation.18.clone.1 | convolution fusion | flops 1171838208 | bytes 215824 | tf_op jit(solution)/shard_map/while/body/eval_jaxpr/conv_general_dilated | solution.py:68
  220.3 1.0 constant_dynamic-slice_fusion.3
  221.4 4.9 %multiply_reduce_fusion.5 = f32[94,188]{1,0:T(8,128)S(1)} fusion(bf16[94,2,256]{0,1,2:T(2,128)(2,1)S(1)} %copy.64, s32[188]{0:T(256)S(1)} %get-tuple-element.532, bf16[188,128]{0,1:T(8,128)(2,1)S(1)} %bitcast.104), kind=kOutput, calls=%fused_computation.18.clone.1 | convolution fusion | flops 1171838208 | bytes 215824 | tf_op jit(solution)/shard_map/while/body/eval_jaxpr/conv_general_dilated | solution.py:68
  227.6 1.0 constant_dynamic-slice_fusion.3
  228.8 4.9 %multiply_reduce_fusion.5 = f32[94,188]{1,0:T(8,128)S(1)} fusion(bf16[94,2,256]{0,1,2:T(2,128)(2,1)S(1)} %copy.64, s32[188]{0:T(256)S(1)} %get-tuple-element.532, bf16[188,128]{0,1:T(8,128)(2,1)S(1)} %bitcast.104), kind=kOutput, calls=%fused_computation.18.clone.1 | convolution fusion | flops 1171838208 | bytes 215824 | tf_op jit(solution)/shard_map/while/body/eval_jaxpr/conv_general_dilated | solution.py:68
  235.0 1.0 constant_dynamic-slice_fusion.3
  236.1 4.9 %multiply_reduce_fusion.5 = f32[94,188]{1,0:T(8,128)S(1)} fusion(bf16[94,2,256]{0,1,2:T(2,128)(2,1)S(1)} %copy.64, s32[188]{0:T(256)S(1)} %get-tuple-element.532, bf16[188,128]{0,1:T(8,128)(2,1)S(1)} %bitcast.104), kind=kOutput, calls=%fused_computation.18.clone.1 | convolution fusion | flops 1171838208 | bytes 215824 | tf_op jit(solution)/shard_map/while/body/eval_jaxpr/conv_general_dilated | solution.py:68
  242.3 1.0 constant_dynamic-slice_fusion.3
  243.5 4.9 %multiply_reduce_fusion.5 = f32[94,188]{1,0:T(8,128)S(1)} fusion(bf16[94,2,256]{0,1,2:T(2,128)(2,1)S(1)} %copy.64, s32[188]{0:T(256)S(1)} %get-tuple-element.532, bf16[188,128]{0,1:T(8,128)(2,1)S(1)} %bitcast.104), kind=kOutput, calls=%fused_computation.18.clone.1 | convolution fusion | flops 1171838208 | bytes 215824 | tf_op jit(solution)/shard_map/while/body/eval_jaxpr/conv_general_dilated | solution.py:68
  249.7 1.0 constant_dynamic-slice_fusion.3
  250.8 4.9 %multiply_reduce_fusion.5 = f32[94,188]{1,0:T(8,128)S(1)} fusion(bf16[94,2,256]{0,1,2:T(2,128)(2,1)S(1)} %copy.64, s32[188]{0:T(256)S(1)} %get-tuple-element.532, bf16[188,128]{0,1:T(8,128)(2,1)S(1)} %bitcast.104), kind=kOutput, calls=%fused_computation.18.clone.1 | convolution fusion | flops 1171838208 | bytes 215824 | tf_op jit(solution)/shard_map/while/body/eval_jaxpr/conv_general_dilated | solution.py:68
  257.0 1.0 constant_dynamic-slice_fusion.3
  258.1 4.9 %multiply_reduce_fusion.5 = f32[94,188]{1,0:T(8,128)S(1)} fusion(bf16[94,2,256]{0,1,2:T(2,128)(2,1)S(1)} %copy.64, s32[188]{0:T(256)S(1)} %get-tuple-element.532, bf16[188,128]{0,1:T(8,128)(2,1)S(1)} %bitcast.104), kind=kOutput, calls=%fused_computation.18.clone.1 | convolution fusion | flops 1171838208 | bytes 215824 | tf_op jit(solution)/shard_map/while/body/eval_jaxpr/conv_general_dilated | solution.py:68
  264.4 1.0 constant_dynamic-slice_fusion.3
  265.5 4.9 %multiply_reduce_fusion.5 = f32[94,188]{1,0:T(8,128)S(1)} fusion(bf16[94,2,256]{0,1,2:T(2,128)(2,1)S(1)} %copy.64, s32[188]{0:T(256)S(1)} %get-tuple-element.532, bf16[188,128]{0,1:T(8,128)(2,1)S(1)} %bitcast.104), kind=kOutput, calls=%fused_computation.18.clone.1 | convolution fusion | flops 1171838208 | bytes 215824 | tf_op jit(solution)/shard_map/while/body/eval_jaxpr/conv_general_dilated | solution.py:68
  272.9 4.9 %multiply_reduce_fusion.5 = f32[94,188]{1,0:T(8,128)S(1)} fusion(bf16[94,2,256]{0,1,2:T(2,128)(2,1)S(1)} %copy.64, s32[188]{0:T(256)S(1)} %get-tuple-element.532, bf16[188,128]{0,1:T(8,128)(2,1)S(1)} %bitcast.104), kind=kOutput, calls=%fused_computation.18.clone.1 | convolution fusion | flops 1171838208 | bytes 215824 | tf_op jit(solution)/shard_map/while/body/eval_jaxpr/conv_general_dilated | solution.py:68
  280.2 4.9 %multiply_reduce_fusion.5 = f32[94,188]{1,0:T(8,128)S(1)} fusion(bf16[94,2,256]{0,1,2:T(2,128)(2,1)S(1)} %copy.64, s32[188]{0:T(256)S(1)} %get-tuple-element.532, bf16[188,128]{0,1:T(8,128)(2,1)S(1)} %bitcast.104), kind=kOutput, calls=%fused_computation.18.clone.1 | convolution fusion | flops 1171838208 | bytes 215824 | tf_op jit(solution)/shard_map/while/body/eval_jaxpr/conv_general_dilated | solution.py:68
  287.5 4.9 %multiply_reduce_fusion.5 = f32[94,188]{1,0:T(8,128)S(1)} fusion(bf16[94,2,256]{0,1,2:T(2,128)(2,1)S(1)} %copy.64, s32[188]{0:T(256)S(1)} %get-tuple-element.532, bf16[188,128]{0,1:T(8,128)(2,1)S(1)} %bitcast.104), kind=kOutput, calls=%fused_computation.18.clone.1 | convolution fusion | flops 1171838208 | bytes 215824 | tf_op jit(solution)/shard_map/while/body/eval_jaxpr/conv_general_dilated | solution.py:68
  293.8 1.0 constant_dynamic-slice_fusion.3
  294.9 4.9 %multiply_reduce_fusion.5 = f32[94,188]{1,0:T(8,128)S(1)} fusion(bf16[94,2,256]{0,1,2:T(2,128)(2,1)S(1)} %copy.64, s32[188]{0:T(256)S(1)} %get-tuple-element.532, bf16[188,128]{0,1:T(8,128)(2,1)S(1)} %bitcast.104), kind=kOutput, calls=%fused_computation.18.clone.1 | convolution fusion | flops 1171838208 | bytes 215824 | tf_op jit(solution)/shard_map/while/body/eval_jaxpr/conv_general_dilated | solution.py:68
  302.2 4.9 %multiply_reduce_fusion.5 = f32[94,188]{1,0:T(8,128)S(1)} fusion(bf16[94,2,256]{0,1,2:T(2,128)(2,1)S(1)} %copy.64, s32[188]{0:T(256)S(1)} %get-tuple-element.532, bf16[188,128]{0,1:T(8,128)(2,1)S(1)} %bitcast.104), kind=kOutput, calls=%fused_computation.18.clone.1 | convolution fusion | flops 1171838208 | bytes 215824 | tf_op jit(solution)/shard_map/while/body/eval_jaxpr/conv_general_dilated | solution.py:68
  309.6 4.9 %multiply_reduce_fusion.5 = f32[94,188]{1,0:T(8,128)S(1)} fusion(bf16[94,2,256]{0,1,2:T(2,128)(2,1)S(1)} %copy.64, s32[188]{0:T(256)S(1)} %get-tuple-element.532, bf16[188,128]{0,1:T(8,128)(2,1)S(1)} %bitcast.104), kind=kOutput, calls=%fused_computation.18.clone.1 | convolution fusion | flops 1171838208 | bytes 215824 | tf_op jit(solution)/shard_map/while/body/eval_jaxpr/conv_general_dilated | solution.py:68
  315.8 2.3 copy.42
  318.1 2.8 broadcast_in_dim_reshape.3
  (316 shorter events, 62.0 us)
Async XLA Ops:
  6.5 190.4 %all-gather.2.cloned.1.call-start = ((), (), s32[]{:S(2)}) async-start(), calls=%async_computation | async-start | bytes 1636352 | tf_op jit(solution)/shard_map/all_gather | solution.py:159
  8.5 10.1 %collective-permute-start = (bf16[1280,64]{1,0:T(8,128)(2,1)}, bf16[1280,64]{1,0:T(8,128)(2,1)}, u32[]{:S(2)}, u32[]{:S(2)}) collective-permute-start(bf16[1280,64]{1,0:T(8,128)(2,1)} %get-tuple-element.348), channel_id=1, source_target_pairs={{0,1},{1,2},{2,3},{3,4},{4,5},{5,6},{6,7},{7,8},{8,9},{9,10},{10,1... | collective-permute-start | bytes 491528 | tf_op jit(solution)/shard_map/ppermute | solution.py:31
  10.4 9.6 %collective-permute-start.1 = (bf16[1280,64]{1,0:T(8,128)(2,1)S(1)}, bf16[1280,64]{1,0:T(8,128)(2,1)}, u32[]{:S(2)}, u32[]{:S(2)}) collective-permute-start(bf16[1280,64]{1,0:T(8,128)(2,1)S(1)} %get-tuple-element.349), channel_id=1, source_target_pairs={{1,0},{2,1},{3,2},{4,3},{5,4},{6,5},{7,6},{8,7},{9,8},{10,9},{11,1... | collective-permute-start | bytes 491528 | tf_op jit(solution)/shard_map/ppermute | solution.py:33
  16.5 1.1 copy-start.2
  16.5 3.5 %copy-start = (bf16[1280,128]{1,0:T(8,128)(2,1)S(1)}, bf16[1280,128]{1,0:T(8,128)(2,1)}, u32[]{:S(2)}) copy-start(bf16[1280,128]{1,0:T(8,128)(2,1)} %param.11) | copy-start | bytes 983044
  62.8 67.6 %copy-start.3 = (u32[256]{0:T(256)S(1)}, u32[256]{0:T(256)}, u32[]{:S(2)}) copy-start(u32[256]{0:T(256)} %constant.228) | copy-start | bytes 3076
  126.3 5.8 %collective-permute-start.4 = (f32[30,256]{1,0:T(8,128)S(1)}, f32[30,256]{1,0:T(8,128)S(1)}, u32[]{:S(2)}, u32[]{:S(2)}) collective-permute-start(f32[30,256]{1,0:T(8,128)S(1)} %slice.55), channel_id=1, source_target_pairs={{0,16},{16,32},{32,48},{48,64},{64,80},{80,96},{96,112},{112,128},... | collective-permute-start | bytes 92168
  132.4 65.9 %copy-start.4 = (s32[188]{0:T(256)S(1)}, s32[188]{0:T(256)}, u32[]{:S(2)}) copy-start(s32[188]{0:T(256)} %constant.197.clone.2) | copy-start | bytes 2260
  132.6 6.9 %collective-permute-start.2 = (f32[94,2,64]{2,1,0:T(2,128)S(1)}, f32[94,2,64]{2,1,0:T(2,128)S(1)}, u32[]{:S(2)}, u32[]{:S(2)}) collective-permute-start(f32[94,2,64]{2,1,0:T(2,128)S(1)} %get-tuple-element.350), channel_id=1, source_target_pairs={{0,1},{1,2},{2,3},{3,4},{4,5},{5,6},{6,7},{7,8},{8,9},{9,10},{10,1... | collective-permute-start | bytes 144392 | tf_op jit(solution)/shard_map/ppermute | solution.py:31
  134.5 6.7 %collective-permute-start.3 = (f32[94,2,64]{2,1,0:T(2,128)S(1)}, f32[94,2,64]{2,1,0:T(2,128)S(1)}, u32[]{:S(2)}, u32[]{:S(2)}) collective-permute-start(f32[94,2,64]{2,1,0:T(2,128)S(1)} %get-tuple-element.351), channel_id=1, source_target_pairs={{1,0},{2,1},{3,2},{4,3},{5,4},{6,5},{7,6},{8,7},{9,8},{10,9},{11,1... | collective-permute-start | bytes 144392 | tf_op jit(solution)/shard_map/ppermute | solution.py:33
  199.4 5.5 %copy-start.1 = (f32[94,2]{0,1:T(2,128)S(1)}, f32[94,2]{0,1:T(2,128)}, u32[]{:S(2)}) copy-start(f32[94,2]{0,1:T(2,128)} %get-tuple-element.524) | copy-start | bytes 2260 | tf_op jit(solution)/shard_map/while
  206.7 5.5 %copy-start.1 = (f32[94,2]{0,1:T(2,128)S(1)}, f32[94,2]{0,1:T(2,128)}, u32[]{:S(2)}) copy-start(f32[94,2]{0,1:T(2,128)} %get-tuple-element.524) | copy-start | bytes 2260 | tf_op jit(solution)/shard_map/while
  214.1 5.5 %copy-start.1 = (f32[94,2]{0,1:T(2,128)S(1)}, f32[94,2]{0,1:T(2,128)}, u32[]{:S(2)}) copy-start(f32[94,2]{0,1:T(2,128)} %get-tuple-element.524) | copy-start | bytes 2260 | tf_op jit(solution)/shard_map/while
  221.4 5.5 %copy-start.1 = (f32[94,2]{0,1:T(2,128)S(1)}, f32[94,2]{0,1:T(2,128)}, u32[]{:S(2)}) copy-start(f32[94,2]{0,1:T(2,128)} %get-tuple-element.524) | copy-start | bytes 2260 | tf_op jit(solution)/shard_map/while
  228.8 5.5 %copy-start.1 = (f32[94,2]{0,1:T(2,128)S(1)}, f32[94,2]{0,1:T(2,128)}, u32[]{:S(2)}) copy-start(f32[94,2]{0,1:T(2,128)} %get-tuple-element.524) | copy-start | bytes 2260 | tf_op jit(solution)/shard_map/while
  236.1 5.5 %copy-start.1 = (f32[94,2]{0,1:T(2,128)S(1)}, f32[94,2]{0,1:T(2,128)}, u32[]{:S(2)}) copy-start(f32[94,2]{0,1:T(2,128)} %get-tuple-element.524) | copy-start | bytes 2260 | tf_op jit(solution)/shard_map/while
  243.5 5.5 %copy-start.1 = (f32[94,2]{0,1:T(2,128)S(1)}, f32[94,2]{0,1:T(2,128)}, u32[]{:S(2)}) copy-start(f32[94,2]{0,1:T(2,128)} %get-tuple-element.524) | copy-start | bytes 2260 | tf_op jit(solution)/shard_map/while
  250.8 5.5 %copy-start.1 = (f32[94,2]{0,1:T(2,128)S(1)}, f32[94,2]{0,1:T(2,128)}, u32[]{:S(2)}) copy-start(f32[94,2]{0,1:T(2,128)} %get-tuple-element.524) | copy-start | bytes 2260 | tf_op jit(solution)/shard_map/while
  258.1 5.5 %copy-start.1 = (f32[94,2]{0,1:T(2,128)S(1)}, f32[94,2]{0,1:T(2,128)}, u32[]{:S(2)}) copy-start(f32[94,2]{0,1:T(2,128)} %get-tuple-element.524) | copy-start | bytes 2260 | tf_op jit(solution)/shard_map/while
  265.5 5.5 %copy-start.1 = (f32[94,2]{0,1:T(2,128)S(1)}, f32[94,2]{0,1:T(2,128)}, u32[]{:S(2)}) copy-start(f32[94,2]{0,1:T(2,128)} %get-tuple-element.524) | copy-start | bytes 2260 | tf_op jit(solution)/shard_map/while
  272.8 5.5 %copy-start.1 = (f32[94,2]{0,1:T(2,128)S(1)}, f32[94,2]{0,1:T(2,128)}, u32[]{:S(2)}) copy-start(f32[94,2]{0,1:T(2,128)} %get-tuple-element.524) | copy-start | bytes 2260 | tf_op jit(solution)/shard_map/while
  280.2 5.5 %copy-start.1 = (f32[94,2]{0,1:T(2,128)S(1)}, f32[94,2]{0,1:T(2,128)}, u32[]{:S(2)}) copy-start(f32[94,2]{0,1:T(2,128)} %get-tuple-element.524) | copy-start | bytes 2260 | tf_op jit(solution)/shard_map/while
  287.5 5.5 %copy-start.1 = (f32[94,2]{0,1:T(2,128)S(1)}, f32[94,2]{0,1:T(2,128)}, u32[]{:S(2)}) copy-start(f32[94,2]{0,1:T(2,128)} %get-tuple-element.524) | copy-start | bytes 2260 | tf_op jit(solution)/shard_map/while
  294.9 5.5 %copy-start.1 = (f32[94,2]{0,1:T(2,128)S(1)}, f32[94,2]{0,1:T(2,128)}, u32[]{:S(2)}) copy-start(f32[94,2]{0,1:T(2,128)} %get-tuple-element.524) | copy-start | bytes 2260 | tf_op jit(solution)/shard_map/while
  302.2 5.5 %copy-start.1 = (f32[94,2]{0,1:T(2,128)S(1)}, f32[94,2]{0,1:T(2,128)}, u32[]{:S(2)}) copy-start(f32[94,2]{0,1:T(2,128)} %get-tuple-element.524) | copy-start | bytes 2260 | tf_op jit(solution)/shard_map/while
  309.6 5.5 %copy-start.1 = (f32[94,2]{0,1:T(2,128)S(1)}, f32[94,2]{0,1:T(2,128)}, u32[]{:S(2)}) copy-start(f32[94,2]{0,1:T(2,128)} %get-tuple-element.524) | copy-start | bytes 2260 | tf_op jit(solution)/shard_map/while
Sparse Core Ops, SparseCore 0:
  142.4 54.4 all-gather.1
where the time goes:
time: 329 us; the launch traced here: 328 us
  matrix products  87.8 us (27%)
  blocking collectives  63.4 us (19%)
  waiting for transfers between devices  55.3 us (17%)
  local copies, waits for them, and re-layouts  52.7 us (16%)
  other arithmetic  24.8 us (8%)
  starting transfers between devices  17.3 us (5%)
  between operations  14.3 us (4%)
  loops' own time  12.1 us (4%)
    conv_general_dilated x16, matrix products, block_value(): lax.conv_general_dilated(visiting, kernel, (LAG_STEP,), 'VALID', dimensio...  79 us
    unnamed x1, blocking collectives  63.4 us
    all_gather x1, waiting for transfers between devices, local(): lax.all_gather(centered, 'vert', axis=0, tiled=True)  51.5 us
    dynamic_slice x32, local copies, waits for them, and re-layouts, add_block(): visiting = lax.dynamic_slice_in_dim(piece, block_idx * par_dev, par_dev, 0)  17.8 us
    dynamic_update_slice x16, other arithmetic, add_block(): lax.dynamic_update_slice(total, guarded(visiting, first)[None], (slot, ze...  11.8 us
    another operation x1, loops' own time, local(): lax.map(one_block, jnp.arange(par_dev * lax.axis_size('vert') // par_dev,...  11 us
    dynamic_slice x16, local copies, waits for them, and re-layouts, local(): lax.map(one_block, jnp.arange(par_dev * lax.axis_size('vert') // par_dev,...  9.38 us
    ppermute x2, starting transfers between devices, extended_2(): lax.ppermute(head, axis, [((i + 1) % count, i) for i in range(ends)])  9.26 us
  transfers between devices with their start and end apart: 6, of which 5 were waited for; matrix products, arithmetic and copies ran while one was open for 2% of the time, Pallas kernels for 0%

commit v1 on v0

v1 whole, which is shorter than its diff:
```python
from functools import partial
import math

import jax
import jax.numpy as jnp
from jax import lax
from jax.experimental import pallas as pl
from jax.experimental.pallas import tpu as pltpu
from jax.sharding import PartitionSpec as P

P1 = 100
P2 = 400
P3 = 1000
BANDS = 2
TAPS = 65
HALF = 32
LAG = 64
LAG_STEP = 1
NLAG = 129

EPSILON = 1e-05

ROW_PAD = 96
LAG_CHUNK = 4
LAG_PAD = 132
COL_TILE = 256


def extended_2(cells, sides, width):
    for axis, dim in sides:
        count = lax.axis_size(axis)
        ends = count - 1
        head = lax.slice_in_dim(cells, 0, width, axis=dim)
        tail = lax.slice_in_dim(cells, cells.shape[dim] - width, cells.shape[dim], axis=dim)
        cells = jnp.concatenate(
            [
                lax.ppermute(tail, axis, [(i, (i + 1) % count) for i in range(ends)]),
                cells,
                lax.ppermute(head, axis, [((i + 1) % count, i) for i in range(ends)]),
            ],
            axis=dim,
        )
    return cells


def toeplitz_band(taps, n_out, n_in):
    period = jnp.concatenate([taps, jnp.zeros((n_in + 1 - taps.shape[0],), taps.dtype)])
    return jnp.tile(period, n_out)[: n_out * n_in].reshape(n_out, n_in)


def resolution_of(parcel):
    first = (parcel >= P1).astype(jnp.int32)
    second = (parcel >= P1 + P2).astype(jnp.int32)
    third = (parcel >= P1 + P2 + P3).astype(jnp.int32)
    return first + second + third


def centered_rows(extended, length):
    level_mean = jnp.mean(extended[:, :, LAG : LAG + length], axis=2, keepdims=True)
    centered = (extended - level_mean).astype(jnp.bfloat16)
    middle = centered[:, :, LAG : LAG + length]
    middle_wide = middle.astype(jnp.float32)
    spread = lax.rsqrt(jnp.mean(middle_wide * middle_wide, axis=2) + EPSILON)
    return (centered, middle, spread)


def fold_kernel(mid_ref, vt_ref, out_ref, lhs_ref):
    cols = vt_ref.shape[1]
    chunk_rows = LAG_CHUNK * ROW_PAD
    base = mid_ref[...].astype(jnp.float32)

    def fill(q, carry):
        rolled = pltpu.roll(base, q, 1)
        lhs_ref[pl.ds(pl.multiple_of(q * ROW_PAD, ROW_PAD), ROW_PAD), :] = rolled.astype(lhs_ref.dtype)
        return carry

    lax.fori_loop(0, NLAG, fill, 0)
    lhs_ref[NLAG * ROW_PAD :, :] = jnp.zeros(
        ((LAG_PAD - NLAG) * ROW_PAD, lhs_ref.shape[1]), lhs_ref.dtype
    )

    def column(c, carry):
        first = pl.multiple_of(c * COL_TILE, COL_TILE)
        rhs = vt_ref[:, pl.ds(first, COL_TILE)]

        def body(k, acc):
            start = pl.multiple_of(k * chunk_rows, chunk_rows)
            rows = lhs_ref[pl.ds(start, chunk_rows), :]
            r = jnp.dot(rows, rhs, preferred_element_type=jnp.float32)
            r = r * r
            return acc + r.reshape(LAG_CHUNK, ROW_PAD, COL_TILE).sum(axis=0)

        acc = lax.fori_loop(
            0, LAG_PAD // LAG_CHUNK, body, jnp.zeros((ROW_PAD, COL_TILE), jnp.float32)
        )
        out_ref[:, pl.ds(first, COL_TILE)] = acc
        return carry

    lax.fori_loop(0, cols // COL_TILE, column, 0)


def lagged_energy(mid, vt):
    bands, rows, k = mid.shape
    cols = vt.shape[2]
    flops = 2 * bands * LAG_PAD * rows * k * cols
    return pl.pallas_call(
        fold_kernel,
        out_shape=jax.ShapeDtypeStruct((bands, rows, cols), jnp.float32),
        grid=(bands,),
        in_specs=[
            pl.BlockSpec((None, rows, k), lambda b: (b, 0, 0)),
            pl.BlockSpec((None, k, cols), lambda b: (b, 0, 0)),
        ],
        out_specs=pl.BlockSpec((None, rows, cols), lambda b: (b, 0, 0)),
        scratch_shapes=[pltpu.VMEM((LAG_PAD * rows, k), jnp.bfloat16)],
        compiler_params=pltpu.CompilerParams(vmem_limit_bytes=48 * 1024 * 1024),
        cost_estimate=pl.CostEstimate(
            flops=flops, bytes_accessed=2 * (mid.size + vt.size) + 4 * bands * rows * cols,
            transcendentals=0,
        ),
    )(mid, vt)


def local(source, band_taps, smooth_taps, parcel_ids):
    vert_dev, t_dev = source.shape
    owners = lax.axis_size("vert")
    total_par = (P1 + P2 + P3 + owners - 1) // owners * owners
    par_dev = total_par // owners
    n_mid = t_dev + 2 * HALF
    n_in = t_dev + 4 * HALF
    first_rows = jax.vmap(partial(toeplitz_band, n_out=n_mid, n_in=n_in))(
        band_taps.reshape(2 * BANDS, TAPS)
    )
    first_mat = first_rows.transpose(2, 0, 1).reshape(n_in, 2 * BANDS * n_mid)
    second_rows = jax.vmap(partial(toeplitz_band, n_out=t_dev, n_in=n_mid))(smooth_taps)
    second_mat = second_rows.transpose(0, 2, 1)
    widened = extended_2(source, (("tm", 1),), 2 * HALF)
    block_rows = math.gcd(vert_dev, 128)

    def filter_block(block):
        wave = jnp.dot(block, first_mat, preferred_element_type=jnp.float32).reshape(
            block_rows, 2, BANDS, n_mid
        )
        power = (wave[:, 0] * wave[:, 0] + wave[:, 1] * wave[:, 1]).astype(jnp.bfloat16)
        return jnp.einsum(
            "vbu,but->vbt", power, second_mat, preferred_element_type=jnp.float32
        ).astype(jnp.bfloat16)

    envelope = lax.map(filter_block, widened.reshape(vert_dev // block_rows, block_rows, n_in))
    flat_env = envelope.reshape(vert_dev, BANDS * t_dev)
    offsets = jnp.array([0, P1, P1 + P2], dtype=jnp.int32)
    global_ids = parcel_ids + offsets[:, None]
    owner_start = lax.axis_index("vert") * par_dev

    wanted = lax.iota(jnp.int32, total_par)
    hits = jnp.sum(
        (global_ids[:, None, :] == wanted[None, :, None]).astype(jnp.bfloat16), axis=0
    )
    pooled = jnp.dot(hits, flat_env, preferred_element_type=jnp.float32)
    own_sums = lax.psum_scatter(pooled, "vert", scatter_dimension=0, tiled=True)
    own_env = own_sums.reshape(par_dev, BANDS, t_dev)
    own_ext = extended_2(own_env, (("tm", 2),), LAG)
    centered, own_middle, own_spread = centered_rows(own_ext, t_dev)

    gathered = lax.all_gather(centered.transpose(1, 0, 2), "vert", axis=1, tiled=True)
    vis_mid = gathered[:, :, LAG : LAG + t_dev].astype(jnp.float32)
    vis_spread = lax.rsqrt(jnp.mean(vis_mid * vis_mid, axis=2) + EPSILON)
    cols = -(-total_par // COL_TILE) * COL_TILE
    vt = jnp.pad(gathered, ((0, 0), (0, cols - total_par), (0, 0))).transpose(0, 2, 1)
    mid = jnp.pad(
        own_middle.transpose(1, 0, 2), ((0, 0), (0, ROW_PAD - par_dev), (0, t_dev))
    )
    energy = lagged_energy(mid, vt)[:, :par_dev, :total_par]

    scale = own_spread.T[:, :, None] * vis_spread[:, None, :] / t_dev
    own_level = resolution_of(owner_start + lax.iota(jnp.int32, par_dev))
    all_level = resolution_of(lax.iota(jnp.int32, total_par))
    same = ((own_level[:, None] == all_level[None, :]) & (own_level[:, None] < 3)).astype(
        jnp.float32
    )
    coupling = energy * scale * scale * same[None] / NLAG
    return coupling[None]


def solution(mesh):
    return jax.shard_map(
        local,
        mesh=mesh,
        in_specs=(P("vert", "tm"), P(), P(), P(None, "vert")),
        out_specs=P("tm", None, "vert", None),
        check_vma=False,
    )
```

time: 329 us -> 300 us (0.912)
  Pallas kernels: 0 us -> 112 us
  matrix products: 87.8 us -> 8.12 us
  local copies, waits for them, and re-layouts: 52.7 us -> 13 us
  other arithmetic: 24.8 us -> 12.6 us
  loops' own time: 12.1 us -> 0.3 us
  waiting for transfers between devices: 55.3 us -> 62.8 us
  blocking collectives: 63.4 us -> 59.6 us
    pallas_call x0 -> x1, Pallas kernels: none -> 112 us  [lagged_energy(): pl.pallas_call(fold_kernel, out_shape=jax.ShapeDtypeStruct((bands, rows,...]
    conv_general_dilated x16 -> x0, matrix products: 79 us -> none  [block_value(): lax.conv_general_dilated(visiting, kernel, (LAG_STEP,), 'VALID', dimensio...]
    dynamic_slice x48 -> x0, local copies, waits for them, and re-layouts: 27.1 us -> none  [the longest x32 17.8 us: add_block(): visiting = lax.dynamic_slice_in_dim(piece, block_idx * par_dev, par_dev, 0)]
    another operation x2 -> x0, loops' own time: 12 us -> none  [the longest x1 11 us: local(): lax.map(one_block, jnp.arange(par_dev * lax.axis_size('vert') // par_dev,...]
    dynamic_update_slice x16 -> x0, other arithmetic: 11.8 us -> none  [add_block(): lax.dynamic_update_slice(total, guarded(visiting, first)[None], (slot, ze...]
    all_gather x1, waiting for transfers between devices: 51.5 us -> 60.7 us  [local(): lax.all_gather(centered.transpose(1, 0, 2), 'vert', axis=1, tiled=True)]
    dynamic_update_slice x10, local copies, waits for them, and re-layouts: 7.04 us -> 0.87 us  [local(): lax.map(filter_block, widened.reshape(vert_dev // block_rows, block_rows,...]
    unnamed x1, blocking collectives: 63.4 us -> 59.6 us
  transfers between devices with their start and end apart: 6 -> 6, of which waited for: 5 -> 3; matrix products, arithmetic and copies ran while one was open for 2% -> 4% of each run, Pallas kernels for 0% -> 0%
where the time goes in v1:
time: 300 us; the launch traced here: 299 us
  Pallas kernels  112 us (37%)
  waiting for transfers between devices  62.8 us (21%)
  blocking collectives  59.6 us (20%)
  starting transfers between devices  16.1 us (5%)
  between operations  14.4 us (5%)
  local copies, waits for them, and re-layouts  13 us (4%)
  other arithmetic  12.6 us (4%)
  matrix products  8.12 us (3%)
    pallas_call x1, Pallas kernels, lagged_energy(): pl.pallas_call(fold_kernel, out_shape=jax.ShapeDtypeStruct((bands, rows,...  112 us
    all_gather x1, waiting for transfers between devices, local(): lax.all_gather(centered.transpose(1, 0, 2), 'vert', axis=1, tiled=True)  60.7 us
    unnamed x1, blocking collectives  59.6 us
    ppermute x2, starting transfers between devices, extended_2(): lax.ppermute(head, axis, [((i + 1) % count, i) for i in range(ends)])  9.26 us
    reduce_sum x1, other arithmetic, local(): jnp.sum((global_ids[:, None, :] == wanted[None, :, None]).astype(jnp.bflo...  6 us
  transfers between devices with their start and end apart: 6, of which 3 were waited for; matrix products, arithmetic and copies ran while one was open for 4% of the time, Pallas kernels for 0%

profile of v1, /device:TPU:8, one launch (start us, length us, event | category | flops | bytes accessed | tf_op | source)
XLA Modules:
  0.0 299.2 jit_solution(14096408911457678659)
XLA Ops:
  6.5 1.2 fusion.21
  7.8 1.9 collective-permute-start
  9.7 4.5 %collective-permute-start.1 = (bf16[1280,64]{1,0:T(8,128)(2,1)S(1)}, bf16[1280,64]{1,0:T(8,128)(2,1)S(1)}, u32[]{:S(2)}, u32[]{:S(2)}) collective-permute-start(bf16[1280,64]{1,0:T(8,128)(2,1)S(1)} %get-tuple-element.79), channel_id=1, source_target_pairs={{1,0},{2,1},{3,2},{4,3},{5,4},{6,5},{7,6},{8,7},{9,8},{10,9},{11,1... | collective-permute-start | bytes 491528 | tf_op jit(solution)/shard_map/ppermute | solution.py:39
  14.3 0.8 broadcast_add_fusion
  15.1 6.0 %fusion.11 = bf16[1504,1280]{1,0:T(8,128)(2,1)} fusion(s32[3,1280]{1,0:T(4,128)S(1)} %broadcast_add_fusion), kind=kLoop, calls=%fused_computation.14 | loop fusion | flops 15400960 | bytes 3865600 | tf_op jit(solution)/shard_map/reduce_sum | solution.py:156
  21.2 0.8 tile.9
  22.3 0.4 tile.21
  23.1 0.4 pad_maximum_fusion
  23.5 6.0 %while.10 = (s32[]{:T(128)}, bf16[10,128,2,128]{3,2,1,0:T(2,128)(2,1)S(1)}, bf16[10,128,256]{2,1,0:T(8,128)(2,1)S(1)}, bf16[256,768]{0,1:T(8,128)(2,1)S(1)}, bf16[2,192,128]{2,1,0:T(8,128)(2,1)S(1)}, /*index=5*/s32[]{:T(128)}) while((s32[]{:T(128)}, bf16[10,128,2,128]{3,2,1,0:T(2,128)(2,1)S(1)}, bf16[10,128,256]{2,1,0:T(8,128)(2,1)S(1)}, ...), condition=%wide.region_2.3_spmd, body=%wide.region_1.2_spmd.sunk | while | flops 63143936 | bytes 1540173 | solution.py:149
  23.5 0.3 fusion.36
  23.7 0.2 fusion.37
  24.1 0.2 fusion.36
  24.3 0.2 fusion.37
  24.7 0.3 fusion.36
  24.9 0.2 fusion.37
  25.3 0.2 fusion.36
  25.5 0.2 fusion.37
  25.9 0.2 fusion.36
  26.1 0.2 fusion.37
  26.5 0.3 fusion.36
  26.8 0.2 fusion.37
  27.1 0.2 fusion.36
  27.4 0.2 fusion.37
  27.7 0.3 fusion.36
  28.0 0.2 fusion.37
  28.3 0.2 fusion.36
  28.6 0.2 fusion.37
  28.9 0.3 fusion.36
  29.2 0.2 fusion.37
  29.5 3.3 %fusion.15 = f32[1504,256]{1,0:T(8,128)S(1)} fusion(bf16[1504,1280]{1,0:T(8,128)(2,1)} %fusion.11, bf16[160,8,2,128]{3,2,1,0:T(2,128)(2,1)S(1)} %bitcast.66), kind=kOutput, calls=%fused_computation.21 | convolution fusion | flops 985661440 | bytes 6045696 | tf_op jit(solution)/shard_map/dot_general | solution.py:159
  32.8 59.6 %fusion = f32[96,256]{1,0:T(8,128)S(1)} fusion(f32[1504,256]{1,0:T(8,128)S(1)} %fusion.15), kind=kCustom, calls=%all-reduce-scatter | all-reduce-scatter fusion | flops 393217 | bytes 1639424
  92.4 3.0 %collective-permute-start.4 = (f32[30,256]{1,0:T(8,128)S(1)}, f32[30,256]{1,0:T(8,128)S(1)}, u32[]{:S(2)}, u32[]{:S(2)}) collective-permute-start(f32[30,256]{1,0:T(8,128)S(1)} %slice.53), channel_id=1, source_target_pairs={{0,16},{16,32},{32,48},{48,64},{64,80},{80,96},{96,112},{112,128},... | collective-permute-start | bytes 92168
  95.4 0.6 dynamic-slice.4
  96.7 0.3 collective-permute-done.4
  97.0 0.2 concatenate.16
  97.4 1.9 collective-permute-start.2
  99.3 4.7 %collective-permute-start.3 = (f32[94,2,64]{2,0,1:T(8,128)S(1)}, f32[94,2,64]{2,0,1:T(8,128)S(1)}, u32[]{:S(2)}, u32[]{:S(2)}) collective-permute-start(f32[94,2,64]{2,0,1:T(8,128)S(1)} %get-tuple-element.81), channel_id=1, source_target_pairs={{1,0},{2,1},{3,2},{4,3},{5,4},{6,5},{7,6},{8,7},{9,8},{10,9},{11,1... | collective-permute-start | bytes 144392 | tf_op jit(solution)/shard_map/ppermute | solution.py:39
  104.3 1.7 collective-permute-done.3
  106.2 0.7 copy.72
  107.1 1.0 and_convert_fusion
  108.3 60.7 %all-gather.2.cloned.1.call-done = bf16[2,1504,256]{2,0,1:T(2,128)(2,1)} async-done(((bf16[2,94,256]{2,0,1:T(2,128)(2,1)}), bf16[2,1504,256]{2,0,1:T(2,128)(2,1)}) %all-gather.2.cloned.1.call-update) | async-done | bytes 1540112 | tf_op jit(solution)/shard_map/all_gather | solution.py:165
  169.0 3.6 %copy.73 = bf16[2,1504,256]{1,2,0:T(8,128)(2,1)S(1)} copy(bf16[2,1504,256]{2,0,1:T(2,128)(2,1)} %all-gather.2.cloned.1.call-done) | data formatting | bytes 3080192 | tf_op jit(solution)/shard_map/all_gather | solution.py:165
  172.7 1.3 copy-done
  174.0 3.5 %multiply_reduce_fusion = f32[2,1504]{0,1:T(8,128)S(1)} fusion(bf16[2,1504,256]{2,0,1:T(2,128)(2,1)S(1)} %copy-done), kind=kLoop, calls=%fused_computation.17 | loop fusion | flops 1152064 | bytes 782080 | tf_op jit(solution)/shard_map/reduce_sum | solution.py:167
  177.5 0.3 copy.74
  177.8 112.3 %shard_map.55 = f32[2,96,1536]{2,1,0:T(8,128)S(1)} custom-call(bf16[2,96,256]{2,1,0:T(8,128)(2,1)S(1)} %pad.10.mid_ref, bf16[2,256,1536]{2,1,0:T(8,128)(2,1)S(1)} %pad_bitcast_fusion.vt_ref), custom_call_target="tpu_custom_call" | custom-call | flops 19931332608 | bytes 2850816 | tf_op jit(solution)/shard_map/pallas_call | solution.py:106
  290.2 0.3 fusion.14
  290.5 1.9 copy.75
  (54 shorter events, 2.5 us)
Async XLA Ops:
  6.5 162.4 %all-gather.2.cloned.1.call-start = ((), (), s32[]{:S(2)}) async-start(), calls=%async_computation | async-start | bytes 1636352 | tf_op jit(solution)/shard_map/all_gather | solution.py:165
  7.8 15.2 %collective-permute-start = (bf16[1280,64]{1,0:T(8,128)(2,1)S(1)}, bf16[1280,64]{1,0:T(8,128)(2,1)S(1)}, u32[]{:S(2)}, u32[]{:S(2)}) collective-permute-start(bf16[1280,64]{1,0:T(8,128)(2,1)S(1)} %get-tuple-element.78), channel_id=1, source_target_pairs={{0,1},{1,2},{2,3},{3,4},{4,5},{5,6},{6,7},{7,8},{8,9},{9,10},{10,1... | collective-permute-start | bytes 491528 | tf_op jit(solution)/shard_map/ppermute | solution.py:37
  9.7 13.3 %collective-permute-start.1 = (bf16[1280,64]{1,0:T(8,128)(2,1)S(1)}, bf16[1280,64]{1,0:T(8,128)(2,1)S(1)}, u32[]{:S(2)}, u32[]{:S(2)}) collective-permute-start(bf16[1280,64]{1,0:T(8,128)(2,1)S(1)} %get-tuple-element.79), channel_id=1, source_target_pairs={{1,0},{2,1},{3,2},{4,3},{5,4},{6,5},{7,6},{8,7},{9,8},{10,9},{11,1... | collective-permute-start | bytes 491528 | tf_op jit(solution)/shard_map/ppermute | solution.py:39
  15.1 6.0 %copy-start.3 = (bf16[2,2,65]{2,1,0:T(2,128)(2,1)S(1)}, bf16[2,2,65]{2,1,0:T(2,128)(2,1)}, u32[]{:S(2)}) copy-start(bf16[2,2,65]{2,1,0:T(2,128)(2,1)} %param.8) | copy-start | bytes 1564
  21.1 1.1 copy-start.4
  22.0 1.0 copy-start.1
  32.8 62.6 %copy-start.5 = (u32[256]{0:T(256)S(1)}, u32[256]{0:T(256)}, u32[]{:S(2)}) copy-start(u32[256]{0:T(256)} %constant.65) | copy-start | bytes 3076
  92.4 4.6 %collective-permute-start.4 = (f32[30,256]{1,0:T(8,128)S(1)}, f32[30,256]{1,0:T(8,128)S(1)}, u32[]{:S(2)}, u32[]{:S(2)}) collective-permute-start(f32[30,256]{1,0:T(8,128)S(1)} %slice.53), channel_id=1, source_target_pairs={{0,16},{16,32},{32,48},{48,64},{64,80},{80,96},{96,112},{112,128},... | collective-permute-start | bytes 92168
  97.4 6.9 %collective-permute-start.2 = (f32[94,2,64]{2,0,1:T(8,128)S(1)}, f32[94,2,64]{2,0,1:T(8,128)S(1)}, u32[]{:S(2)}, u32[]{:S(2)}) collective-permute-start(f32[94,2,64]{2,0,1:T(8,128)S(1)} %get-tuple-element.80), channel_id=1, source_target_pairs={{0,1},{1,2},{2,3},{3,4},{4,5},{5,6},{6,7},{7,8},{8,9},{9,10},{10,1... | collective-permute-start | bytes 144392 | tf_op jit(solution)/shard_map/ppermute | solution.py:37
  99.3 6.7 %collective-permute-start.3 = (f32[94,2,64]{2,0,1:T(8,128)S(1)}, f32[94,2,64]{2,0,1:T(8,128)S(1)}, u32[]{:S(2)}, u32[]{:S(2)}) collective-permute-start(f32[94,2,64]{2,0,1:T(8,128)S(1)} %get-tuple-element.81), channel_id=1, source_target_pairs={{1,0},{2,1},{3,2},{4,3},{5,4},{6,5},{7,6},{8,7},{9,8},{10,9},{11,1... | collective-permute-start | bytes 144392 | tf_op jit(solution)/shard_map/ppermute | solution.py:39
  172.6 1.4 copy-start
  177.8 112.4 %copy-start.2 = (f32[94,1504]{1,0:T(8,128)S(1)}, f32[94,1504]{1,0:T(8,128)}, u32[]{:S(2)}) copy-start(f32[94,1504]{1,0:T(8,128)} %and_convert_fusion) | copy-start | bytes 1696516
Sparse Core Ops, SparseCore 0:
  107.1 61.8 all-gather.1

commit v2 on v1

--- a/solution.py
+++ b/solution.py
@@ -21,7 +21,7 @@
 EPSILON = 1e-05
 
 ROW_PAD = 96
-LAG_CHUNK = 4
+LAG_CHUNKS = 11
 LAG_PAD = 132
 COL_TILE = 256
 
@@ -66,33 +66,22 @@
 
 def fold_kernel(mid_ref, vt_ref, out_ref, lhs_ref):
     cols = vt_ref.shape[1]
-    chunk_rows = LAG_CHUNK * ROW_PAD
     base = mid_ref[...].astype(jnp.float32)
-
-    def fill(q, carry):
-        rolled = pltpu.roll(base, q, 1)
-        lhs_ref[pl.ds(pl.multiple_of(q * ROW_PAD, ROW_PAD), ROW_PAD), :] = rolled.astype(lhs_ref.dtype)
-        return carry
-
-    lax.fori_loop(0, NLAG, fill, 0)
+    for q in range(NLAG):
+        lhs_ref[q * ROW_PAD : (q + 1) * ROW_PAD, :] = pltpu.roll(base, q, 1).astype(lhs_ref.dtype)
     lhs_ref[NLAG * ROW_PAD :, :] = jnp.zeros(
         ((LAG_PAD - NLAG) * ROW_PAD, lhs_ref.shape[1]), lhs_ref.dtype
     )
+    step = LAG_PAD // LAG_CHUNKS
 
     def column(c, carry):
         first = pl.multiple_of(c * COL_TILE, COL_TILE)
         rhs = vt_ref[:, pl.ds(first, COL_TILE)]
-
-        def body(k, acc):
-            start = pl.multiple_of(k * chunk_rows, chunk_rows)
-            rows = lhs_ref[pl.ds(start, chunk_rows), :]
+        acc = jnp.zeros((ROW_PAD, COL_TILE), jnp.float32)
+        for h in range(LAG_CHUNKS):
+            rows = lhs_ref[h * step * ROW_PAD : (h + 1) * step * ROW_PAD, :]
             r = jnp.dot(rows, rhs, preferred_element_type=jnp.float32)
-            r = r * r
-            return acc + r.reshape(LAG_CHUNK, ROW_PAD, COL_TILE).sum(axis=0)
-
-        acc = lax.fori_loop(
-            0, LAG_PAD // LAG_CHUNK, body, jnp.zeros((ROW_PAD, COL_TILE), jnp.float32)
-        )
+            acc = acc + (r * r).reshape(step, ROW_PAD, COL_TILE).sum(axis=0)
         out_ref[:, pl.ds(first, COL_TILE)] = acc
         return carry
 

time: 300 us -> 214 us (0.71)
  Pallas kernels: 112 us -> 25.8 us
    pallas_call x1, Pallas kernels: 112 us -> 25.8 us  [lagged_energy(): pl.pallas_call(fold_kernel, out_shape=jax.ShapeDtypeStruct((bands, rows,...]
  transfers between devices with their start and end apart: 6 -> 6, of which waited for: 3 -> 3; matrix products, arithmetic and copies ran while one was open for 4% -> 5% of each run, Pallas kernels for 0% -> 0%
where the time goes in v2:
time: 214 us; the launch traced here: 213 us
  waiting for transfers between devices  62.8 us (29%)
  blocking collectives  59.6 us (28%)
  Pallas kernels  25.8 us (12%)
  starting transfers between devices  16.1 us (8%)
  between operations  14.4 us (7%)
  local copies, waits for them, and re-layouts  13 us (6%)
  other arithmetic  12.6 us (6%)
  matrix products  8.12 us (4%)
    all_gather x1, waiting for transfers between devices, local(): lax.all_gather(centered.transpose(1, 0, 2), 'vert', axis=1, tiled=True)  60.7 us
    unnamed x1, blocking collectives  59.6 us
    pallas_call x1, Pallas kernels, lagged_energy(): pl.pallas_call(fold_kernel, out_shape=jax.ShapeDtypeStruct((bands, rows,...  25.8 us
    ppermute x2, starting transfers between devices, extended_2(): lax.ppermute(head, axis, [((i + 1) % count, i) for i in range(ends)])  9.26 us
    reduce_sum x1, other arithmetic, local(): jnp.sum((global_ids[:, None, :] == wanted[None, :, None]).astype(jnp.bflo...  6 us
  transfers between devices with their start and end apart: 6, of which 3 were waited for; matrix products, arithmetic and copies ran while one was open for 5% of the time, Pallas kernels for 0%

profile of v2, /device:TPU:8, one launch (start us, length us, event | category | flops | bytes accessed | tf_op | source)
XLA Modules:
  0.0 212.7 jit_solution(15782212781557759488)
XLA Ops:
  6.5 1.2 fusion.21
  7.8 1.9 collective-permute-start
  9.7 4.5 %collective-permute-start.1 = (bf16[1280,64]{1,0:T(8,128)(2,1)S(1)}, bf16[1280,64]{1,0:T(8,128)(2,1)S(1)}, u32[]{:S(2)}, u32[]{:S(2)}) collective-permute-start(bf16[1280,64]{1,0:T(8,128)(2,1)S(1)} %get-tuple-element.79), channel_id=1, source_target_pairs={{1,0},{2,1},{3,2},{4,3},{5,4},{6,5},{7,6},{8,7},{9,8},{10,9},{11,1... | collective-permute-start | bytes 491528 | tf_op jit(solution)/shard_map/ppermute | solution.py:39
  14.3 0.8 broadcast_add_fusion
  15.1 6.0 %fusion.11 = bf16[1504,1280]{1,0:T(8,128)(2,1)} fusion(s32[3,1280]{1,0:T(4,128)S(1)} %broadcast_add_fusion), kind=kLoop, calls=%fused_computation.14 | loop fusion | flops 15400960 | bytes 3865600 | tf_op jit(solution)/shard_map/reduce_sum | solution.py:145
  21.2 0.8 tile.9
  22.3 0.4 tile.21
  23.1 0.4 pad_maximum_fusion
  23.5 6.0 %while.10 = (s32[]{:T(128)}, bf16[10,128,2,128]{3,2,1,0:T(2,128)(2,1)S(1)}, bf16[10,128,256]{2,1,0:T(8,128)(2,1)S(1)}, bf16[256,768]{0,1:T(8,128)(2,1)S(1)}, bf16[2,192,128]{2,1,0:T(8,128)(2,1)S(1)}, /*index=5*/s32[]{:T(128)}) while((s32[]{:T(128)}, bf16[10,128,2,128]{3,2,1,0:T(2,128)(2,1)S(1)}, bf16[10,128,256]{2,1,0:T(8,128)(2,1)S(1)}, ...), condition=%wide.region_2.3_spmd, body=%wide.region_1.2_spmd.sunk | while | flops 63143936 | bytes 1540173 | solution.py:138
  23.5 0.3 fusion.36
  23.7 0.2 fusion.37
  24.1 0.2 fusion.36
  24.3 0.2 fusion.37
  24.7 0.3 fusion.36
  24.9 0.2 fusion.37
  25.3 0.2 fusion.36
  25.5 0.2 fusion.37
  25.9 0.2 fusion.36
  26.1 0.2 fusion.37
  26.5 0.3 fusion.36
  26.8 0.2 fusion.37
  27.1 0.2 fusion.36
  27.4 0.2 fusion.37
  27.7 0.3 fusion.36
  28.0 0.2 fusion.37
  28.3 0.2 fusion.36
  28.6 0.2 fusion.37
  28.9 0.3 fusion.36
  29.2 0.2 fusion.37
  29.5 3.3 %fusion.15 = f32[1504,256]{1,0:T(8,128)S(1)} fusion(bf16[1504,1280]{1,0:T(8,128)(2,1)} %fusion.11, bf16[160,8,2,128]{3,2,1,0:T(2,128)(2,1)S(1)} %bitcast.66), kind=kOutput, calls=%fused_computation.21 | convolution fusion | flops 985661440 | bytes 6045696 | tf_op jit(solution)/shard_map/dot_general | solution.py:148
  32.8 59.6 %fusion = f32[96,256]{1,0:T(8,128)S(1)} fusion(f32[1504,256]{1,0:T(8,128)S(1)} %fusion.15), kind=kCustom, calls=%all-reduce-scatter | all-reduce-scatter fusion | flops 393217 | bytes 1639424
  92.4 3.0 %collective-permute-start.4 = (f32[30,256]{1,0:T(8,128)S(1)}, f32[30,256]{1,0:T(8,128)S(1)}, u32[]{:S(2)}, u32[]{:S(2)}) collective-permute-start(f32[30,256]{1,0:T(8,128)S(1)} %slice.53), channel_id=1, source_target_pairs={{0,16},{16,32},{32,48},{48,64},{64,80},{80,96},{96,112},{112,128},... | collective-permute-start | bytes 92168
  95.4 0.6 dynamic-slice.4
  96.7 0.3 collective-permute-done.4
  97.0 0.2 concatenate.16
  97.4 1.9 collective-permute-start.2
  99.3 4.7 %collective-permute-start.3 = (f32[94,2,64]{2,0,1:T(8,128)S(1)}, f32[94,2,64]{2,0,1:T(8,128)S(1)}, u32[]{:S(2)}, u32[]{:S(2)}) collective-permute-start(f32[94,2,64]{2,0,1:T(8,128)S(1)} %get-tuple-element.81), channel_id=1, source_target_pairs={{1,0},{2,1},{3,2},{4,3},{5,4},{6,5},{7,6},{8,7},{9,8},{10,9},{11,1... | collective-permute-start | bytes 144392 | tf_op jit(solution)/shard_map/ppermute | solution.py:39
  104.3 1.7 collective-permute-done.3
  106.2 0.7 copy.72
  107.1 1.0 and_convert_fusion
  108.3 60.7 %all-gather.2.cloned.1.call-done = bf16[2,1504,256]{2,0,1:T(2,128)(2,1)} async-done(((bf16[2,94,256]{2,0,1:T(2,128)(2,1)}), bf16[2,1504,256]{2,0,1:T(2,128)(2,1)}) %all-gather.2.cloned.1.call-update) | async-done | bytes 1540112 | tf_op jit(solution)/shard_map/all_gather | solution.py:154
  169.0 3.6 %copy.73 = bf16[2,1504,256]{1,2,0:T(8,128)(2,1)S(1)} copy(bf16[2,1504,256]{2,0,1:T(2,128)(2,1)} %all-gather.2.cloned.1.call-done) | data formatting | bytes 3080192 | tf_op jit(solution)/shard_map/all_gather | solution.py:154
  172.7 1.3 copy-done
  174.0 3.5 %multiply_reduce_fusion = f32[2,1504]{0,1:T(8,128)S(1)} fusion(bf16[2,1504,256]{2,0,1:T(2,128)(2,1)S(1)} %copy-done), kind=kLoop, calls=%fused_computation.17 | loop fusion | flops 1152064 | bytes 782080 | tf_op jit(solution)/shard_map/reduce_sum | solution.py:156
  177.5 0.3 copy.74
  177.8 25.8 %shard_map.55 = f32[2,96,1536]{2,1,0:T(8,128)S(1)} custom-call(bf16[2,96,256]{2,1,0:T(8,128)(2,1)S(1)} %pad.10.mid_ref, bf16[2,256,1536]{2,1,0:T(8,128)(2,1)S(1)} %pad_bitcast_fusion.vt_ref), custom_call_target="tpu_custom_call" | custom-call | flops 19931332608 | bytes 2850816 | tf_op jit(solution)/shard_map/pallas_call | solution.py:95
  203.7 0.3 fusion.14
  204.0 1.9 copy.75
  (54 shorter events, 2.5 us)
Async XLA Ops:
  6.5 162.4 %all-gather.2.cloned.1.call-start = ((), (), s32[]{:S(2)}) async-start(), calls=%async_computation | async-start | bytes 1636352 | tf_op jit(solution)/shard_map/all_gather | solution.py:154
  7.8 15.2 %collective-permute-start = (bf16[1280,64]{1,0:T(8,128)(2,1)S(1)}, bf16[1280,64]{1,0:T(8,128)(2,1)S(1)}, u32[]{:S(2)}, u32[]{:S(2)}) collective-permute-start(bf16[1280,64]{1,0:T(8,128)(2,1)S(1)} %get-tuple-element.78), channel_id=1, source_target_pairs={{0,1},{1,2},{2,3},{3,4},{4,5},{5,6},{6,7},{7,8},{8,9},{9,10},{10,1... | collective-permute-start | bytes 491528 | tf_op jit(solution)/shard_map/ppermute | solution.py:37
  9.7 13.3 %collective-permute-start.1 = (bf16[1280,64]{1,0:T(8,128)(2,1)S(1)}, bf16[1280,64]{1,0:T(8,128)(2,1)S(1)}, u32[]{:S(2)}, u32[]{:S(2)}) collective-permute-start(bf16[1280,64]{1,0:T(8,128)(2,1)S(1)} %get-tuple-element.79), channel_id=1, source_target_pairs={{1,0},{2,1},{3,2},{4,3},{5,4},{6,5},{7,6},{8,7},{9,8},{10,9},{11,1... | collective-permute-start | bytes 491528 | tf_op jit(solution)/shard_map/ppermute | solution.py:39
  15.1 6.0 %copy-start.3 = (bf16[2,2,65]{2,1,0:T(2,128)(2,1)S(1)}, bf16[2,2,65]{2,1,0:T(2,128)(2,1)}, u32[]{:S(2)}) copy-start(bf16[2,2,65]{2,1,0:T(2,128)(2,1)} %param.8) | copy-start | bytes 1564
  21.1 1.1 copy-start.4
  22.0 1.0 copy-start.1
  32.8 62.6 %copy-start.5 = (u32[256]{0:T(256)S(1)}, u32[256]{0:T(256)}, u32[]{:S(2)}) copy-start(u32[256]{0:T(256)} %constant.65) | copy-start | bytes 3076
  92.4 4.6 %collective-permute-start.4 = (f32[30,256]{1,0:T(8,128)S(1)}, f32[30,256]{1,0:T(8,128)S(1)}, u32[]{:S(2)}, u32[]{:S(2)}) collective-permute-start(f32[30,256]{1,0:T(8,128)S(1)} %slice.53), channel_id=1, source_target_pairs={{0,16},{16,32},{32,48},{48,64},{64,80},{80,96},{96,112},{112,128},... | collective-permute-start | bytes 92168
  97.4 6.9 %collective-permute-start.2 = (f32[94,2,64]{2,0,1:T(8,128)S(1)}, f32[94,2,64]{2,0,1:T(8,128)S(1)}, u32[]{:S(2)}, u32[]{:S(2)}) collective-permute-start(f32[94,2,64]{2,0,1:T(8,128)S(1)} %get-tuple-element.80), channel_id=1, source_target_pairs={{0,1},{1,2},{2,3},{3,4},{4,5},{5,6},{6,7},{7,8},{8,9},{9,10},{10,1... | collective-permute-start | bytes 144392 | tf_op jit(solution)/shard_map/ppermute | solution.py:37
  99.3 6.7 %collective-permute-start.3 = (f32[94,2,64]{2,0,1:T(8,128)S(1)}, f32[94,2,64]{2,0,1:T(8,128)S(1)}, u32[]{:S(2)}, u32[]{:S(2)}) collective-permute-start(f32[94,2,64]{2,0,1:T(8,128)S(1)} %get-tuple-element.81), channel_id=1, source_target_pairs={{1,0},{2,1},{3,2},{4,3},{5,4},{6,5},{7,6},{8,7},{9,8},{10,9},{11,1... | collective-permute-start | bytes 144392 | tf_op jit(solution)/shard_map/ppermute | solution.py:39
  172.6 1.4 copy-start
  177.8 25.9 %copy-start.2 = (f32[94,1504]{1,0:T(8,128)S(1)}, f32[94,1504]{1,0:T(8,128)}, u32[]{:S(2)}) copy-start(f32[94,1504]{1,0:T(8,128)} %and_convert_fusion) | copy-start | bytes 1696516
Sparse Core Ops, SparseCore 0:
  107.1 61.8 all-gather.1

commit v3 on v2

--- a/solution.py
+++ b/solution.py
@@ -110,6 +110,53 @@
     )(mid, vt)
 
 
+def exchange_kernel(spread, x_ref, out_ref, send_sems, recv_sems, local_sem):
+    n = out_ref.shape[0]
+    me = lax.axis_index("vert")
+    tm = lax.axis_index("tm")
+    barrier = pltpu.get_barrier_semaphore()
+    for k in range(1, n):
+        peer = lax.rem(me + k, n)
+        pl.semaphore_signal(
+            barrier, inc=1, device_id=(peer, tm), device_id_type=pl.DeviceIdType.MESH
+        )
+    pl.semaphore_wait(barrier, n - 1)
+    copies = []
+    for k in range(1, n):
+        peer = lax.rem(me + k, n)
+        copy = pltpu.make_async_remote_copy(
+            src_ref=x_ref.at[peer] if spread else x_ref,
+            dst_ref=out_ref.at[me],
+            send_sem=send_sems.at[k],
+            recv_sem=recv_sems.at[k],
+            device_id=(peer, tm),
+            device_id_type=pl.DeviceIdType.MESH,
+        )
+        copy.start()
+        copies.append(copy)
+    own = pltpu.make_async_copy(x_ref.at[me] if spread else x_ref, out_ref.at[me], local_sem)
+    own.start()
+    own.wait()
+    for copy in copies:
+        copy.wait()
+
+
+def exchange(x, n, spread, collective_id):
+    block = x.shape[1:] if spread else x.shape
+    return pl.pallas_call(
+        partial(exchange_kernel, spread),
+        out_shape=jax.ShapeDtypeStruct((n,) + block, x.dtype),
+        in_specs=[pl.BlockSpec(memory_space=pl.ANY)],
+        out_specs=pl.BlockSpec(memory_space=pl.ANY),
+        scratch_shapes=[
+            pltpu.SemaphoreType.DMA((n,)),
+            pltpu.SemaphoreType.DMA((n,)),
+            pltpu.SemaphoreType.DMA(()),
+        ],
+        compiler_params=pltpu.CompilerParams(collective_id=collective_id, has_side_effects=True),
+    )(x)
+
+
 def local(source, band_taps, smooth_taps, parcel_ids):
     vert_dev, t_dev = source.shape
     owners = lax.axis_size("vert")
@@ -146,12 +193,14 @@
         (global_ids[:, None, :] == wanted[None, :, None]).astype(jnp.bfloat16), axis=0
     )
     pooled = jnp.dot(hits, flat_env, preferred_element_type=jnp.float32)
-    own_sums = lax.psum_scatter(pooled, "vert", scatter_dimension=0, tiled=True)
+    parts = exchange(pooled.reshape(owners, par_dev, BANDS * t_dev), owners, True, 0)
+    own_sums = jnp.sum(parts, axis=0)
     own_env = own_sums.reshape(par_dev, BANDS, t_dev)
     own_ext = extended_2(own_env, (("tm", 2),), LAG)
     centered, own_middle, own_spread = centered_rows(own_ext, t_dev)
 
-    gathered = lax.all_gather(centered.transpose(1, 0, 2), "vert", axis=1, tiled=True)
+    blocks = exchange(centered.transpose(1, 0, 2), owners, False, 1)
+    gathered = blocks.transpose(1, 0, 2, 3).reshape(BANDS, total_par, 2 * LAG + t_dev)
     vis_mid = gathered[:, :, LAG : LAG + t_dev].astype(jnp.float32)
     vis_spread = lax.rsqrt(jnp.mean(vis_mid * vis_mid, axis=2) + EPSILON)
     cols = -(-total_par // COL_TILE) * COL_TILE

time: 214 us -> 165 us (0.77)
  Pallas kernels: 25.8 us -> 111 us
  blocking collectives: 59.6 us -> 0 us
  waiting for transfers between devices: 62.8 us -> 4.65 us
  between operations: 14.4 us -> 0.37 us
  starting transfers between devices: 16.1 us -> 11.4 us
    pallas_call x0 -> x2, Pallas kernels: none -> 85.4 us  [exchange(): pl.pallas_call(partial(exchange_kernel, spread), out_shape=jax.ShapeDtype...]
    all_gather x1 -> x0, waiting for transfers between devices: 60.7 us -> none  [local(): lax.all_gather(centered.transpose(1, 0, 2), 'vert', axis=1, tiled=True)]
    unnamed x1 -> x0, blocking collectives: 59.6 us -> none
    dot_general x0 -> x1, local copies, waits for them, and re-layouts: none -> 4.93 us  [local(): pooled = jnp.dot(hits, flat_env, preferred_element_type=jnp.float32)]
    ppermute x2, waiting for transfers between devices: 0.01 us -> 4.64 us  [extended_2(): lax.ppermute(tail, axis, [(i, (i + 1) % count) for i in range(ends)])]
    all_gather x1 -> x0, local copies, waits for them, and re-layouts: 3.6 us -> none  [local(): lax.all_gather(centered.transpose(1, 0, 2), 'vert', axis=1, tiled=True)]
    unnamed x1 -> x0, starting transfers between devices: 3.02 us -> none
    reduce_sum x1, other arithmetic: 3.53 us -> 0.74 us  [local(): vis_spread = lax.rsqrt(jnp.mean(vis_mid * vis_mid, axis=2) + EPSILON)]
  transfers between devices with their start and end apart: 6 -> 4, of which waited for: 3 -> 1; matrix products, arithmetic and copies ran while one was open for 5% -> 9% of each run, Pallas kernels for 0% -> 0%
where the time goes in v3:
time: 165 us; the launch traced here: 163 us
  Pallas kernels  111 us (67%)
  local copies, waits for them, and re-layouts  14.9 us (9%)
  starting transfers between devices  11.4 us (7%)
  other arithmetic  11.3 us (7%)
  matrix products  9.32 us (6%)
  waiting for transfers between devices  4.65 us (3%)
    pallas_call x2, Pallas kernels, exchange(): pl.pallas_call(partial(exchange_kernel, spread), out_shape=jax.ShapeDtype...  85.4 us
    pallas_call x1, Pallas kernels, lagged_energy(): pl.pallas_call(fold_kernel, out_shape=jax.ShapeDtypeStruct((bands, rows,...  25.8 us
    ppermute x2, starting transfers between devices, extended_2(): lax.ppermute(head, axis, [((i + 1) % count, i) for i in range(ends)])  7.39 us
    reduce_sum x1, other arithmetic, local(): jnp.sum((global_ids[:, None, :] == wanted[None, :, None]).astype(jnp.bflo...  6.02 us
    dot_general x1, local copies, waits for them, and re-layouts, local(): pooled = jnp.dot(hits, flat_env, preferred_element_type=jnp.float32)  4.93 us
    ppermute x2, waiting for transfers between devices, extended_2(): lax.ppermute(tail, axis, [(i, (i + 1) % count) for i in range(ends)])  4.64 us
    dot_general x1, matrix products, local(): pooled = jnp.dot(hits, flat_env, preferred_element_type=jnp.float32)  4.47 us
    ppermute x2, starting transfers between devices, extended_2(): lax.ppermute(tail, axis, [(i, (i + 1) % count) for i in range(ends)])  4.02 us
  transfers between devices with their start and end apart: 4, of which 1 were waited for; matrix products, arithmetic and copies ran while one was open for 9% of the time, Pallas kernels for 0%

profile of v3, /device:TPU:8, one launch (start us, length us, event | category | flops | bytes accessed | tf_op | source)
XLA Modules:
  0.0 163.4 jit_solution(13957039833389836031)
XLA Ops:
  0.0 1.2 fusion.17
  1.2 3.2 %collective-permute-start.1 = (bf16[1280,64]{1,0:T(8,128)(2,1)S(1)}, bf16[1280,64]{1,0:T(8,128)(2,1)S(1)}, u32[]{:S(2)}, u32[]{:S(2)}) collective-permute-start(bf16[1280,64]{1,0:T(8,128)(2,1)S(1)} %get-tuple-element.69), channel_id=1, source_target_pairs={{1,0},{2,1},{3,2},{4,3},{5,4},{6,5},{7,6},{8,7},{9,8},{10,9},{11,1... | collective-permute-start | bytes 491528 | tf_op jit(solution)/shard_map/ppermute | solution.py:39
  4.4 1.9 %collective-permute-start = (bf16[1280,64]{1,0:T(8,128)(2,1)S(1)}, bf16[1280,64]{1,0:T(8,128)(2,1)S(1)}, u32[]{:S(2)}, u32[]{:S(2)}) collective-permute-start(bf16[1280,64]{1,0:T(8,128)(2,1)S(1)} %get-tuple-element.68), channel_id=1, source_target_pairs={{0,1},{1,2},{2,3},{3,4},{4,5},{5,6},{6,7},{7,8},{8,9},{9,10},{10,1... | collective-permute-start | bytes 491528 | tf_op jit(solution)/shard_map/ppermute | solution.py:37
  6.4 0.8 broadcast_add_fusion
  7.2 1.0 and_convert_fusion
  8.1 6.0 %fusion.10 = bf16[1504,1280]{1,0:T(8,128)(2,1)} fusion(s32[3,1280]{1,0:T(4,128)S(1)} %broadcast_add_fusion), kind=kLoop, calls=%fused_computation.14 | loop fusion | flops 15400960 | bytes 3865600 | tf_op jit(solution)/shard_map/reduce_sum | solution.py:192
  14.2 4.9 %dot_general.15 = bf16[16,94,1280]{2,1,0:T(8,128)(2,1)} reshape(bf16[1504,1280]{1,0:T(8,128)(2,1)} %fusion.10) | data formatting | bytes 7700480 | tf_op jit(solution)/shard_map/dot_general | solution.py:195
  19.2 0.8 tile.9
  20.3 0.4 tile.21
  21.1 0.4 pad_maximum_fusion
  21.5 6.0 %while.10 = (s32[]{:T(128)}, bf16[10,128,2,128]{3,2,1,0:T(2,128)(2,1)S(1)}, bf16[10,128,256]{2,1,0:T(8,128)(2,1)S(1)}, bf16[256,768]{0,1:T(8,128)(2,1)S(1)}, bf16[2,192,128]{2,1,0:T(8,128)(2,1)S(1)}, /*index=5*/s32[]{:T(128)}) while((s32[]{:T(128)}, bf16[10,128,2,128]{3,2,1,0:T(2,128)(2,1)S(1)}, bf16[10,128,256]{2,1,0:T(8,128)(2,1)S(1)}, ...), condition=%wide.region_2.3_spmd, body=%wide.region_1.2_spmd.sunk | while | flops 63143936 | bytes 1540181 | solution.py:185
  21.5 0.2 fusion.34
  21.8 0.2 fusion.35
  22.1 0.3 fusion.34
  22.4 0.2 fusion.35
  22.7 0.2 fusion.34
  23.0 0.2 fusion.35
  23.3 0.2 fusion.34
  23.6 0.2 fusion.35
  23.9 0.3 fusion.34
  24.2 0.2 fusion.35
  24.5 0.2 fusion.34
  24.8 0.2 fusion.35
  25.1 0.3 fusion.34
  25.4 0.2 fusion.35
  25.7 0.2 fusion.34
  26.0 0.2 fusion.35
  26.3 0.3 fusion.34
  26.6 0.2 fusion.35
  26.9 0.2 fusion.34
  27.2 0.2 fusion.35
  27.5 0.4 reshape.131
  27.9 4.5 %fusion.19.x_ref = f32[16,94,256]{2,1,0:T(8,128)} fusion(bf16[16,94,1280]{2,1,0:T(8,128)(2,1)} %dot_general.15, bf16[1280,256,1]{1,0,2:T(8,128)(2,1)S(1)} %reshape.131), kind=kOutput, calls=%fused_computation.44 | convolution fusion | flops 985661440 | bytes 6045696 | tf_op jit(solution)/shard_map/dot_general | solution.py:195
  32.4 44.0 %shard_map.55 = f32[16,94,256]{2,1,0:T(8,128)} custom-call(f32[16,94,256]{2,1,0:T(8,128)} %fusion.19.x_ref), custom_call_target="tpu_custom_call" | custom-call | tf_op jit(solution)/shard_map/pallas_call | solution.py:146
  76.4 1.5 reduce_sum.49
  78.3 4.2 %collective-permute-start.3 = (f32[94,2,64]{2,0,1:T(8,128)S(1)}, f32[94,2,64]{2,0,1:T(8,128)S(1)}, u32[]{:S(2)}, u32[]{:S(2)}) collective-permute-start(f32[94,2,64]{2,0,1:T(8,128)S(1)} %get-tuple-element.71), channel_id=1, source_target_pairs={{1,0},{2,1},{3,2},{4,3},{5,4},{6,5},{7,6},{8,7},{9,8},{10,9},{11,1... | collective-permute-start | bytes 144392 | tf_op jit(solution)/shard_map/ppermute | solution.py:39
  82.5 2.1 %collective-permute-start.2 = (f32[94,2,64]{2,0,1:T(8,128)S(1)}, f32[94,2,64]{2,0,1:T(8,128)S(1)}, u32[]{:S(2)}, u32[]{:S(2)}) collective-permute-start(f32[94,2,64]{2,0,1:T(8,128)S(1)} %get-tuple-element.70), channel_id=1, source_target_pairs={{0,1},{1,2},{2,3},{3,4},{4,5},{5,6},{6,7},{7,8},{8,9},{9,10},{10,1... | collective-permute-start | bytes 144392 | tf_op jit(solution)/shard_map/ppermute | solution.py:37
  84.7 4.6 %collective-permute-done.2 = f32[94,2,64]{2,0,1:T(8,128)S(1)} collective-permute-done((f32[94,2,64]{2,0,1:T(8,128)S(1)}, f32[94,2,64]{2,0,1:T(8,128)S(1)}, u32[]{:S(2)}, u32[]{:S(2)}) %collective-permute-start.2) | collective-permute-done | bytes 48160 | tf_op jit(solution)/shard_map/ppermute | solution.py:37
  89.6 0.5 copy-done.2
  90.2 41.4 %shard_map.56 = bf16[16,2,94,256]{3,2,1,0:T(8,128)(2,1)} custom-call(bf16[2,94,256]{2,1,0:T(8,128)(2,1)} %bitcast.58), custom_call_target="tpu_custom_call" | custom-call | tf_op jit(solution)/shard_map/pallas_call | solution.py:146
  131.6 1.5 copy.58
  133.1 0.4 reshape.129
  133.5 0.7 copy.59
  134.3 0.7 multiply_reduce_fusion
  135.0 0.2 multiply_reduce_fusion.1
  135.4 25.8 %shard_map.57 = f32[2,96,1536]{2,1,0:T(8,128)S(1)} custom-call(bf16[2,96,256]{2,1,0:T(8,128)(2,1)S(1)} %pad.10.mid_ref, bf16[2,256,1536]{2,1,0:T(8,128)(2,1)S(1)} %pad_bitcast_fusion.vt_ref), custom_call_target="tpu_custom_call" | custom-call | flops 19931332608 | bytes 2850816 | tf_op jit(solution)/shard_map/pallas_call | solution.py:95
  161.2 0.3 fusion.13
  161.5 1.9 %copy.60 = f32[1,2,94,1504]{3,1,2,0:T(2,128)} copy(f32[1,2,94,1504]{3,2,1,0:T(8,128)S(1)} %fusion.13) | data formatting | bytes 2262016 | tf_op jit(solution)/shard_map/broadcast_in_dim | solution.py:220
  (49 shorter events, 2.3 us)
Async XLA Ops:
  1.2 19.8 %collective-permute-start.1 = (bf16[1280,64]{1,0:T(8,128)(2,1)S(1)}, bf16[1280,64]{1,0:T(8,128)(2,1)S(1)}, u32[]{:S(2)}, u32[]{:S(2)}) collective-permute-start(bf16[1280,64]{1,0:T(8,128)(2,1)S(1)} %get-tuple-element.69), channel_id=1, source_target_pairs={{1,0},{2,1},{3,2},{4,3},{5,4},{6,5},{7,6},{8,7},{9,8},{10,9},{11,1... | collective-permute-start | bytes 491528 | tf_op jit(solution)/shard_map/ppermute | solution.py:39
  4.4 16.7 %collective-permute-start = (bf16[1280,64]{1,0:T(8,128)(2,1)S(1)}, bf16[1280,64]{1,0:T(8,128)(2,1)S(1)}, u32[]{:S(2)}, u32[]{:S(2)}) collective-permute-start(bf16[1280,64]{1,0:T(8,128)(2,1)S(1)} %get-tuple-element.68), channel_id=1, source_target_pairs={{0,1},{1,2},{2,3},{3,4},{4,5},{5,6},{6,7},{7,8},{8,9},{9,10},{10,1... | collective-permute-start | bytes 491528 | tf_op jit(solution)/shard_map/ppermute | solution.py:37
  14.2 4.9 %copy-start.4 = (bf16[2,2,65]{2,1,0:T(2,128)(2,1)S(1)}, bf16[2,2,65]{2,1,0:T(2,128)(2,1)}, u32[]{:S(2)}) copy-start(bf16[2,2,65]{2,1,0:T(2,128)(2,1)} %param.8) | copy-start | bytes 1564
  19.1 1.1 copy-start.5
  20.0 1.0 copy-start
  78.3 6.4 %collective-permute-start.3 = (f32[94,2,64]{2,0,1:T(8,128)S(1)}, f32[94,2,64]{2,0,1:T(8,128)S(1)}, u32[]{:S(2)}, u32[]{:S(2)}) collective-permute-start(f32[94,2,64]{2,0,1:T(8,128)S(1)} %get-tuple-element.71), channel_id=1, source_target_pairs={{1,0},{2,1},{3,2},{4,3},{5,4},{6,5},{7,6},{8,7},{9,8},{10,9},{11,1... | collective-permute-start | bytes 144392 | tf_op jit(solution)/shard_map/ppermute | solution.py:39
  82.5 6.8 %collective-permute-start.2 = (f32[94,2,64]{2,0,1:T(8,128)S(1)}, f32[94,2,64]{2,0,1:T(8,128)S(1)}, u32[]{:S(2)}, u32[]{:S(2)}) collective-permute-start(f32[94,2,64]{2,0,1:T(8,128)S(1)} %get-tuple-element.70), channel_id=1, source_target_pairs={{0,1},{1,2},{2,3},{3,4},{4,5},{5,6},{6,7},{7,8},{8,9},{9,10},{10,1... | collective-permute-start | bytes 144392 | tf_op jit(solution)/shard_map/ppermute | solution.py:37
  89.5 0.6 copy-start.2
  133.5 1.5 copy-start.3
  135.4 25.9 %copy-start.1 = (f32[94,1504]{1,0:T(8,128)S(1)}, f32[94,1504]{1,0:T(8,128)}, u32[]{:S(2)}) copy-start(f32[94,1504]{1,0:T(8,128)} %and_convert_fusion) | copy-start | bytes 1696516

commit v4 on v2

--- a/solution.py
+++ b/solution.py
@@ -24,6 +24,7 @@
 LAG_CHUNKS = 11
 LAG_PAD = 132
 COL_TILE = 256
+VERT_MINOR = 4
 
 
 def extended_2(cells, sides, width):
@@ -110,6 +111,134 @@
     )(mid, vt)
 
 
+def mesh_peers(nx, nz):
+    me = lax.axis_index("vert")
+    tm = lax.axis_index("tm")
+    mx, mz = me // nz, me % nz
+    return me, tm, mx, mz
+
+
+def greet(mx, mz, tm, nx, nz):
+    barrier = pltpu.get_barrier_semaphore()
+    for k in range(1, nx):
+        pl.semaphore_signal(
+            barrier, inc=1, device_id=(lax.rem(mx + k, nx) * nz + mz, tm),
+            device_id_type=pl.DeviceIdType.MESH,
+        )
+    for k in range(1, nz):
+        pl.semaphore_signal(
+            barrier, inc=1, device_id=(mx * nz + lax.rem(mz + k, nz), tm),
+            device_id_type=pl.DeviceIdType.MESH,
+        )
+    pl.semaphore_wait(barrier, nx + nz - 2)
+
+
+def reduce_kernel(nx, nz, x_ref, out_ref, recv_a, part, recv_b, a_send, a_recv, b_send, b_recv):
+    me, tm, mx, mz = mesh_peers(nx, nz)
+    greet(mx, mz, tm, nx, nz)
+    copies = []
+    for k in range(1, nx):
+        px = lax.rem(mx + k, nx)
+        copy = pltpu.make_async_remote_copy(
+            src_ref=x_ref.at[pl.ds(px * nz, nz)], dst_ref=recv_a.at[k - 1],
+            send_sem=a_send.at[k - 1], recv_sem=a_recv.at[k - 1],
+            device_id=(px * nz + mz, tm), device_id_type=pl.DeviceIdType.MESH,
+        )
+        copy.start()
+        copies.append(copy)
+    for copy in copies:
+        copy.wait()
+    acc = x_ref[pl.ds(mx * nz, nz)]
+    for k in range(1, nx):
+        acc = acc + recv_a[k - 1]
+    part[...] = acc
+    copies = []
+    for k in range(1, nz):
+        pz = lax.rem(mz + k, nz)
+        copy = pltpu.make_async_remote_copy(
+            src_ref=part.at[pz], dst_ref=recv_b.at[k - 1],
+            send_sem=b_send.at[k - 1], recv_sem=b_recv.at[k - 1],
+            device_id=(mx * nz + pz, tm), device_id_type=pl.DeviceIdType.MESH,
+        )
+        copy.start()
+        copies.append(copy)
+    for copy in copies:
+        copy.wait()
+    total = part[mz]
+    for k in range(1, nz):
+        total = total + recv_b[k - 1]
+    out_ref[...] = total
+
+
+def reduce_to_owner(x, nx, nz):
+    n, rows, w = x.shape
+    return pl.pallas_call(
+        partial(reduce_kernel, nx, nz),
+        out_shape=jax.ShapeDtypeStruct((rows, w), x.dtype),
+        in_specs=[pl.BlockSpec(memory_space=pltpu.VMEM)],
+        out_specs=pl.BlockSpec(memory_space=pltpu.VMEM),
+        scratch_shapes=[
+            pltpu.VMEM((nx - 1, nz, rows, w), x.dtype),
+            pltpu.VMEM((nz, rows, w), x.dtype),
+            pltpu.VMEM((nz - 1, rows, w), x.dtype),
+            pltpu.SemaphoreType.DMA((nx - 1,)),
+            pltpu.SemaphoreType.DMA((nx - 1,)),
+            pltpu.SemaphoreType.DMA((nz - 1,)),
+            pltpu.SemaphoreType.DMA((nz - 1,)),
+        ],
+        compiler_params=pltpu.CompilerParams(collective_id=0, has_side_effects=True),
+    )(x)
+
+
+def gather_kernel(nx, nz, x_ref, out_ref, a_send, a_recv, b_send, b_recv, local_sem):
+    me, tm, mx, mz = mesh_peers(nx, nz)
+    greet(mx, mz, tm, nx, nz)
+    own = pltpu.make_async_copy(x_ref, out_ref.at[me], local_sem)
+    own.start()
+    copies = []
+    for k in range(1, nz):
+        pz = lax.rem(mz + k, nz)
+        copy = pltpu.make_async_remote_copy(
+            src_ref=x_ref, dst_ref=out_ref.at[me],
+            send_sem=a_send.at[k - 1], recv_sem=a_recv.at[k - 1],
+            device_id=(mx * nz + pz, tm), device_id_type=pl.DeviceIdType.MESH,
+        )
+        copy.start()
+        copies.append(copy)
+    own.wait()
+    for copy in copies:
+        copy.wait()
+    copies = []
+    for k in range(1, nx):
+        px = lax.rem(mx + k, nx)
+        copy = pltpu.make_async_remote_copy(
+            src_ref=out_ref.at[pl.ds(mx * nz, nz)], dst_ref=out_ref.at[pl.ds(mx * nz, nz)],
+            send_sem=b_send.at[k - 1], recv_sem=b_recv.at[k - 1],
+            device_id=(px * nz + mz, tm), device_id_type=pl.DeviceIdType.MESH,
+        )
+        copy.start()
+        copies.append(copy)
+    for copy in copies:
+        copy.wait()
+
+
+def gather_all(x, nx, nz):
+    return pl.pallas_call(
+        partial(gather_kernel, nx, nz),
+        out_shape=jax.ShapeDtypeStruct((nx * nz,) + x.shape, x.dtype),
+        in_specs=[pl.BlockSpec(memory_space=pl.ANY)],
+        out_specs=pl.BlockSpec(memory_space=pl.ANY),
+        scratch_shapes=[
+            pltpu.SemaphoreType.DMA((nz - 1,)),
+            pltpu.SemaphoreType.DMA((nz - 1,)),
+            pltpu.SemaphoreType.DMA((nx - 1,)),
+            pltpu.SemaphoreType.DMA((nx - 1,)),
+            pltpu.SemaphoreType.DMA(()),
+        ],
+        compiler_params=pltpu.CompilerParams(collective_id=1, has_side_effects=True),
+    )(x)
+
+
 def local(source, band_taps, smooth_taps, parcel_ids):
     vert_dev, t_dev = source.shape
     owners = lax.axis_size("vert")
@@ -146,12 +275,14 @@
         (global_ids[:, None, :] == wanted[None, :, None]).astype(jnp.bfloat16), axis=0
     )
     pooled = jnp.dot(hits, flat_env, preferred_element_type=jnp.float32)
-    own_sums = lax.psum_scatter(pooled, "vert", scatter_dimension=0, tiled=True)
+    nx = owners // VERT_MINOR
+    own_sums = reduce_to_owner(pooled.reshape(owners, par_dev, BANDS * t_dev), nx, VERT_MINOR)
     own_env = own_sums.reshape(par_dev, BANDS, t_dev)
     own_ext = extended_2(own_env, (("tm", 2),), LAG)
     centered, own_middle, own_spread = centered_rows(own_ext, t_dev)
 
-    gathered = lax.all_gather(centered.transpose(1, 0, 2), "vert", axis=1, tiled=True)
+    blocks = gather_all(centered.transpose(1, 0, 2), nx, VERT_MINOR)
+    gathered = blocks.transpose(1, 0, 2, 3).reshape(BANDS, total_par, 2 * LAG + t_dev)
     vis_mid = gathered[:, :, LAG : LAG + t_dev].astype(jnp.float32)
     vis_spread = lax.rsqrt(jnp.mean(vis_mid * vis_mid, axis=2) + EPSILON)
     cols = -(-total_par // COL_TILE) * COL_TILE

time: 214 us -> 148 us (0.69)
  the two profiles are of different devices: /device:TPU:8 before, /device:TPU:16 now
where the time goes in v4:
time: 148 us
  Pallas kernels  98.8 us (67%)
  local copies, waits for them, and re-layouts  15.8 us (11%)
  other arithmetic  9.79 us (7%)
  starting transfers between devices  9.58 us (6%)
  matrix products  9.33 us (6%)
  waiting for transfers between devices  3.98 us (3%)
    pallas_call x1, Pallas kernels, reduce_to_owner(): pl.pallas_call(partial(reduce_kernel, nx, nz), out_shape=jax.ShapeDtypeSt...  40.8 us
    pallas_call x1, Pallas kernels, gather_all(): pl.pallas_call(partial(gather_kernel, nx, nz), out_shape=jax.ShapeDtypeSt...  32.1 us
    pallas_call x1, Pallas kernels, lagged_energy(): pl.pallas_call(fold_kernel, out_shape=jax.ShapeDtypeStruct((bands, rows,...  25.8 us
    reduce_sum x1, other arithmetic, local(): jnp.sum((global_ids[:, None, :] == wanted[None, :, None]).astype(jnp.bflo...  6.03 us
    ppermute x2, starting transfers between devices, extended_2(): lax.ppermute(head, axis, [((i + 1) % count, i) for i in range(ends)])  5.07 us
    dot_general x1, local copies, waits for them, and re-layouts, local(): pooled = jnp.dot(hits, flat_env, preferred_element_type=jnp.float32)  4.93 us
    ppermute x2, starting transfers between devices, extended_2(): lax.ppermute(tail, axis, [(i, (i + 1) % count) for i in range(ends)])  4.51 us
    dot_general x1, matrix products, local(): pooled = jnp.dot(hits, flat_env, preferred_element_type=jnp.float32)  4.45 us
  transfers between devices with their start and end apart: 4, of which 1 were waited for; matrix products, arithmetic and copies ran while one was open for 10% of the time, Pallas kernels for 0%

profile of v4, /device:TPU:16, one launch (start us, length us, event | category | flops | bytes accessed | tf_op | source)
XLA Modules:
  0.0 147.9 jit_solution(15515899344551780041)
XLA Ops:
  0.0 1.2 fusion.17
  1.2 3.2 %collective-permute-start.1 = (bf16[1280,64]{1,0:T(8,128)(2,1)S(1)}, bf16[1280,64]{1,0:T(8,128)(2,1)S(1)}, u32[]{:S(2)}, u32[]{:S(2)}) collective-permute-start(bf16[1280,64]{1,0:T(8,128)(2,1)S(1)} %get-tuple-element.69), channel_id=1, source_target_pairs={{1,0},{2,1},{3,2},{4,3},{5,4},{6,5},{7,6},{8,7},{9,8},{10,9},{11,1... | collective-permute-start | bytes 491528 | tf_op jit(solution)/shard_map/ppermute | solution.py:40
  4.4 1.9 %collective-permute-start = (bf16[1280,64]{1,0:T(8,128)(2,1)S(1)}, bf16[1280,64]{1,0:T(8,128)(2,1)S(1)}, u32[]{:S(2)}, u32[]{:S(2)}) collective-permute-start(bf16[1280,64]{1,0:T(8,128)(2,1)S(1)} %get-tuple-element.68), channel_id=1, source_target_pairs={{0,1},{1,2},{2,3},{3,4},{4,5},{5,6},{6,7},{7,8},{8,9},{9,10},{10,1... | collective-permute-start | bytes 491528 | tf_op jit(solution)/shard_map/ppermute | solution.py:38
  6.4 0.8 broadcast_add_fusion
  7.2 1.0 and_convert_fusion
  8.1 6.0 %fusion.10 = bf16[1504,1280]{1,0:T(8,128)(2,1)} fusion(s32[3,1280]{1,0:T(4,128)S(1)} %broadcast_add_fusion), kind=kLoop, calls=%fused_computation.14 | loop fusion | flops 15400960 | bytes 3865600 | tf_op jit(solution)/shard_map/reduce_sum | solution.py:274
  14.2 4.9 %dot_general.15 = bf16[16,94,1280]{2,1,0:T(8,128)(2,1)} reshape(bf16[1504,1280]{1,0:T(8,128)(2,1)} %fusion.10) | data formatting | bytes 7700480 | tf_op jit(solution)/shard_map/dot_general | solution.py:277
  19.2 0.8 tile.9
  20.3 0.4 tile.21
  21.1 0.4 pad_maximum_fusion
  21.5 6.0 %while.10 = (s32[]{:T(128)}, bf16[10,128,2,128]{3,2,1,0:T(2,128)(2,1)S(1)}, bf16[10,128,256]{2,1,0:T(8,128)(2,1)S(1)}, bf16[256,768]{0,1:T(8,128)(2,1)S(1)}, bf16[2,192,128]{2,1,0:T(8,128)(2,1)S(1)}, /*index=5*/s32[]{:T(128)}) while((s32[]{:T(128)}, bf16[10,128,2,128]{3,2,1,0:T(2,128)(2,1)S(1)}, bf16[10,128,256]{2,1,0:T(8,128)(2,1)S(1)}, ...), condition=%wide.region_2.3_spmd, body=%wide.region_1.2_spmd.sunk | while | flops 63143936 | bytes 1540181 | solution.py:267
  21.5 0.3 fusion.34
  21.8 0.2 fusion.35
  22.1 0.2 fusion.34
  22.4 0.2 fusion.35
  22.7 0.3 fusion.34
  23.0 0.2 fusion.35
  23.3 0.2 fusion.34
  23.6 0.2 fusion.35
  23.9 0.3 fusion.34
  24.2 0.2 fusion.35
  24.5 0.2 fusion.34
  24.8 0.2 fusion.35
  25.1 0.2 fusion.34
  25.4 0.2 fusion.35
  25.7 0.3 fusion.34
  26.0 0.2 fusion.35
  26.3 0.2 fusion.34
  26.6 0.2 fusion.35
  26.9 0.3 fusion.34
  27.2 0.2 fusion.35
  27.5 0.4 reshape.131
  28.0 4.5 %fusion.19.x_ref = f32[16,94,256]{2,1,0:T(8,128)} fusion(bf16[16,94,1280]{2,1,0:T(8,128)(2,1)} %dot_general.15, bf16[1280,256,1]{1,0,2:T(8,128)(2,1)S(1)} %reshape.131), kind=kOutput, calls=%fused_computation.44 | convolution fusion | flops 985661440 | bytes 6045696 | tf_op jit(solution)/shard_map/dot_general | solution.py:277
  32.4 40.8 %shard_map.55 = f32[94,256]{1,0:T(8,128)} custom-call(f32[16,94,256]{2,1,0:T(8,128)} %fusion.19.x_ref), custom_call_target="tpu_custom_call" | custom-call | tf_op jit(solution)/shard_map/pallas_call | solution.py:175
  73.3 0.9 reshape.128
  74.3 1.9 %collective-permute-start.3 = (f32[94,2,64]{2,0,1:T(8,128)S(1)}, f32[94,2,64]{2,0,1:T(8,128)S(1)}, u32[]{:S(2)}, u32[]{:S(2)}) collective-permute-start(f32[94,2,64]{2,0,1:T(8,128)S(1)} %get-tuple-element.71), channel_id=1, source_target_pairs={{1,0},{2,1},{3,2},{4,3},{5,4},{6,5},{7,6},{8,7},{9,8},{10,9},{11,1... | collective-permute-start | bytes 144392 | tf_op jit(solution)/shard_map/ppermute | solution.py:40
  76.3 2.6 %collective-permute-start.2 = (f32[94,2,64]{2,0,1:T(8,128)S(1)}, f32[94,2,64]{2,0,1:T(8,128)S(1)}, u32[]{:S(2)}, u32[]{:S(2)}) collective-permute-start(f32[94,2,64]{2,0,1:T(8,128)S(1)} %get-tuple-element.70), channel_id=1, source_target_pairs={{0,1},{1,2},{2,3},{3,4},{4,5},{5,6},{6,7},{7,8},{8,9},{9,10},{10,1... | collective-permute-start | bytes 144392 | tf_op jit(solution)/shard_map/ppermute | solution.py:38
  79.1 4.0 %collective-permute-done.2 = f32[94,2,64]{2,0,1:T(8,128)S(1)} collective-permute-done((f32[94,2,64]{2,0,1:T(8,128)S(1)}, f32[94,2,64]{2,0,1:T(8,128)S(1)}, u32[]{:S(2)}, u32[]{:S(2)}) %collective-permute-start.2) | collective-permute-done | bytes 48160 | tf_op jit(solution)/shard_map/ppermute | solution.py:38
  83.4 0.5 copy-done.2
  83.9 32.1 %shard_map.56 = bf16[16,2,94,256]{3,2,1,0:T(8,128)(2,1)} custom-call(bf16[2,94,256]{2,1,0:T(8,128)(2,1)} %bitcast.58), custom_call_target="tpu_custom_call" | custom-call | tf_op jit(solution)/shard_map/pallas_call | solution.py:226
  116.0 1.5 %copy.58 = bf16[2,16,94,256]{3,2,1,0:T(8,128)(2,1)S(1)} copy(bf16[2,16,94,256]{3,2,0,1:T(8,128)(2,1)} %bitcast.55) | data formatting | bytes 3080192 | tf_op jit(solution)/shard_map/transpose | solution.py:285
  117.5 0.4 reshape.129
  118.0 0.7 copy.59
  118.7 0.7 multiply_reduce_fusion
  119.4 0.2 multiply_reduce_fusion.1
  119.8 25.8 %shard_map.57 = f32[2,96,1536]{2,1,0:T(8,128)S(1)} custom-call(bf16[2,96,256]{2,1,0:T(8,128)(2,1)S(1)} %pad.10.mid_ref, bf16[2,256,1536]{2,1,0:T(8,128)(2,1)S(1)} %pad_bitcast_fusion.vt_ref), custom_call_target="tpu_custom_call" | custom-call | flops 19931332608 | bytes 2850816 | tf_op jit(solution)/shard_map/pallas_call | solution.py:96
  145.7 0.3 fusion.13
  146.0 1.9 %copy.60 = f32[1,2,94,1504]{3,1,2,0:T(2,128)} copy(f32[1,2,94,1504]{3,2,1,0:T(8,128)S(1)} %fusion.13) | data formatting | bytes 2262016 | tf_op jit(solution)/shard_map/broadcast_in_dim | solution.py:302
  (48 shorter events, 2.3 us)
Async XLA Ops:
  1.2 19.8 %collective-permute-start.1 = (bf16[1280,64]{1,0:T(8,128)(2,1)S(1)}, bf16[1280,64]{1,0:T(8,128)(2,1)S(1)}, u32[]{:S(2)}, u32[]{:S(2)}) collective-permute-start(bf16[1280,64]{1,0:T(8,128)(2,1)S(1)} %get-tuple-element.69), channel_id=1, source_target_pairs={{1,0},{2,1},{3,2},{4,3},{5,4},{6,5},{7,6},{8,7},{9,8},{10,9},{11,1... | collective-permute-start | bytes 491528 | tf_op jit(solution)/shard_map/ppermute | solution.py:40
  4.4 16.7 %collective-permute-start = (bf16[1280,64]{1,0:T(8,128)(2,1)S(1)}, bf16[1280,64]{1,0:T(8,128)(2,1)S(1)}, u32[]{:S(2)}, u32[]{:S(2)}) collective-permute-start(bf16[1280,64]{1,0:T(8,128)(2,1)S(1)} %get-tuple-element.68), channel_id=1, source_target_pairs={{0,1},{1,2},{2,3},{3,4},{4,5},{5,6},{6,7},{7,8},{8,9},{9,10},{10,1... | collective-permute-start | bytes 491528 | tf_op jit(solution)/shard_map/ppermute | solution.py:38
  14.2 4.9 %copy-start.4 = (bf16[2,2,65]{2,1,0:T(2,128)(2,1)S(1)}, bf16[2,2,65]{2,1,0:T(2,128)(2,1)}, u32[]{:S(2)}) copy-start(bf16[2,2,65]{2,1,0:T(2,128)(2,1)} %param.8) | copy-start | bytes 1564
  19.1 1.1 copy-start.5
  20.0 1.0 copy-start
  74.3 4.8 %collective-permute-start.3 = (f32[94,2,64]{2,0,1:T(8,128)S(1)}, f32[94,2,64]{2,0,1:T(8,128)S(1)}, u32[]{:S(2)}, u32[]{:S(2)}) collective-permute-start(f32[94,2,64]{2,0,1:T(8,128)S(1)} %get-tuple-element.71), channel_id=1, source_target_pairs={{1,0},{2,1},{3,2},{4,3},{5,4},{6,5},{7,6},{8,7},{9,8},{10,9},{11,1... | collective-permute-start | bytes 144392 | tf_op jit(solution)/shard_map/ppermute | solution.py:40
  76.3 6.8 %collective-permute-start.2 = (f32[94,2,64]{2,0,1:T(8,128)S(1)}, f32[94,2,64]{2,0,1:T(8,128)S(1)}, u32[]{:S(2)}, u32[]{:S(2)}) collective-permute-start(f32[94,2,64]{2,0,1:T(8,128)S(1)} %get-tuple-element.70), channel_id=1, source_target_pairs={{0,1},{1,2},{2,3},{3,4},{4,5},{5,6},{6,7},{7,8},{8,9},{9,10},{10,1... | collective-permute-start | bytes 144392 | tf_op jit(solution)/shard_map/ppermute | solution.py:38
  83.3 0.6 copy-start.2
  117.9 1.5 copy-start.3
  119.8 25.9 %copy-start.1 = (f32[94,1504]{1,0:T(8,128)S(1)}, f32[94,1504]{1,0:T(8,128)}, u32[]{:S(2)}) copy-start(f32[94,1504]{1,0:T(8,128)} %and_convert_fusion) | copy-start | bytes 1696516

commit v5 on v4

--- a/solution.py
+++ b/solution.py
@@ -23,7 +23,6 @@
 ROW_PAD = 96
 LAG_CHUNKS = 11
 LAG_PAD = 132
-COL_TILE = 256
 VERT_MINOR = 4
 
 
@@ -63,52 +62,6 @@
     middle_wide = middle.astype(jnp.float32)
     spread = lax.rsqrt(jnp.mean(middle_wide * middle_wide, axis=2) + EPSILON)
     return (centered, middle, spread)
-
-
-def fold_kernel(mid_ref, vt_ref, out_ref, lhs_ref):
-    cols = vt_ref.shape[1]
-    base = mid_ref[...].astype(jnp.float32)
-    for q in range(NLAG):
-        lhs_ref[q * ROW_PAD : (q + 1) * ROW_PAD, :] = pltpu.roll(base, q, 1).astype(lhs_ref.dtype)
-    lhs_ref[NLAG * ROW_PAD :, :] = jnp.zeros(
-        ((LAG_PAD - NLAG) * ROW_PAD, lhs_ref.shape[1]), lhs_ref.dtype
-    )
-    step = LAG_PAD // LAG_CHUNKS
-
-    def column(c, carry):
-        first = pl.multiple_of(c * COL_TILE, COL_TILE)
-        rhs = vt_ref[:, pl.ds(first, COL_TILE)]
-        acc = jnp.zeros((ROW_PAD, COL_TILE), jnp.float32)
-        for h in range(LAG_CHUNKS):
-            rows = lhs_ref[h * step * ROW_PAD : (h + 1) * step * ROW_PAD, :]
-            r = jnp.dot(rows, rhs, preferred_element_type=jnp.float32)
-            acc = acc + (r * r).reshape(step, ROW_PAD, COL_TILE).sum(axis=0)
-        out_ref[:, pl.ds(first, COL_TILE)] = acc
-        return carry
-
-    lax.fori_loop(0, cols // COL_TILE, column, 0)
-
-
-def lagged_energy(mid, vt):
-    bands, rows, k = mid.shape
-    cols = vt.shape[2]
-    flops = 2 * bands * LAG_PAD * rows * k * cols
-    return pl.pallas_call(
-        fold_kernel,
-        out_shape=jax.ShapeDtypeStruct((bands, rows, cols), jnp.float32),
-        grid=(bands,),
-        in_specs=[
-            pl.BlockSpec((None, rows, k), lambda b: (b, 0, 0)),
-            pl.BlockSpec((None, k, cols), lambda b: (b, 0, 0)),
-        ],
-        out_specs=pl.BlockSpec((None, rows, cols), lambda b: (b, 0, 0)),
-        scratch_shapes=[pltpu.VMEM((LAG_PAD * rows, k), jnp.bfloat16)],
-        compiler_params=pltpu.CompilerParams(vmem_limit_bytes=48 * 1024 * 1024),
-        cost_estimate=pl.CostEstimate(
-            flops=flops, bytes_accessed=2 * (mid.size + vt.size) + 4 * bands * rows * cols,
-            transcendentals=0,
-        ),
-    )(mid, vt)
 
 
 def mesh_peers(nx, nz):
@@ -190,53 +143,112 @@
     )(x)
 
 
-def gather_kernel(nx, nz, x_ref, out_ref, a_send, a_recv, b_send, b_recv, local_sem):
+def fill_lags(mid_ref, lhs_ref, band):
+    rows = mid_ref.shape[1]
+    base = mid_ref[band].astype(jnp.float32)
+    for q in range(NLAG):
+        lhs_ref[band, q * rows : (q + 1) * rows, :] = pltpu.roll(base, q, 1).astype(lhs_ref.dtype)
+    lhs_ref[band, NLAG * rows :, :] = jnp.zeros(
+        ((LAG_PAD - NLAG) * rows, lhs_ref.shape[2]), lhs_ref.dtype
+    )
+
+
+def fold_group(g, group, lhs_ref, gath, out_ref, sums_ref, t_dev):
+    rows = out_ref.shape[1]
+    step = LAG_PAD // LAG_CHUNKS
+    first = pl.multiple_of(g * group, 128)
+    for band in range(out_ref.shape[0]):
+        block = gath[band, pl.ds(first, group), :].astype(jnp.float32)
+        rhs_wide = block.T
+        rhs = rhs_wide.astype(jnp.bfloat16)
+        middle = rhs_wide[LAG : LAG + t_dev, :]
+        sums_ref[band, :, pl.ds(first, group)] = jnp.sum(middle * middle, axis=0, keepdims=True)
+        acc = jnp.zeros((rows, group), jnp.float32)
+        for h in range(LAG_CHUNKS):
+            lhs = lhs_ref[band, h * step * rows : (h + 1) * step * rows, :]
+            r = jnp.dot(lhs, rhs, preferred_element_type=jnp.float32)
+            acc = acc + (r * r).reshape(step, rows, group).sum(axis=0)
+        out_ref[band, :, pl.ds(first, group)] = acc
+
+
+def gather_fold_kernel(nx, nz, t_dev, own_ref, mid_ref, out_ref, sums_ref, gath, lhs_ref,
+                       a_send, a_recv, b_send, b_recv, local_sem):
     me, tm, mx, mz = mesh_peers(nx, nz)
+    rows = own_ref.shape[1]
+    group = nz * rows
     greet(mx, mz, tm, nx, nz)
-    own = pltpu.make_async_copy(x_ref, out_ref.at[me], local_sem)
+    mine = gath.at[:, pl.ds(me * rows, rows), :]
+    own = pltpu.make_async_copy(own_ref, mine, local_sem)
     own.start()
     copies = []
     for k in range(1, nz):
-        pz = lax.rem(mz + k, nz)
         copy = pltpu.make_async_remote_copy(
-            src_ref=x_ref, dst_ref=out_ref.at[me],
+            src_ref=own_ref, dst_ref=mine,
             send_sem=a_send.at[k - 1], recv_sem=a_recv.at[k - 1],
-            device_id=(mx * nz + pz, tm), device_id_type=pl.DeviceIdType.MESH,
+            device_id=(mx * nz + lax.rem(mz + k, nz), tm), device_id_type=pl.DeviceIdType.MESH,
         )
         copy.start()
         copies.append(copy)
+    for band in range(mid_ref.shape[0]):
+        fill_lags(mid_ref, lhs_ref, band)
     own.wait()
     for copy in copies:
         copy.wait()
+    ours = gath.at[:, pl.ds(mx * group, group), :]
     copies = []
     for k in range(1, nx):
-        px = lax.rem(mx + k, nx)
         copy = pltpu.make_async_remote_copy(
-            src_ref=out_ref.at[pl.ds(mx * nz, nz)], dst_ref=out_ref.at[pl.ds(mx * nz, nz)],
+            src_ref=ours, dst_ref=ours,
             send_sem=b_send.at[k - 1], recv_sem=b_recv.at[k - 1],
-            device_id=(px * nz + mz, tm), device_id_type=pl.DeviceIdType.MESH,
+            device_id=(lax.rem(mx + k, nx) * nz + mz, tm), device_id_type=pl.DeviceIdType.MESH,
         )
         copy.start()
         copies.append(copy)
+    fold_group(mx, group, lhs_ref, gath, out_ref, sums_ref, t_dev)
+
+    def landed(k, carry):
+        pltpu.make_async_remote_copy(
+            src_ref=ours, dst_ref=ours,
+            send_sem=b_send.at[k - 1], recv_sem=b_recv.at[k - 1],
+            device_id=(lax.rem(mx + k, nx) * nz + mz, tm), device_id_type=pl.DeviceIdType.MESH,
+        ).wait_recv()
+        fold_group(lax.rem(mx + nx - k, nx), group, lhs_ref, gath, out_ref, sums_ref, t_dev)
+        return carry
+
+    lax.fori_loop(1, nx, landed, 0)
     for copy in copies:
-        copy.wait()
-
-
-def gather_all(x, nx, nz):
+        copy.wait_send()
+
+
+def gather_fold(own, mid, nx, nz, t_dev):
+    bands, rows, width = own.shape
+    cols = nx * nz * rows
+    flops = 2 * bands * LAG_PAD * rows * width * cols
     return pl.pallas_call(
-        partial(gather_kernel, nx, nz),
-        out_shape=jax.ShapeDtypeStruct((nx * nz,) + x.shape, x.dtype),
-        in_specs=[pl.BlockSpec(memory_space=pl.ANY)],
-        out_specs=pl.BlockSpec(memory_space=pl.ANY),
+        partial(gather_fold_kernel, nx, nz, t_dev),
+        out_shape=(
+            jax.ShapeDtypeStruct((bands, rows, cols), jnp.float32),
+            jax.ShapeDtypeStruct((bands, 1, cols), jnp.float32),
+        ),
+        in_specs=[pl.BlockSpec(memory_space=pltpu.VMEM)] * 2,
+        out_specs=(pl.BlockSpec(memory_space=pltpu.VMEM),) * 2,
         scratch_shapes=[
+            pltpu.VMEM((bands, cols, width), own.dtype),
+            pltpu.VMEM((bands, LAG_PAD * rows, width), jnp.bfloat16),
             pltpu.SemaphoreType.DMA((nz - 1,)),
             pltpu.SemaphoreType.DMA((nz - 1,)),
             pltpu.SemaphoreType.DMA((nx - 1,)),
             pltpu.SemaphoreType.DMA((nx - 1,)),
             pltpu.SemaphoreType.DMA(()),
         ],
-        compiler_params=pltpu.CompilerParams(collective_id=1, has_side_effects=True),
-    )(x)
+        compiler_params=pltpu.CompilerParams(
+            collective_id=1, has_side_effects=True, vmem_limit_bytes=48 * 1024 * 1024
+        ),
+        cost_estimate=pl.CostEstimate(
+            flops=flops, bytes_accessed=2 * (own.size + mid.size) + 4 * bands * (rows + 1) * cols,
+            transcendentals=0,
+        ),
+    )(own, mid)
 
 
 def local(source, band_taps, smooth_taps, parcel_ids):
@@ -281,16 +293,15 @@
     own_ext = extended_2(own_env, (("tm", 2),), LAG)
     centered, own_middle, own_spread = centered_rows(own_ext, t_dev)
 
-    blocks = gather_all(centered.transpose(1, 0, 2), nx, VERT_MINOR)
-    gathered = blocks.transpose(1, 0, 2, 3).reshape(BANDS, total_par, 2 * LAG + t_dev)
-    vis_mid = gathered[:, :, LAG : LAG + t_dev].astype(jnp.float32)
-    vis_spread = lax.rsqrt(jnp.mean(vis_mid * vis_mid, axis=2) + EPSILON)
-    cols = -(-total_par // COL_TILE) * COL_TILE
-    vt = jnp.pad(gathered, ((0, 0), (0, cols - total_par), (0, 0))).transpose(0, 2, 1)
+    own = jnp.pad(centered.transpose(1, 0, 2), ((0, 0), (0, ROW_PAD - par_dev), (0, 0)))
     mid = jnp.pad(
         own_middle.transpose(1, 0, 2), ((0, 0), (0, ROW_PAD - par_dev), (0, t_dev))
     )
-    energy = lagged_energy(mid, vt)[:, :par_dev, :total_par]
+    padded_energy, sums = gather_fold(own, mid, nx, VERT_MINOR, t_dev)
+    energy = padded_energy.reshape(BANDS, ROW_PAD, owners, ROW_PAD)[:, :par_dev, :, :par_dev]
+    energy = energy.reshape(BANDS, par_dev, total_par)
+    vis_sums = sums.reshape(BANDS, owners, ROW_PAD)[:, :, :par_dev].reshape(BANDS, total_par)
+    vis_spread = lax.rsqrt(vis_sums / t_dev + EPSILON)
 
     scale = own_spread.T[:, :, None] * vis_spread[:, None, :] / t_dev
     own_level = resolution_of(owner_start + lax.iota(jnp.int32, par_dev))

time: 148 us -> 143 us (0.966)
  the two profiles are of different devices: /device:TPU:16 before, /device:TPU:72 now
where the time goes in v5:
time: 143 us; the launch traced here: 142 us
  Pallas kernels  92.5 us (65%)
  local copies, waits for them, and re-layouts  14.8 us (10%)
  other arithmetic  11.7 us (8%)
  starting transfers between devices  9.58 us (7%)
  matrix products  9.31 us (7%)
  waiting for transfers between devices  3.98 us (3%)
    pallas_call x1, Pallas kernels, gather_fold(): pl.pallas_call(partial(gather_fold_kernel, nx, nz, t_dev), out_shape=(jax...  53.5 us
    pallas_call x1, Pallas kernels, reduce_to_owner(): pl.pallas_call(partial(reduce_kernel, nx, nz), out_shape=jax.ShapeDtypeSt...  39 us
    reduce_sum x1, other arithmetic, local(): jnp.sum((global_ids[:, None, :] == wanted[None, :, None]).astype(jnp.bflo...  6.03 us
    ppermute x2, starting transfers between devices, extended_2(): lax.ppermute(head, axis, [((i + 1) % count, i) for i in range(ends)])  5.07 us
    dot_general x1, local copies, waits for them, and re-layouts, local(): pooled = jnp.dot(hits, flat_env, preferred_element_type=jnp.float32)  4.93 us
    ppermute x2, starting transfers between devices, extended_2(): lax.ppermute(tail, axis, [(i, (i + 1) % count) for i in range(ends)])  4.51 us
    dot_general x1, matrix products, local(): pooled = jnp.dot(hits, flat_env, preferred_element_type=jnp.float32)  4.45 us
    ppermute x2, waiting for transfers between devices, extended_2(): lax.ppermute(tail, axis, [(i, (i + 1) % count) for i in range(ends)])  3.98 us
  transfers between devices with their start and end apart: 4, of which 1 were waited for; matrix products, arithmetic and copies ran while one was open for 9% of the time, Pallas kernels for 0%

profile of v5, /device:TPU:72, one launch (start us, length us, event | category | flops | bytes accessed | tf_op | source)
XLA Modules:
  0.0 142.5 jit_solution(6080991886105568628)
XLA Ops:
  0.0 1.3 fusion.18
  1.3 3.2 %collective-permute-start.1 = (bf16[1280,64]{1,0:T(8,128)(2,1)S(1)}, bf16[1280,64]{1,0:T(8,128)(2,1)}, u32[]{:S(2)}, u32[]{:S(2)}) collective-permute-start(bf16[1280,64]{1,0:T(8,128)(2,1)S(1)} %get-tuple-element.73), channel_id=1, source_target_pairs={{1,0},{2,1},{3,2},{4,3},{5,4},{6,5},{7,6},{8,7},{9,8},{10,9},{11,1... | collective-permute-start | bytes 491528 | tf_op jit(solution)/shard_map/ppermute | solution.py:39
  4.5 1.9 %collective-permute-start = (bf16[1280,64]{1,0:T(8,128)(2,1)S(1)}, bf16[1280,64]{1,0:T(8,128)(2,1)}, u32[]{:S(2)}, u32[]{:S(2)}) collective-permute-start(bf16[1280,64]{1,0:T(8,128)(2,1)S(1)} %get-tuple-element.72), channel_id=1, source_target_pairs={{0,1},{1,2},{2,3},{3,4},{4,5},{5,6},{6,7},{7,8},{8,9},{9,10},{10,1... | collective-permute-start | bytes 491528 | tf_op jit(solution)/shard_map/ppermute | solution.py:37
  6.6 0.1 and_convert_fusion
  6.7 6.0 %fusion.10 = bf16[1504,1280]{1,0:T(8,128)(2,1)} fusion(s32[3,1280]{1,0:T(4,128)S(1)} %broadcast_add_fusion), kind=kLoop, calls=%fused_computation.14 | loop fusion | flops 15400960 | bytes 3865600 | tf_op jit(solution)/shard_map/reduce_sum | solution.py:286
  12.7 4.9 %dot_general.15 = bf16[16,94,1280]{2,1,0:T(8,128)(2,1)} reshape(bf16[1504,1280]{1,0:T(8,128)(2,1)} %fusion.10) | data formatting | bytes 7700480 | tf_op jit(solution)/shard_map/dot_general | solution.py:289
  17.8 0.8 tile.9
  18.6 0.1 slice.46
  18.8 0.4 tile.21
  19.4 0.1 reshape.168
  19.7 1.5 %pad_maximum_fusion = bf16[1280,256]{1,0:T(8,128)(2,1)S(1)} fusion(bf16[1280,64]{1,0:T(8,128)(2,1)} %collective-permute-done.1, bf16[1280,128]{1,0:T(8,128)(2,1)S(1)} %copy-done, bf16[1280,64]{1,0:T(8,128)(2,1)} %collective-permute-done), kind=kLoop, calls=%fused_computation.18 | loop fusion | flops 1966080 | bytes 1310720 | tf_op jit(solution)/shard_map/concatenate | solution.py:35
  21.1 6.0 %while.10 = (s32[]{:T(128)}, bf16[10,128,2,128]{3,2,1,0:T(2,128)(2,1)S(1)}, bf16[10,128,256]{2,1,0:T(8,128)(2,1)S(1)}, bf16[256,768]{0,1:T(8,128)(2,1)S(1)}, bf16[2,192,128]{2,1,0:T(8,128)(2,1)S(1)}, /*index=5*/s32[]{:T(128)}) while((s32[]{:T(128)}, bf16[10,128,2,128]{3,2,1,0:T(2,128)(2,1)S(1)}, bf16[10,128,256]{2,1,0:T(8,128)(2,1)S(1)}, ...), condition=%wide.region_2.3_spmd, body=%wide.region_1.2_spmd.sunk | while | flops 63143936 | bytes 1540181 | solution.py:279
  21.1 0.3 fusion.35
  21.4 0.2 fusion.36
  21.7 0.2 fusion.35
  22.0 0.2 fusion.36
  22.3 0.3 fusion.35
  22.6 0.2 fusion.36
  22.9 0.2 fusion.35
  23.2 0.2 fusion.36
  23.5 0.2 fusion.35
  23.8 0.2 fusion.36
  24.1 0.3 fusion.35
  24.4 0.2 fusion.36
  24.8 0.2 fusion.35
  25.0 0.2 fusion.36
  25.4 0.3 fusion.35
  25.6 0.2 fusion.36
  26.0 0.2 fusion.35
  26.2 0.2 fusion.36
  26.6 0.3 fusion.35
  26.8 0.2 fusion.36
  27.2 0.4 reshape.175
  27.6 4.5 %fusion.20.x_ref = f32[16,94,256]{2,1,0:T(8,128)} fusion(bf16[16,94,1280]{2,1,0:T(8,128)(2,1)} %dot_general.15, bf16[1280,256,1]{1,0,2:T(8,128)(2,1)S(1)} %reshape.175), kind=kOutput, calls=%fused_computation.43 | convolution fusion | flops 985661440 | bytes 6045696 | tf_op jit(solution)/shard_map/dot_general | solution.py:289
  32.0 39.0 %shard_map.55 = f32[94,256]{1,0:T(8,128)} custom-call(f32[16,94,256]{2,1,0:T(8,128)} %fusion.20.x_ref), custom_call_target="tpu_custom_call" | custom-call | tf_op jit(solution)/shard_map/pallas_call | solution.py:128
  71.1 0.9 reshape.170
  72.1 1.9 %collective-permute-start.3 = (f32[94,2,64]{2,0,1:T(8,128)S(1)}, f32[94,2,64]{2,0,1:T(8,128)S(1)}, u32[]{:S(2)}, u32[]{:S(2)}) collective-permute-start(f32[94,2,64]{2,0,1:T(8,128)S(1)} %get-tuple-element.75), channel_id=1, source_target_pairs={{1,0},{2,1},{3,2},{4,3},{5,4},{6,5},{7,6},{8,7},{9,8},{10,9},{11,1... | collective-permute-start | bytes 144392 | tf_op jit(solution)/shard_map/ppermute | solution.py:39
  74.1 2.6 %collective-permute-start.2 = (f32[94,2,64]{2,0,1:T(8,128)S(1)}, f32[94,2,64]{2,0,1:T(8,128)S(1)}, u32[]{:S(2)}, u32[]{:S(2)}) collective-permute-start(f32[94,2,64]{2,0,1:T(8,128)S(1)} %get-tuple-element.74), channel_id=1, source_target_pairs={{0,1},{1,2},{2,3},{3,4},{4,5},{5,6},{6,7},{7,8},{8,9},{9,10},{10,1... | collective-permute-start | bytes 144392 | tf_op jit(solution)/shard_map/ppermute | solution.py:37
  76.6 0.2 reduce_sum.31
  76.9 4.0 %collective-permute-done.2 = f32[94,2,64]{2,0,1:T(8,128)S(1)} collective-permute-done((f32[94,2,64]{2,0,1:T(8,128)S(1)}, f32[94,2,64]{2,0,1:T(8,128)S(1)}, u32[]{:S(2)}, u32[]{:S(2)}) %collective-permute-start.2) | collective-permute-done | bytes 48160 | tf_op jit(solution)/shard_map/ppermute | solution.py:37
  80.9 0.2 fusion.13
  81.2 0.2 multiply_reduce_fusion
  81.4 53.5 %shard_map.56 = (f32[2,96,1536]{2,1,0:T(8,128)S(1)}, f32[2,1,1536]{2,1,0:T(1,128)S(1)}) custom-call(bf16[2,96,256]{2,1,0:T(8,128)(2,1)S(1)} %pad.10.own_ref, bf16[2,96,256]{2,1,0:T(8,128)(2,1)S(1)} %pad.11.mid_ref), custom_call_target="tpu_custom_call" | custom-call | flops 19931332608 | bytes 1388544 | tf_op jit(solution)/shard_map/pallas_call | solution.py:227
  134.9 0.5 reshape.171
  135.4 1.2 slice.51
  136.6 2.1 %reshape.177 = f32[1,2,94,1504]{3,2,1,0:T(8,128)S(1)} reshape(f32[2,94,16,94]{3,2,1,0:T(8,128)} %slice.51) | data formatting | bytes 2262016 | tf_op jit(solution)/shard_map/reshape | solution.py:302
  139.0 0.1 copy.49
  139.1 3.4 %fusion.12 = f32[1,2,94,1504]{3,1,2,0:T(2,128)} fusion(f32[1,2,94,1504]{3,2,1,0:T(8,128)S(1)} %reshape.177, f32[94,1504]{1,0:T(8,128)S(1)} %and_convert_fusion, f32[2,1504]{1,0:T(2,128)S(1)} %rsqrt.20, f32[2,94]{0,1:T(8,128)S(1)} %copy.49), kind=kLoop, calls=%fused_computation.17 | loop fusion | flops 1696512 | bytes 2840304 | tf_op jit(solution)/shard_map/div | solution.py:312
  (47 shorter events, 1.8 us)
Async XLA Ops:
  0.0 6.5 %copy-start.4 = (s32[3]{0:T(128)S(1)}, s32[3]{0:T(128)}, u32[]{:S(2)}) copy-start(s32[3]{0:T(128)} %constant.54.clone) | copy-start | bytes 40
  0.0 6.5 %copy-start.1 = (s32[3,1280]{1,0:T(4,128)S(1)}, s32[3,1280]{1,0:T(4,128)}, u32[]{:S(2)}) copy-start(s32[3,1280]{1,0:T(4,128)} %param.10) | copy-start | bytes 46084
  1.3 18.3 %collective-permute-start.1 = (bf16[1280,64]{1,0:T(8,128)(2,1)S(1)}, bf16[1280,64]{1,0:T(8,128)(2,1)}, u32[]{:S(2)}, u32[]{:S(2)}) collective-permute-start(bf16[1280,64]{1,0:T(8,128)(2,1)S(1)} %get-tuple-element.73), channel_id=1, source_target_pairs={{1,0},{2,1},{3,2},{4,3},{5,4},{6,5},{7,6},{8,7},{9,8},{10,9},{11,1... | collective-permute-start | bytes 491528 | tf_op jit(solution)/shard_map/ppermute | solution.py:39
  4.5 15.2 %collective-permute-start = (bf16[1280,64]{1,0:T(8,128)(2,1)S(1)}, bf16[1280,64]{1,0:T(8,128)(2,1)}, u32[]{:S(2)}, u32[]{:S(2)}) collective-permute-start(bf16[1280,64]{1,0:T(8,128)(2,1)S(1)} %get-tuple-element.72), channel_id=1, source_target_pairs={{0,1},{1,2},{2,3},{3,4},{4,5},{5,6},{6,7},{7,8},{8,9},{9,10},{10,1... | collective-permute-start | bytes 491528 | tf_op jit(solution)/shard_map/ppermute | solution.py:37
  12.7 4.9 %copy-start.2 = (bf16[2,2,65]{2,1,0:T(2,128)(2,1)S(1)}, bf16[2,2,65]{2,1,0:T(2,128)(2,1)}, u32[]{:S(2)}) copy-start(bf16[2,2,65]{2,1,0:T(2,128)(2,1)} %param.8) | copy-start | bytes 1564
  17.7 1.1 copy-start.3
  18.6 1.0 copy-start
  72.1 4.8 %collective-permute-start.3 = (f32[94,2,64]{2,0,1:T(8,128)S(1)}, f32[94,2,64]{2,0,1:T(8,128)S(1)}, u32[]{:S(2)}, u32[]{:S(2)}) collective-permute-start(f32[94,2,64]{2,0,1:T(8,128)S(1)} %get-tuple-element.75), channel_id=1, source_target_pairs={{1,0},{2,1},{3,2},{4,3},{5,4},{6,5},{7,6},{8,7},{9,8},{10,9},{11,1... | collective-permute-start | bytes 144392 | tf_op jit(solution)/shard_map/ppermute | solution.py:39
  74.1 6.8 %collective-permute-start.2 = (f32[94,2,64]{2,0,1:T(8,128)S(1)}, f32[94,2,64]{2,0,1:T(8,128)S(1)}, u32[]{:S(2)}, u32[]{:S(2)}) collective-permute-start(f32[94,2,64]{2,0,1:T(8,128)S(1)} %get-tuple-element.74), channel_id=1, source_target_pairs={{0,1},{1,2},{2,3},{3,4},{4,5},{5,6},{6,7},{7,8},{8,9},{9,10},{10,1... | collective-permute-start | bytes 144392 | tf_op jit(solution)/shard_map/ppermute | solution.py:37

commit v6 on v5

--- a/solution.py
+++ b/solution.py
@@ -157,7 +157,8 @@
     rows = out_ref.shape[1]
     step = LAG_PAD // LAG_CHUNKS
     first = pl.multiple_of(g * group, 128)
-    for band in range(out_ref.shape[0]):
+
+    def one_band(band, carry):
         block = gath[band, pl.ds(first, group), :].astype(jnp.float32)
         rhs_wide = block.T
         rhs = rhs_wide.astype(jnp.bfloat16)
@@ -169,6 +170,9 @@
             r = jnp.dot(lhs, rhs, preferred_element_type=jnp.float32)
             acc = acc + (r * r).reshape(step, rows, group).sum(axis=0)
         out_ref[band, :, pl.ds(first, group)] = acc
+        return carry
+
+    lax.fori_loop(0, out_ref.shape[0], one_band, 0)
 
 
 def gather_fold_kernel(nx, nz, t_dev, own_ref, mid_ref, out_ref, sums_ref, gath, lhs_ref,
@@ -194,33 +198,37 @@
     own.wait()
     for copy in copies:
         copy.wait()
-    ours = gath.at[:, pl.ds(mx * group, group), :]
-    copies = []
-    for k in range(1, nx):
-        copy = pltpu.make_async_remote_copy(
-            src_ref=ours, dst_ref=ours,
-            send_sem=b_send.at[k - 1], recv_sem=b_recv.at[k - 1],
-            device_id=(lax.rem(mx + k, nx) * nz + mz, tm), device_id_type=pl.DeviceIdType.MESH,
-        )
-        copy.start()
-        copies.append(copy)
+    left, right = lax.rem(mx + nx - 1, nx), lax.rem(mx + 1, nx)
+    half = group // 2
+
+    def ring_copy(start, size, peer, slot):
+        rows_at = gath.at[:, pl.ds(start, size), :]
+        return pltpu.make_async_remote_copy(
+            src_ref=rows_at, dst_ref=rows_at,
+            send_sem=b_send.at[slot], recv_sem=b_recv.at[slot],
+            device_id=(peer * nz + mz, tm), device_id_type=pl.DeviceIdType.MESH,
+        )
+
+    near = [ring_copy(mx * group, group, right, 0), ring_copy(mx * group, group, left, 1)]
+    for copy in near:
+        copy.start()
     fold_group(mx, group, lhs_ref, gath, out_ref, sums_ref, t_dev)
-
-    def landed(k, carry):
-        pltpu.make_async_remote_copy(
-            src_ref=ours, dst_ref=ours,
-            send_sem=b_send.at[k - 1], recv_sem=b_recv.at[k - 1],
-            device_id=(lax.rem(mx + k, nx) * nz + mz, tm), device_id_type=pl.DeviceIdType.MESH,
-        ).wait_recv()
-        fold_group(lax.rem(mx + nx - k, nx), group, lhs_ref, gath, out_ref, sums_ref, t_dev)
-        return carry
-
-    lax.fori_loop(1, nx, landed, 0)
-    for copy in copies:
+    for copy in near:
+        copy.wait_recv()
+    far = [ring_copy(left * group, half, right, 2), ring_copy(right * group + half, half, left, 3)]
+    for copy in far:
+        copy.start()
+    fold_group(left, group, lhs_ref, gath, out_ref, sums_ref, t_dev)
+    fold_group(right, group, lhs_ref, gath, out_ref, sums_ref, t_dev)
+    for copy in far:
+        copy.wait_recv()
+    fold_group(lax.rem(mx + 2, nx), group, lhs_ref, gath, out_ref, sums_ref, t_dev)
+    for copy in near + far:
         copy.wait_send()
 
 
 def gather_fold(own, mid, nx, nz, t_dev):
+    assert nx == 4
     bands, rows, width = own.shape
     cols = nx * nz * rows
     flops = 2 * bands * LAG_PAD * rows * width * cols
@@ -237,8 +245,8 @@
             pltpu.VMEM((bands, LAG_PAD * rows, width), jnp.bfloat16),
             pltpu.SemaphoreType.DMA((nz - 1,)),
             pltpu.SemaphoreType.DMA((nz - 1,)),
-            pltpu.SemaphoreType.DMA((nx - 1,)),
-            pltpu.SemaphoreType.DMA((nx - 1,)),
+            pltpu.SemaphoreType.DMA((4,)),
+            pltpu.SemaphoreType.DMA((4,)),
             pltpu.SemaphoreType.DMA(()),
         ],
         compiler_params=pltpu.CompilerParams(

time: 143 us -> 137 us (0.958)
  the two profiles are of different devices: /device:TPU:72 before, /device:TPU:8 now
where the time goes in v6:
time: 137 us; the launch traced here: 135 us
  Pallas kernels  85 us (62%)
  local copies, waits for them, and re-layouts  14.8 us (11%)
  other arithmetic  11.7 us (9%)
  starting transfers between devices  9.58 us (7%)
  matrix products  9.32 us (7%)
  waiting for transfers between devices  3.98 us (3%)
    pallas_call x1, Pallas kernels, gather_fold(): pl.pallas_call(partial(gather_fold_kernel, nx, nz, t_dev), out_shape=(jax...  44.1 us
    pallas_call x1, Pallas kernels, reduce_to_owner(): pl.pallas_call(partial(reduce_kernel, nx, nz), out_shape=jax.ShapeDtypeSt...  40.9 us
    reduce_sum x1, other arithmetic, local(): jnp.sum((global_ids[:, None, :] == wanted[None, :, None]).astype(jnp.bflo...  6.03 us
    ppermute x2, starting transfers between devices, extended_2(): lax.ppermute(head, axis, [((i + 1) % count, i) for i in range(ends)])  5.07 us
    dot_general x1, local copies, waits for them, and re-layouts, local(): pooled = jnp.dot(hits, flat_env, preferred_element_type=jnp.float32)  4.93 us
    ppermute x2, starting transfers between devices, extended_2(): lax.ppermute(tail, axis, [(i, (i + 1) % count) for i in range(ends)])  4.51 us
    dot_general x1, matrix products, local(): pooled = jnp.dot(hits, flat_env, preferred_element_type=jnp.float32)  4.45 us
    ppermute x2, waiting for transfers between devices, extended_2(): lax.ppermute(tail, axis, [(i, (i + 1) % count) for i in range(ends)])  3.98 us
  transfers between devices with their start and end apart: 4, of which 1 were waited for; matrix products, arithmetic and copies ran while one was open for 10% of the time, Pallas kernels for 0%

profile of v6, /device:TPU:8, one launch (start us, length us, event | category | flops | bytes accessed | tf_op | source)
XLA Modules:
  0.0 135.0 jit_solution(9944304651634698373)
XLA Ops:
  0.0 1.3 fusion.18
  1.3 3.2 %collective-permute-start.1 = (bf16[1280,64]{1,0:T(8,128)(2,1)S(1)}, bf16[1280,64]{1,0:T(8,128)(2,1)}, u32[]{:S(2)}, u32[]{:S(2)}) collective-permute-start(bf16[1280,64]{1,0:T(8,128)(2,1)S(1)} %get-tuple-element.73), channel_id=1, source_target_pairs={{1,0},{2,1},{3,2},{4,3},{5,4},{6,5},{7,6},{8,7},{9,8},{10,9},{11,1... | collective-permute-start | bytes 491528 | tf_op jit(solution)/shard_map/ppermute | solution.py:39
  4.5 1.9 %collective-permute-start = (bf16[1280,64]{1,0:T(8,128)(2,1)S(1)}, bf16[1280,64]{1,0:T(8,128)(2,1)}, u32[]{:S(2)}, u32[]{:S(2)}) collective-permute-start(bf16[1280,64]{1,0:T(8,128)(2,1)S(1)} %get-tuple-element.72), channel_id=1, source_target_pairs={{0,1},{1,2},{2,3},{3,4},{4,5},{5,6},{6,7},{7,8},{8,9},{9,10},{10,1... | collective-permute-start | bytes 491528 | tf_op jit(solution)/shard_map/ppermute | solution.py:37
  6.6 0.1 and_convert_fusion
  6.7 6.0 %fusion.10 = bf16[1504,1280]{1,0:T(8,128)(2,1)} fusion(s32[3,1280]{1,0:T(4,128)S(1)} %broadcast_add_fusion), kind=kLoop, calls=%fused_computation.14 | loop fusion | flops 15400960 | bytes 3865600 | tf_op jit(solution)/shard_map/reduce_sum | solution.py:294
  12.7 4.9 %dot_general.15 = bf16[16,94,1280]{2,1,0:T(8,128)(2,1)} reshape(bf16[1504,1280]{1,0:T(8,128)(2,1)} %fusion.10) | data formatting | bytes 7700480 | tf_op jit(solution)/shard_map/dot_general | solution.py:297
  17.8 0.8 tile.9
  18.6 0.1 slice.46
  18.8 0.4 tile.21
  19.4 0.1 reshape.168
  19.7 1.5 %pad_maximum_fusion = bf16[1280,256]{1,0:T(8,128)(2,1)S(1)} fusion(bf16[1280,64]{1,0:T(8,128)(2,1)} %collective-permute-done.1, bf16[1280,128]{1,0:T(8,128)(2,1)S(1)} %copy-done, bf16[1280,64]{1,0:T(8,128)(2,1)} %collective-permute-done), kind=kLoop, calls=%fused_computation.18 | loop fusion | flops 1966080 | bytes 1310720 | tf_op jit(solution)/shard_map/concatenate | solution.py:35
  21.1 6.0 %while.10 = (s32[]{:T(128)}, bf16[10,128,2,128]{3,2,1,0:T(2,128)(2,1)S(1)}, bf16[10,128,256]{2,1,0:T(8,128)(2,1)S(1)}, bf16[256,768]{0,1:T(8,128)(2,1)S(1)}, bf16[2,192,128]{2,1,0:T(8,128)(2,1)S(1)}, /*index=5*/s32[]{:T(128)}) while((s32[]{:T(128)}, bf16[10,128,2,128]{3,2,1,0:T(2,128)(2,1)S(1)}, bf16[10,128,256]{2,1,0:T(8,128)(2,1)S(1)}, ...), condition=%wide.region_2.3_spmd, body=%wide.region_1.2_spmd.sunk | while | flops 63143936 | bytes 1540181 | solution.py:287
  21.1 0.3 fusion.35
  21.4 0.2 fusion.36
  21.7 0.2 fusion.35
  22.0 0.2 fusion.36
  22.3 0.3 fusion.35
  22.6 0.2 fusion.36
  22.9 0.2 fusion.35
  23.2 0.2 fusion.36
  23.5 0.3 fusion.35
  23.8 0.2 fusion.36
  24.1 0.2 fusion.35
  24.4 0.2 fusion.36
  24.7 0.2 fusion.35
  25.0 0.2 fusion.36
  25.4 0.3 fusion.35
  25.6 0.2 fusion.36
  26.0 0.2 fusion.35
  26.2 0.2 fusion.36
  26.6 0.3 fusion.35
  26.8 0.2 fusion.36
  27.2 0.4 reshape.175
  27.6 4.5 %fusion.20.x_ref = f32[16,94,256]{2,1,0:T(8,128)} fusion(bf16[16,94,1280]{2,1,0:T(8,128)(2,1)} %dot_general.15, bf16[1280,256,1]{1,0,2:T(8,128)(2,1)S(1)} %reshape.175), kind=kOutput, calls=%fused_computation.43 | convolution fusion | flops 985661440 | bytes 6045696 | tf_op jit(solution)/shard_map/dot_general | solution.py:297
  32.0 40.9 %shard_map.55 = f32[94,256]{1,0:T(8,128)} custom-call(f32[16,94,256]{2,1,0:T(8,128)} %fusion.20.x_ref), custom_call_target="tpu_custom_call" | custom-call | tf_op jit(solution)/shard_map/pallas_call | solution.py:128
  72.9 0.9 reshape.170
  74.0 1.9 %collective-permute-start.3 = (f32[94,2,64]{2,0,1:T(8,128)S(1)}, f32[94,2,64]{2,0,1:T(8,128)S(1)}, u32[]{:S(2)}, u32[]{:S(2)}) collective-permute-start(f32[94,2,64]{2,0,1:T(8,128)S(1)} %get-tuple-element.75), channel_id=1, source_target_pairs={{1,0},{2,1},{3,2},{4,3},{5,4},{6,5},{7,6},{8,7},{9,8},{10,9},{11,1... | collective-permute-start | bytes 144392 | tf_op jit(solution)/shard_map/ppermute | solution.py:39
  75.9 2.6 %collective-permute-start.2 = (f32[94,2,64]{2,0,1:T(8,128)S(1)}, f32[94,2,64]{2,0,1:T(8,128)S(1)}, u32[]{:S(2)}, u32[]{:S(2)}) collective-permute-start(f32[94,2,64]{2,0,1:T(8,128)S(1)} %get-tuple-element.74), channel_id=1, source_target_pairs={{0,1},{1,2},{2,3},{3,4},{4,5},{5,6},{6,7},{7,8},{8,9},{9,10},{10,1... | collective-permute-start | bytes 144392 | tf_op jit(solution)/shard_map/ppermute | solution.py:37
  78.5 0.2 reduce_sum.31
  78.7 4.0 %collective-permute-done.2 = f32[94,2,64]{2,0,1:T(8,128)S(1)} collective-permute-done((f32[94,2,64]{2,0,1:T(8,128)S(1)}, f32[94,2,64]{2,0,1:T(8,128)S(1)}, u32[]{:S(2)}, u32[]{:S(2)}) %collective-permute-start.2) | collective-permute-done | bytes 48160 | tf_op jit(solution)/shard_map/ppermute | solution.py:37
  82.7 0.2 fusion.13
  83.0 0.2 multiply_reduce_fusion
  83.2 44.1 %shard_map.56 = (f32[2,96,1536]{2,1,0:T(8,128)S(1)}, f32[2,1,1536]{2,1,0:T(1,128)S(1)}) custom-call(bf16[2,96,256]{2,1,0:T(8,128)(2,1)S(1)} %pad.10.own_ref, bf16[2,96,256]{2,1,0:T(8,128)(2,1)S(1)} %pad.11.mid_ref), custom_call_target="tpu_custom_call" | custom-call | flops 19931332608 | bytes 1388544 | tf_op jit(solution)/shard_map/pallas_call | solution.py:235
  127.4 0.5 reshape.171
  127.9 1.2 slice.51
  129.1 2.1 %reshape.177 = f32[1,2,94,1504]{3,2,1,0:T(8,128)S(1)} reshape(f32[2,94,16,94]{3,2,1,0:T(8,128)} %slice.51) | data formatting | bytes 2262016 | tf_op jit(solution)/shard_map/reshape | solution.py:310
  131.5 0.1 copy.49
  131.6 3.4 %fusion.12 = f32[1,2,94,1504]{3,1,2,0:T(2,128)} fusion(f32[1,2,94,1504]{3,2,1,0:T(8,128)S(1)} %reshape.177, f32[94,1504]{1,0:T(8,128)S(1)} %and_convert_fusion, f32[2,1504]{1,0:T(2,128)S(1)} %rsqrt.20, f32[2,94]{0,1:T(8,128)S(1)} %copy.49), kind=kLoop, calls=%fused_computation.17 | loop fusion | flops 1696512 | bytes 2840304 | tf_op jit(solution)/shard_map/div | solution.py:320
  (47 shorter events, 1.8 us)
Async XLA Ops:
  0.0 6.5 %copy-start.4 = (s32[3]{0:T(128)S(1)}, s32[3]{0:T(128)}, u32[]{:S(2)}) copy-start(s32[3]{0:T(128)} %constant.54.clone) | copy-start | bytes 40
  0.0 6.5 %copy-start.1 = (s32[3,1280]{1,0:T(4,128)S(1)}, s32[3,1280]{1,0:T(4,128)}, u32[]{:S(2)}) copy-start(s32[3,1280]{1,0:T(4,128)} %param.10) | copy-start | bytes 46084
  1.3 18.3 %collective-permute-start.1 = (bf16[1280,64]{1,0:T(8,128)(2,1)S(1)}, bf16[1280,64]{1,0:T(8,128)(2,1)}, u32[]{:S(2)}, u32[]{:S(2)}) collective-permute-start(bf16[1280,64]{1,0:T(8,128)(2,1)S(1)} %get-tuple-element.73), channel_id=1, source_target_pairs={{1,0},{2,1},{3,2},{4,3},{5,4},{6,5},{7,6},{8,7},{9,8},{10,9},{11,1... | collective-permute-start | bytes 491528 | tf_op jit(solution)/shard_map/ppermute | solution.py:39
  4.5 15.2 %collective-permute-start = (bf16[1280,64]{1,0:T(8,128)(2,1)S(1)}, bf16[1280,64]{1,0:T(8,128)(2,1)}, u32[]{:S(2)}, u32[]{:S(2)}) collective-permute-start(bf16[1280,64]{1,0:T(8,128)(2,1)S(1)} %get-tuple-element.72), channel_id=1, source_target_pairs={{0,1},{1,2},{2,3},{3,4},{4,5},{5,6},{6,7},{7,8},{8,9},{9,10},{10,1... | collective-permute-start | bytes 491528 | tf_op jit(solution)/shard_map/ppermute | solution.py:37
  12.7 4.9 %copy-start.2 = (bf16[2,2,65]{2,1,0:T(2,128)(2,1)S(1)}, bf16[2,2,65]{2,1,0:T(2,128)(2,1)}, u32[]{:S(2)}) copy-start(bf16[2,2,65]{2,1,0:T(2,128)(2,1)} %param.8) | copy-start | bytes 1564
  17.7 1.1 copy-start.3
  18.6 1.0 copy-start
  74.0 4.8 %collective-permute-start.3 = (f32[94,2,64]{2,0,1:T(8,128)S(1)}, f32[94,2,64]{2,0,1:T(8,128)S(1)}, u32[]{:S(2)}, u32[]{:S(2)}) collective-permute-start(f32[94,2,64]{2,0,1:T(8,128)S(1)} %get-tuple-element.75), channel_id=1, source_target_pairs={{1,0},{2,1},{3,2},{4,3},{5,4},{6,5},{7,6},{8,7},{9,8},{10,9},{11,1... | collective-permute-start | bytes 144392 | tf_op jit(solution)/shard_map/ppermute | solution.py:39
  75.9 6.8 %collective-permute-start.2 = (f32[94,2,64]{2,0,1:T(8,128)S(1)}, f32[94,2,64]{2,0,1:T(8,128)S(1)}, u32[]{:S(2)}, u32[]{:S(2)}) collective-permute-start(f32[94,2,64]{2,0,1:T(8,128)S(1)} %get-tuple-element.74), channel_id=1, source_target_pairs={{0,1},{1,2},{2,3},{3,4},{4,5},{5,6},{6,7},{7,8},{8,9},{9,10},{10,1... | collective-permute-start | bytes 144392 | tf_op jit(solution)/shard_map/ppermute | solution.py:37

commit v7 on v6

--- a/solution.py
+++ b/solution.py
@@ -86,25 +86,35 @@
     pl.semaphore_wait(barrier, nx + nz - 2)
 
 
-def reduce_kernel(nx, nz, x_ref, out_ref, recv_a, part, recv_b, a_send, a_recv, b_send, b_recv):
+def reduce_kernel(nx, nz, x_ref, out_ref, recv_a, send_a, part, recv_b, a_send, a_recv, b_send, b_recv):
     me, tm, mx, mz = mesh_peers(nx, nz)
     greet(mx, mz, tm, nx, nz)
-    copies = []
-    for k in range(1, nx):
-        px = lax.rem(mx + k, nx)
-        copy = pltpu.make_async_remote_copy(
-            src_ref=x_ref.at[pl.ds(px * nz, nz)], dst_ref=recv_a.at[k - 1],
-            send_sem=a_send.at[k - 1], recv_sem=a_recv.at[k - 1],
-            device_id=(px * nz + mz, tm), device_id_type=pl.DeviceIdType.MESH,
-        )
-        copy.start()
-        copies.append(copy)
-    for copy in copies:
-        copy.wait()
-    acc = x_ref[pl.ds(mx * nz, nz)]
-    for k in range(1, nx):
-        acc = acc + recv_a[k - 1]
-    part[...] = acc
+    hz = nz // 2
+    peers = (lax.rem(mx + 1, nx), lax.rem(mx + nx - 1, nx))
+
+    def owners_of(g, d):
+        return pl.ds(g * nz + d * hz, hz)
+
+    for s in range(1, nx):
+        copies = []
+        for d in range(2):
+            g = lax.rem(mx + (s if d else nx * s - s), nx)
+            if s == 1:
+                src = x_ref.at[owners_of(g, d)]
+            else:
+                send_a[d, s - 2] = recv_a[d, s - 2] + x_ref[owners_of(g, d)]
+                src = send_a.at[d, s - 2]
+            copy = pltpu.make_async_remote_copy(
+                src_ref=src, dst_ref=recv_a.at[d, s - 1],
+                send_sem=a_send.at[d, s - 1], recv_sem=a_recv.at[d, s - 1],
+                device_id=(peers[d] * nz + mz, tm), device_id_type=pl.DeviceIdType.MESH,
+            )
+            copy.start()
+            copies.append(copy)
+        for copy in copies:
+            copy.wait()
+    for d in range(2):
+        part[d * hz : (d + 1) * hz] = recv_a[d, nx - 2] + x_ref[owners_of(mx, d)]
     copies = []
     for k in range(1, nz):
         pz = lax.rem(mz + k, nz)
@@ -125,17 +135,19 @@
 
 def reduce_to_owner(x, nx, nz):
     n, rows, w = x.shape
+    hz = nz // 2
     return pl.pallas_call(
         partial(reduce_kernel, nx, nz),
         out_shape=jax.ShapeDtypeStruct((rows, w), x.dtype),
         in_specs=[pl.BlockSpec(memory_space=pltpu.VMEM)],
         out_specs=pl.BlockSpec(memory_space=pltpu.VMEM),
         scratch_shapes=[
-            pltpu.VMEM((nx - 1, nz, rows, w), x.dtype),
+            pltpu.VMEM((2, nx - 1, hz, rows, w), x.dtype),
+            pltpu.VMEM((2, nx - 2, hz, rows, w), x.dtype),
             pltpu.VMEM((nz, rows, w), x.dtype),
             pltpu.VMEM((nz - 1, rows, w), x.dtype),
-            pltpu.SemaphoreType.DMA((nx - 1,)),
-            pltpu.SemaphoreType.DMA((nx - 1,)),
+            pltpu.SemaphoreType.DMA((2, nx - 1)),
+            pltpu.SemaphoreType.DMA((2, nx - 1)),
             pltpu.SemaphoreType.DMA((nz - 1,)),
             pltpu.SemaphoreType.DMA((nz - 1,)),
         ],

time: 137 us -> 135 us (0.985); the launches traced: 135 us -> 135 us
  Pallas kernels: 85 us -> 82 us
  starting transfers between devices: 9.58 us -> 11.9 us
    pallas_call x1, Pallas kernels: 40.9 us -> 36.8 us  [reduce_to_owner(): pl.pallas_call(partial(reduce_kernel, nx, nz), out_shape=jax.ShapeDtypeSt...]
    ppermute x2, starting transfers between devices: 5.07 us -> 7.84 us  [extended_2(): lax.ppermute(head, axis, [((i + 1) % count, i) for i in range(ends)])]
where the time goes in v7:
time: 135 us
  Pallas kernels  82 us (61%)
  local copies, waits for them, and re-layouts  14.8 us (11%)
  starting transfers between devices  11.9 us (9%)
  other arithmetic  11.7 us (9%)
  matrix products  9.32 us (7%)
  waiting for transfers between devices  4.47 us (3%)
    pallas_call x1, Pallas kernels, gather_fold(): pl.pallas_call(partial(gather_fold_kernel, nx, nz, t_dev), out_shape=(jax...  45.2 us
    pallas_call x1, Pallas kernels, reduce_to_owner(): pl.pallas_call(partial(reduce_kernel, nx, nz), out_shape=jax.ShapeDtypeSt...  36.8 us
    ppermute x2, starting transfers between devices, extended_2(): lax.ppermute(head, axis, [((i + 1) % count, i) for i in range(ends)])  7.84 us
    reduce_sum x1, other arithmetic, local(): jnp.sum((global_ids[:, None, :] == wanted[None, :, None]).astype(jnp.bflo...  6.03 us
    dot_general x1, local copies, waits for them, and re-layouts, local(): pooled = jnp.dot(hits, flat_env, preferred_element_type=jnp.float32)  4.93 us
    ppermute x2, waiting for transfers between devices, extended_2(): lax.ppermute(tail, axis, [(i, (i + 1) % count) for i in range(ends)])  4.46 us
    dot_general x1, matrix products, local(): pooled = jnp.dot(hits, flat_env, preferred_element_type=jnp.float32)  4.45 us
    ppermute x2, starting transfers between devices, extended_2(): lax.ppermute(tail, axis, [(i, (i + 1) % count) for i in range(ends)])  4.02 us
  transfers between devices with their start and end apart: 4, of which 1 were waited for; matrix products, arithmetic and copies ran while one was open for 10% of the time, Pallas kernels for 0%

profile of v7, /device:TPU:8, one launch (start us, length us, event | category | flops | bytes accessed | tf_op | source)
XLA Modules:
  0.0 134.8 jit_solution(17932416955939034513)
XLA Ops:
  0.0 1.3 fusion.18
  1.3 3.2 %collective-permute-start.1 = (bf16[1280,64]{1,0:T(8,128)(2,1)S(1)}, bf16[1280,64]{1,0:T(8,128)(2,1)}, u32[]{:S(2)}, u32[]{:S(2)}) collective-permute-start(bf16[1280,64]{1,0:T(8,128)(2,1)S(1)} %get-tuple-element.73), channel_id=1, source_target_pairs={{1,0},{2,1},{3,2},{4,3},{5,4},{6,5},{7,6},{8,7},{9,8},{10,9},{11,1... | collective-permute-start | bytes 491528 | tf_op jit(solution)/shard_map/ppermute | solution.py:39
  4.5 1.9 %collective-permute-start = (bf16[1280,64]{1,0:T(8,128)(2,1)S(1)}, bf16[1280,64]{1,0:T(8,128)(2,1)}, u32[]{:S(2)}, u32[]{:S(2)}) collective-permute-start(bf16[1280,64]{1,0:T(8,128)(2,1)S(1)} %get-tuple-element.72), channel_id=1, source_target_pairs={{0,1},{1,2},{2,3},{3,4},{4,5},{5,6},{6,7},{7,8},{8,9},{9,10},{10,1... | collective-permute-start | bytes 491528 | tf_op jit(solution)/shard_map/ppermute | solution.py:37
  6.6 0.1 and_convert_fusion
  6.7 6.0 %fusion.10 = bf16[1504,1280]{1,0:T(8,128)(2,1)} fusion(s32[3,1280]{1,0:T(4,128)S(1)} %broadcast_add_fusion), kind=kLoop, calls=%fused_computation.14 | loop fusion | flops 15400960 | bytes 3865600 | tf_op jit(solution)/shard_map/reduce_sum | solution.py:306
  12.7 4.9 %dot_general.15 = bf16[16,94,1280]{2,1,0:T(8,128)(2,1)} reshape(bf16[1504,1280]{1,0:T(8,128)(2,1)} %fusion.10) | data formatting | bytes 7700480 | tf_op jit(solution)/shard_map/dot_general | solution.py:309
  17.8 0.8 tile.9
  18.6 0.1 slice.46
  18.8 0.4 tile.21
  19.4 0.1 reshape.168
  19.7 1.5 %pad_maximum_fusion = bf16[1280,256]{1,0:T(8,128)(2,1)S(1)} fusion(bf16[1280,64]{1,0:T(8,128)(2,1)} %collective-permute-done.1, bf16[1280,128]{1,0:T(8,128)(2,1)S(1)} %copy-done, bf16[1280,64]{1,0:T(8,128)(2,1)} %collective-permute-done), kind=kLoop, calls=%fused_computation.18 | loop fusion | flops 1966080 | bytes 1310720 | tf_op jit(solution)/shard_map/concatenate | solution.py:35
  21.1 6.0 %while.10 = (s32[]{:T(128)}, bf16[10,128,2,128]{3,2,1,0:T(2,128)(2,1)S(1)}, bf16[10,128,256]{2,1,0:T(8,128)(2,1)S(1)}, bf16[256,768]{0,1:T(8,128)(2,1)S(1)}, bf16[2,192,128]{2,1,0:T(8,128)(2,1)S(1)}, /*index=5*/s32[]{:T(128)}) while((s32[]{:T(128)}, bf16[10,128,2,128]{3,2,1,0:T(2,128)(2,1)S(1)}, bf16[10,128,256]{2,1,0:T(8,128)(2,1)S(1)}, ...), condition=%wide.region_2.3_spmd, body=%wide.region_1.2_spmd.sunk | while | flops 63143936 | bytes 1540181 | solution.py:299
  21.1 0.3 fusion.35
  21.4 0.2 fusion.36
  21.7 0.2 fusion.35
  22.0 0.2 fusion.36
  22.3 0.3 fusion.35
  22.6 0.2 fusion.36
  22.9 0.2 fusion.35
  23.2 0.2 fusion.36
  23.5 0.3 fusion.35
  23.8 0.2 fusion.36
  24.1 0.2 fusion.35
  24.4 0.2 fusion.36
  24.7 0.2 fusion.35
  25.0 0.2 fusion.36
  25.4 0.3 fusion.35
  25.6 0.2 fusion.36
  26.0 0.2 fusion.35
  26.2 0.2 fusion.36
  26.6 0.3 fusion.35
  26.8 0.2 fusion.36
  27.2 0.4 reshape.175
  27.6 4.5 %fusion.20.x_ref = f32[16,94,256]{2,1,0:T(8,128)} fusion(bf16[16,94,1280]{2,1,0:T(8,128)(2,1)} %dot_general.15, bf16[1280,256,1]{1,0,2:T(8,128)(2,1)S(1)} %reshape.175), kind=kOutput, calls=%fused_computation.43 | convolution fusion | flops 985661440 | bytes 6045696 | tf_op jit(solution)/shard_map/dot_general | solution.py:309
  32.0 36.8 %shard_map.55 = f32[94,256]{1,0:T(8,128)} custom-call(f32[16,94,256]{2,1,0:T(8,128)} %fusion.20.x_ref), custom_call_target="tpu_custom_call" | custom-call | tf_op jit(solution)/shard_map/pallas_call | solution.py:139
  68.9 0.9 reshape.170
  69.9 4.7 %collective-permute-start.3 = (f32[94,2,64]{2,0,1:T(8,128)S(1)}, f32[94,2,64]{2,0,1:T(8,128)S(1)}, u32[]{:S(2)}, u32[]{:S(2)}) collective-permute-start(f32[94,2,64]{2,0,1:T(8,128)S(1)} %get-tuple-element.75), channel_id=1, source_target_pairs={{1,0},{2,1},{3,2},{4,3},{5,4},{6,5},{7,6},{8,7},{9,8},{10,9},{11,1... | collective-permute-start | bytes 144392 | tf_op jit(solution)/shard_map/ppermute | solution.py:39
  74.6 2.1 %collective-permute-start.2 = (f32[94,2,64]{2,0,1:T(8,128)S(1)}, f32[94,2,64]{2,0,1:T(8,128)S(1)}, u32[]{:S(2)}, u32[]{:S(2)}) collective-permute-start(f32[94,2,64]{2,0,1:T(8,128)S(1)} %get-tuple-element.74), channel_id=1, source_target_pairs={{0,1},{1,2},{2,3},{3,4},{4,5},{5,6},{6,7},{7,8},{8,9},{9,10},{10,1... | collective-permute-start | bytes 144392 | tf_op jit(solution)/shard_map/ppermute | solution.py:37
  76.7 0.2 reduce_sum.31
  77.0 4.5 %collective-permute-done.2 = f32[94,2,64]{2,0,1:T(8,128)S(1)} collective-permute-done((f32[94,2,64]{2,0,1:T(8,128)S(1)}, f32[94,2,64]{2,0,1:T(8,128)S(1)}, u32[]{:S(2)}, u32[]{:S(2)}) %collective-permute-start.2) | collective-permute-done | bytes 48160 | tf_op jit(solution)/shard_map/ppermute | solution.py:37
  81.5 0.2 fusion.13
  81.7 0.2 multiply_reduce_fusion
  81.9 45.2 %shard_map.56 = (f32[2,96,1536]{2,1,0:T(8,128)S(1)}, f32[2,1,1536]{2,1,0:T(1,128)S(1)}) custom-call(bf16[2,96,256]{2,1,0:T(8,128)(2,1)S(1)} %pad.10.own_ref, bf16[2,96,256]{2,1,0:T(8,128)(2,1)S(1)} %pad.11.mid_ref), custom_call_target="tpu_custom_call" | custom-call | flops 19931332608 | bytes 1388544 | tf_op jit(solution)/shard_map/pallas_call | solution.py:247
  127.2 0.5 reshape.171
  127.7 1.2 slice.51
  128.9 2.1 %reshape.177 = f32[1,2,94,1504]{3,2,1,0:T(8,128)S(1)} reshape(f32[2,94,16,94]{3,2,1,0:T(8,128)} %slice.51) | data formatting | bytes 2262016 | tf_op jit(solution)/shard_map/reshape | solution.py:322
  131.3 0.1 copy.49
  131.4 3.4 %fusion.12 = f32[1,2,94,1504]{3,1,2,0:T(2,128)} fusion(f32[1,2,94,1504]{3,2,1,0:T(8,128)S(1)} %reshape.177, f32[94,1504]{1,0:T(8,128)S(1)} %and_convert_fusion, f32[2,1504]{1,0:T(2,128)S(1)} %rsqrt.20, f32[2,94]{0,1:T(8,128)S(1)} %copy.49), kind=kLoop, calls=%fused_computation.17 | loop fusion | flops 1696512 | bytes 2840304 | tf_op jit(solution)/shard_map/div | solution.py:332
  (47 shorter events, 1.8 us)
Async XLA Ops:
  0.0 6.5 %copy-start.4 = (s32[3]{0:T(128)S(1)}, s32[3]{0:T(128)}, u32[]{:S(2)}) copy-start(s32[3]{0:T(128)} %constant.54.clone) | copy-start | bytes 40
  0.0 6.5 %copy-start.1 = (s32[3,1280]{1,0:T(4,128)S(1)}, s32[3,1280]{1,0:T(4,128)}, u32[]{:S(2)}) copy-start(s32[3,1280]{1,0:T(4,128)} %param.10) | copy-start | bytes 46084
  1.3 18.3 %collective-permute-start.1 = (bf16[1280,64]{1,0:T(8,128)(2,1)S(1)}, bf16[1280,64]{1,0:T(8,128)(2,1)}, u32[]{:S(2)}, u32[]{:S(2)}) collective-permute-start(bf16[1280,64]{1,0:T(8,128)(2,1)S(1)} %get-tuple-element.73), channel_id=1, source_target_pairs={{1,0},{2,1},{3,2},{4,3},{5,4},{6,5},{7,6},{8,7},{9,8},{10,9},{11,1... | collective-permute-start | bytes 491528 | tf_op jit(solution)/shard_map/ppermute | solution.py:39
  4.5 15.2 %collective-permute-start = (bf16[1280,64]{1,0:T(8,128)(2,1)S(1)}, bf16[1280,64]{1,0:T(8,128)(2,1)}, u32[]{:S(2)}, u32[]{:S(2)}) collective-permute-start(bf16[1280,64]{1,0:T(8,128)(2,1)S(1)} %get-tuple-element.72), channel_id=1, source_target_pairs={{0,1},{1,2},{2,3},{3,4},{4,5},{5,6},{6,7},{7,8},{8,9},{9,10},{10,1... | collective-permute-start | bytes 491528 | tf_op jit(solution)/shard_map/ppermute | solution.py:37
  12.7 4.9 %copy-start.2 = (bf16[2,2,65]{2,1,0:T(2,128)(2,1)S(1)}, bf16[2,2,65]{2,1,0:T(2,128)(2,1)}, u32[]{:S(2)}) copy-start(bf16[2,2,65]{2,1,0:T(2,128)(2,1)} %param.8) | copy-start | bytes 1564
  17.7 1.1 copy-start.3
  18.6 1.0 copy-start
  69.9 7.1 %collective-permute-start.3 = (f32[94,2,64]{2,0,1:T(8,128)S(1)}, f32[94,2,64]{2,0,1:T(8,128)S(1)}, u32[]{:S(2)}, u32[]{:S(2)}) collective-permute-start(f32[94,2,64]{2,0,1:T(8,128)S(1)} %get-tuple-element.75), channel_id=1, source_target_pairs={{1,0},{2,1},{3,2},{4,3},{5,4},{6,5},{7,6},{8,7},{9,8},{10,9},{11,1... | collective-permute-start | bytes 144392 | tf_op jit(solution)/shard_map/ppermute | solution.py:39
  74.6 6.8 %collective-permute-start.2 = (f32[94,2,64]{2,0,1:T(8,128)S(1)}, f32[94,2,64]{2,0,1:T(8,128)S(1)}, u32[]{:S(2)}, u32[]{:S(2)}) collective-permute-start(f32[94,2,64]{2,0,1:T(8,128)S(1)} %get-tuple-element.74), channel_id=1, source_target_pairs={{0,1},{1,2},{2,3},{3,4},{4,5},{5,6},{6,7},{7,8},{8,9},{9,10},{10,1... | collective-permute-start | bytes 144392 | tf_op jit(solution)/shard_map/ppermute | solution.py:37

commit v8 on v7

--- a/solution.py
+++ b/solution.py
@@ -271,6 +271,38 @@
     )(own, mid)
 
 
+def pool_kernel(par_dev, ids_ref, env_ref, out_ref):
+    rows = out_ref.shape[0]
+    vertices = env_ref.shape[0]
+    r = lax.broadcasted_iota(jnp.int32, (rows, vertices), 0)
+    wanted = pl.program_id(0) * par_dev + r
+    hits = jnp.zeros((rows, vertices), jnp.float32)
+    for level in range(ids_ref.shape[0]):
+        hits = hits + (ids_ref[level] == wanted).astype(jnp.float32)
+    hits = jnp.where(r < par_dev, hits, 0.0).astype(jnp.bfloat16)
+    out_ref[...] = jnp.dot(hits, env_ref[...], preferred_element_type=jnp.float32)
+
+
+def pool(global_ids, flat_env, owners, par_dev):
+    levels, vertices = global_ids.shape
+    width = flat_env.shape[1]
+    return pl.pallas_call(
+        partial(pool_kernel, par_dev),
+        out_shape=jax.ShapeDtypeStruct((owners, ROW_PAD, width), jnp.float32),
+        grid=(owners,),
+        in_specs=[
+            pl.BlockSpec((levels, 1, vertices), lambda k: (0, 0, 0)),
+            pl.BlockSpec((vertices, width), lambda k: (0, 0)),
+        ],
+        out_specs=pl.BlockSpec((None, ROW_PAD, width), lambda k: (k, 0, 0)),
+        cost_estimate=pl.CostEstimate(
+            flops=2 * owners * ROW_PAD * vertices * width,
+            bytes_accessed=4 * levels * vertices + 2 * vertices * width + 4 * owners * ROW_PAD * width,
+            transcendentals=0,
+        ),
+    )(global_ids.reshape(levels, 1, vertices), flat_env)
+
+
 def local(source, band_taps, smooth_taps, parcel_ids):
     vert_dev, t_dev = source.shape
     owners = lax.axis_size("vert")
@@ -302,13 +334,9 @@
     global_ids = parcel_ids + offsets[:, None]
     owner_start = lax.axis_index("vert") * par_dev
 
-    wanted = lax.iota(jnp.int32, total_par)
-    hits = jnp.sum(
-        (global_ids[:, None, :] == wanted[None, :, None]).astype(jnp.bfloat16), axis=0
-    )
-    pooled = jnp.dot(hits, flat_env, preferred_element_type=jnp.float32)
+    pooled = pool(global_ids, flat_env, owners, par_dev)
     nx = owners // VERT_MINOR
-    own_sums = reduce_to_owner(pooled.reshape(owners, par_dev, BANDS * t_dev), nx, VERT_MINOR)
+    own_sums = reduce_to_owner(pooled, nx, VERT_MINOR)[:par_dev]
     own_env = own_sums.reshape(par_dev, BANDS, t_dev)
     own_ext = extended_2(own_env, (("tm", 2),), LAG)
     centered, own_middle, own_spread = centered_rows(own_ext, t_dev)

time: 135 us -> 137 us (1.015)
  the two profiles are of different devices: /device:TPU:8 before, /device:TPU:72 now
where the time goes in v8:
time: 137 us; the launch traced here: 136 us
  Pallas kernels  96.4 us (70%)
  starting transfers between devices  13.1 us (10%)
  local copies, waits for them, and re-layouts  11.7 us (9%)
  other arithmetic  5.69 us (4%)
  matrix products  4.86 us (4%)
  waiting for transfers between devices  4.06 us (3%)
    pallas_call x1, Pallas kernels, gather_fold(): pl.pallas_call(partial(gather_fold_kernel, nx, nz, t_dev), out_shape=(jax...  48.8 us
    pallas_call x1, Pallas kernels, reduce_to_owner(): pl.pallas_call(partial(reduce_kernel, nx, nz), out_shape=jax.ShapeDtypeSt...  38.8 us
    ppermute x2, starting transfers between devices, extended_2(): lax.ppermute(head, axis, [((i + 1) % count, i) for i in range(ends)])  9.26 us
    pallas_call x1, Pallas kernels, pool(): pl.pallas_call(partial(pool_kernel, par_dev), out_shape=jax.ShapeDtypeStr...  8.76 us
    ppermute x2, starting transfers between devices, extended_2(): lax.ppermute(tail, axis, [(i, (i + 1) % count) for i in range(ends)])  3.83 us
    div x1, other arithmetic, local(): coupling = energy * scale * scale * same[None] / NLAG  3.42 us
    ppermute x2, waiting for transfers between devices, extended_2(): lax.ppermute(head, axis, [((i + 1) % count, i) for i in range(ends)])  2.79 us
  transfers between devices with their start and end apart: 4, of which 4 were waited for; matrix products, arithmetic and copies ran while one was open for 2% of the time, Pallas kernels for 0%

profile of v8, /device:TPU:72, one launch (start us, length us, event | category | flops | bytes accessed | tf_op | source)
XLA Modules:
  0.0 136.4 jit_solution(15357930681974861919)
XLA Ops:
  0.0 2.0 %fusion.16 = (bf16[1280,64]{1,0:T(8,128)(2,1)}, bf16[1280,64]{1,0:T(8,128)(2,1)}) fusion(bf16[1280,128]{1,0:T(8,128)(2,1)} %param.7), kind=kLoop, calls=%fused_computation.39 | loop fusion | bytes 655360 | tf_op jit(solution)/shard_map/slice | solution.py:34
  2.1 1.9 %collective-permute-start = (bf16[1280,64]{1,0:T(8,128)(2,1)}, bf16[1280,64]{1,0:T(8,128)(2,1)}, u32[]{:S(2)}, u32[]{:S(2)}) collective-permute-start(bf16[1280,64]{1,0:T(8,128)(2,1)} %get-tuple-element.67), channel_id=1, source_target_pairs={{0,1},{1,2},{2,3},{3,4},{4,5},{5,6},{6,7},{7,8},{8,9},{9,10},{10,1... | collective-permute-start | bytes 491528 | tf_op jit(solution)/shard_map/ppermute | solution.py:37
  4.0 4.5 %collective-permute-start.1 = (bf16[1280,64]{1,0:T(8,128)(2,1)}, bf16[1280,64]{1,0:T(8,128)(2,1)}, u32[]{:S(2)}, u32[]{:S(2)}) collective-permute-start(bf16[1280,64]{1,0:T(8,128)(2,1)} %get-tuple-element.68), channel_id=1, source_target_pairs={{1,0},{2,1},{3,2},{4,3},{5,4},{6,5},{7,6},{8,7},{9,8},{10,9},{11,1... | collective-permute-start | bytes 491528 | tf_op jit(solution)/shard_map/ppermute | solution.py:39
  8.6 0.1 and_convert_fusion
  8.9 0.8 tile.9
  10.0 0.4 tile.21
  10.5 0.1 reshape.169
  10.8 0.6 reshape.164.ids_ref
  11.4 0.6 collective-permute-done
  12.0 1.7 %collective-permute-done.1 = bf16[1280,64]{1,0:T(8,128)(2,1)} collective-permute-done((bf16[1280,64]{1,0:T(8,128)(2,1)}, bf16[1280,64]{1,0:T(8,128)(2,1)}, u32[]{:S(2)}, u32[]{:S(2)}) %collective-permute-start.1) | collective-permute-done | bytes 163872 | tf_op jit(solution)/shard_map/ppermute | solution.py:39
  13.7 1.5 %pad_maximum_fusion = bf16[1280,256]{1,0:T(8,128)(2,1)S(1)} fusion(bf16[1280,64]{1,0:T(8,128)(2,1)} %collective-permute-done.1, bf16[1280,128]{1,0:T(8,128)(2,1)S(1)} %copy-done, bf16[1280,64]{1,0:T(8,128)(2,1)} %collective-permute-done), kind=kLoop, calls=%fused_computation.16 | loop fusion | flops 1966080 | bytes 1310720 | tf_op jit(solution)/shard_map/concatenate | solution.py:35
  15.2 6.0 %while.10 = (s32[]{:T(128)}, bf16[10,128,2,128]{3,2,1,0:T(2,128)(2,1)S(1)}, bf16[10,128,256]{2,1,0:T(8,128)(2,1)S(1)}, bf16[256,768]{0,1:T(8,128)(2,1)S(1)}, bf16[2,192,128]{2,1,0:T(8,128)(2,1)S(1)}, /*index=5*/s32[]{:T(128)}) while((s32[]{:T(128)}, bf16[10,128,2,128]{3,2,1,0:T(2,128)(2,1)S(1)}, bf16[10,128,256]{2,1,0:T(8,128)(2,1)S(1)}, ...), condition=%wide.region_1.2_spmd, body=%wide.region_0.1_spmd.sunk | while | flops 63143936 | bytes 1540173 | solution.py:331
  15.2 0.3 fusion.30
  15.5 0.2 fusion.31
  15.8 0.2 fusion.30
  16.1 0.2 fusion.31
  16.4 0.3 fusion.30
  16.7 0.2 fusion.31
  17.0 0.2 fusion.30
  17.3 0.2 fusion.31
  17.6 0.3 fusion.30
  17.9 0.2 fusion.31
  18.2 0.2 fusion.30
  18.5 0.2 fusion.31
  18.8 0.2 fusion.30
  19.1 0.2 fusion.31
  19.4 0.3 fusion.30
  19.7 0.2 fusion.31
  20.0 0.2 fusion.30
  20.3 0.2 fusion.31
  20.6 0.3 fusion.30
  20.9 0.2 fusion.31
  21.2 0.9 copy.55
  22.1 8.8 %shard_map.55.x_ref = f32[16,96,256]{2,1,0:T(8,128)} custom-call(s32[3,1,1280]{2,1,0:T(1,128)} %reshape.164.ids_ref, bf16[1280,256]{1,0:T(8,128)(2,1)} %bitcast.60), custom_call_target="tpu_custom_call" | custom-call | flops 1006632960 | bytes 2243584 | tf_op jit(solution)/shard_map/pallas_call | solution.py:289
  30.9 38.8 %shard_map.56 = f32[96,256]{1,0:T(8,128)} custom-call(f32[16,96,256]{2,1,0:T(8,128)} %shard_map.55.x_ref), custom_call_target="tpu_custom_call" | custom-call | tf_op jit(solution)/shard_map/pallas_call | solution.py:139
  69.7 0.9 reshape.171
  70.7 1.9 %collective-permute-start.2 = (f32[94,2,64]{2,0,1:T(8,128)S(1)}, f32[94,2,64]{2,0,1:T(8,128)S(1)}, u32[]{:S(2)}, u32[]{:S(2)}) collective-permute-start(f32[94,2,64]{2,0,1:T(8,128)S(1)} %get-tuple-element.69), channel_id=1, source_target_pairs={{0,1},{1,2},{2,3},{3,4},{4,5},{5,6},{6,7},{7,8},{8,9},{9,10},{10,1... | collective-permute-start | bytes 144392 | tf_op jit(solution)/shard_map/ppermute | solution.py:37
  72.6 4.7 %collective-permute-start.3 = (f32[94,2,64]{2,0,1:T(8,128)S(1)}, f32[94,2,64]{2,0,1:T(8,128)S(1)}, u32[]{:S(2)}, u32[]{:S(2)}) collective-permute-start(f32[94,2,64]{2,0,1:T(8,128)S(1)} %get-tuple-element.70), channel_id=1, source_target_pairs={{1,0},{2,1},{3,2},{4,3},{5,4},{6,5},{7,6},{8,7},{9,8},{10,9},{11,1... | collective-permute-start | bytes 144392 | tf_op jit(solution)/shard_map/ppermute | solution.py:39
  77.4 0.2 reduce_sum.18
  77.6 0.7 collective-permute-done.2
  78.3 1.1 collective-permute-done.3
  79.4 0.2 fusion.11
  79.6 0.2 multiply_reduce_fusion
  79.9 48.8 %shard_map.57 = (f32[2,96,1536]{2,1,0:T(8,128)S(1)}, f32[2,1,1536]{2,1,0:T(1,128)S(1)}) custom-call(bf16[2,96,256]{2,1,0:T(8,128)(2,1)S(1)} %pad.10.own_ref, bf16[2,96,256]{2,1,0:T(8,128)(2,1)S(1)} %pad.11.mid_ref), custom_call_target="tpu_custom_call" | custom-call | flops 19931332608 | bytes 1388544 | tf_op jit(solution)/shard_map/pallas_call | solution.py:247
  128.7 0.5 reshape.172
  129.3 1.3 slice.55
  130.5 2.1 %reshape.176 = f32[1,2,94,1504]{3,2,1,0:T(8,128)S(1)} reshape(f32[2,94,16,94]{3,2,1,0:T(8,128)} %slice.55) | data formatting | bytes 2262016 | tf_op jit(solution)/shard_map/reshape | solution.py:350
  133.0 3.4 %fusion.10 = f32[1,2,94,1504]{3,1,2,0:T(2,128)} fusion(f32[1,2,94,1504]{3,2,1,0:T(8,128)S(1)} %reshape.176, f32[94,1504]{1,0:T(8,128)S(1)} %and_convert_fusion, f32[2,1504]{1,0:T(2,128)S(1)} %rsqrt.20, f32[2,94]{0,1:T(8,128)S(1)} %copy.40), kind=kLoop, calls=%fused_computation.14 | loop fusion | flops 1696512 | bytes 2840304 | tf_op jit(solution)/shard_map/div | solution.py:360
  (46 shorter events, 2.1 us)
Async XLA Ops:
  0.0 8.7 %copy-start.4 = (s32[3]{0:T(128)S(1)}, s32[3]{0:T(128)}, u32[]{:S(2)}) copy-start(s32[3]{0:T(128)} %constant.53.clone) | copy-start | bytes 40
  0.0 8.7 %copy-start.1 = (s32[3,1280]{1,0:T(4,128)S(1)}, s32[3,1280]{1,0:T(4,128)}, u32[]{:S(2)}) copy-start(s32[3,1280]{1,0:T(4,128)} %param.10) | copy-start | bytes 46084
  0.0 8.8 %copy-start.2 = (bf16[2,2,65]{2,1,0:T(2,128)(2,1)S(1)}, bf16[2,2,65]{2,1,0:T(2,128)(2,1)}, u32[]{:S(2)}) copy-start(bf16[2,2,65]{2,1,0:T(2,128)(2,1)} %param.8) | copy-start | bytes 1564
  2.1 9.9 %collective-permute-start = (bf16[1280,64]{1,0:T(8,128)(2,1)}, bf16[1280,64]{1,0:T(8,128)(2,1)}, u32[]{:S(2)}, u32[]{:S(2)}) collective-permute-start(bf16[1280,64]{1,0:T(8,128)(2,1)} %get-tuple-element.67), channel_id=1, source_target_pairs={{0,1},{1,2},{2,3},{3,4},{4,5},{5,6},{6,7},{7,8},{8,9},{9,10},{10,1... | collective-permute-start | bytes 491528 | tf_op jit(solution)/shard_map/ppermute | solution.py:37
  4.0 9.7 %collective-permute-start.1 = (bf16[1280,64]{1,0:T(8,128)(2,1)}, bf16[1280,64]{1,0:T(8,128)(2,1)}, u32[]{:S(2)}, u32[]{:S(2)}) collective-permute-start(bf16[1280,64]{1,0:T(8,128)(2,1)} %get-tuple-element.68), channel_id=1, source_target_pairs={{1,0},{2,1},{3,2},{4,3},{5,4},{6,5},{7,6},{8,7},{9,8},{10,9},{11,1... | collective-permute-start | bytes 491528 | tf_op jit(solution)/shard_map/ppermute | solution.py:39
  8.9 1.1 copy-start.3
  9.8 4.0 %copy-start = (bf16[1280,128]{1,0:T(8,128)(2,1)S(1)}, bf16[1280,128]{1,0:T(8,128)(2,1)}, u32[]{:S(2)}) copy-start(bf16[1280,128]{1,0:T(8,128)(2,1)} %param.7) | copy-start | bytes 983044
  70.7 7.6 %collective-permute-start.2 = (f32[94,2,64]{2,0,1:T(8,128)S(1)}, f32[94,2,64]{2,0,1:T(8,128)S(1)}, u32[]{:S(2)}, u32[]{:S(2)}) collective-permute-start(f32[94,2,64]{2,0,1:T(8,128)S(1)} %get-tuple-element.69), channel_id=1, source_target_pairs={{0,1},{1,2},{2,3},{3,4},{4,5},{5,6},{6,7},{7,8},{8,9},{9,10},{10,1... | collective-permute-start | bytes 144392 | tf_op jit(solution)/shard_map/ppermute | solution.py:37
  72.6 6.7 %collective-permute-start.3 = (f32[94,2,64]{2,0,1:T(8,128)S(1)}, f32[94,2,64]{2,0,1:T(8,128)S(1)}, u32[]{:S(2)}, u32[]{:S(2)}) collective-permute-start(f32[94,2,64]{2,0,1:T(8,128)S(1)} %get-tuple-element.70), channel_id=1, source_target_pairs={{1,0},{2,1},{3,2},{4,3},{5,4},{6,5},{7,6},{8,7},{9,8},{10,9},{11,1... | collective-permute-start | bytes 144392 | tf_op jit(solution)/shard_map/ppermute | solution.py:39

commit v9 on v8

--- a/solution.py
+++ b/solution.py
@@ -71,24 +71,22 @@
     return me, tm, mx, mz
 
 
-def greet(mx, mz, tm, nx, nz):
+def greet(mx, mz, tm, nx, nz, n_tm=0):
     barrier = pltpu.get_barrier_semaphore()
-    for k in range(1, nx):
-        pl.semaphore_signal(
-            barrier, inc=1, device_id=(lax.rem(mx + k, nx) * nz + mz, tm),
-            device_id_type=pl.DeviceIdType.MESH,
-        )
-    for k in range(1, nz):
-        pl.semaphore_signal(
-            barrier, inc=1, device_id=(mx * nz + lax.rem(mz + k, nz), tm),
-            device_id_type=pl.DeviceIdType.MESH,
-        )
-    pl.semaphore_wait(barrier, nx + nz - 2)
-
-
-def reduce_kernel(nx, nz, x_ref, out_ref, recv_a, send_a, part, recv_b, a_send, a_recv, b_send, b_recv):
+    me = mx * nz + mz
+    peers = [(lax.rem(mx + k, nx) * nz + mz, tm) for k in range(1, nx)]
+    peers += [(mx * nz + lax.rem(mz + k, nz), tm) for k in range(1, nz)]
+    if n_tm:
+        peers += [(me, lax.rem(tm + 1, n_tm)), (me, lax.rem(tm + n_tm - 1, n_tm))]
+    for peer in peers:
+        pl.semaphore_signal(barrier, inc=1, device_id=peer, device_id_type=pl.DeviceIdType.MESH)
+    pl.semaphore_wait(barrier, len(peers))
+
+
+def reduce_kernel(nx, nz, n_tm, x_ref, out_ref, recv_a, send_a, part, recv_b, mine, halo, a_send, a_recv,
+                  b_send, b_recv, t_send, t_recv):
     me, tm, mx, mz = mesh_peers(nx, nz)
-    greet(mx, mz, tm, nx, nz)
+    greet(mx, mz, tm, nx, nz, n_tm)
     hz = nz // 2
     peers = (lax.rem(mx + 1, nx), lax.rem(mx + nx - 1, nx))
 
@@ -130,15 +128,29 @@
     total = part[mz]
     for k in range(1, nz):
         total = total + recv_b[k - 1]
-    out_ref[...] = total
-
-
-def reduce_to_owner(x, nx, nz):
+    mine[...] = total
+    copies = []
+    for d, step in enumerate((1, n_tm - 1)):
+        copy = pltpu.make_async_remote_copy(
+            src_ref=mine, dst_ref=halo.at[d],
+            send_sem=t_send.at[d], recv_sem=t_recv.at[d],
+            device_id=(me, lax.rem(tm + step, n_tm)), device_id_type=pl.DeviceIdType.MESH,
+        )
+        copy.start()
+        copies.append(copy)
+    out_ref[1] = total
+    for copy in copies:
+        copy.wait()
+    out_ref[0] = halo[0]
+    out_ref[2] = halo[1]
+
+
+def reduce_to_owner(x, nx, nz, n_tm):
     n, rows, w = x.shape
     hz = nz // 2
     return pl.pallas_call(
-        partial(reduce_kernel, nx, nz),
-        out_shape=jax.ShapeDtypeStruct((rows, w), x.dtype),
+        partial(reduce_kernel, nx, nz, n_tm),
+        out_shape=jax.ShapeDtypeStruct((3, rows, w), x.dtype),
         in_specs=[pl.BlockSpec(memory_space=pltpu.VMEM)],
         out_specs=pl.BlockSpec(memory_space=pltpu.VMEM),
         scratch_shapes=[
@@ -146,10 +158,14 @@
             pltpu.VMEM((2, nx - 2, hz, rows, w), x.dtype),
             pltpu.VMEM((nz, rows, w), x.dtype),
             pltpu.VMEM((nz - 1, rows, w), x.dtype),
+            pltpu.VMEM((rows, w), x.dtype),
+            pltpu.VMEM((2, rows, w), x.dtype),
             pltpu.SemaphoreType.DMA((2, nx - 1)),
             pltpu.SemaphoreType.DMA((2, nx - 1)),
             pltpu.SemaphoreType.DMA((nz - 1,)),
             pltpu.SemaphoreType.DMA((nz - 1,)),
+            pltpu.SemaphoreType.DMA((2,)),
+            pltpu.SemaphoreType.DMA((2,)),
         ],
         compiler_params=pltpu.CompilerParams(collective_id=0, has_side_effects=True),
     )(x)
@@ -336,9 +352,12 @@
 
     pooled = pool(global_ids, flat_env, owners, par_dev)
     nx = owners // VERT_MINOR
-    own_sums = reduce_to_owner(pooled, nx, VERT_MINOR)[:par_dev]
-    own_env = own_sums.reshape(par_dev, BANDS, t_dev)
-    own_ext = extended_2(own_env, (("tm", 2),), LAG)
+    n_tm = lax.axis_size("tm")
+    tm = lax.axis_index("tm")
+    sums3 = reduce_to_owner(pooled, nx, VERT_MINOR, n_tm)[:, :par_dev].reshape(3, par_dev, BANDS, t_dev)
+    before = jnp.where(tm > 0, sums3[0, :, :, t_dev - LAG :], 0.0)
+    after = jnp.where(tm < n_tm - 1, sums3[2, :, :, :LAG], 0.0)
+    own_ext = jnp.concatenate([before, sums3[1], after], axis=2)
     centered, own_middle, own_spread = centered_rows(own_ext, t_dev)
 
     own = jnp.pad(centered.transpose(1, 0, 2), ((0, 0), (0, ROW_PAD - par_dev), (0, 0)))

time: 137 us -> 133 us (0.971)
  the two profiles are of different devices: /device:TPU:72 before, /device:TPU:8 now
where the time goes in v9:
time: 133 us
  Pallas kernels  101 us (76%)
  local copies, waits for them, and re-layouts  12.1 us (9%)
  starting transfers between devices  6.46 us (5%)
  other arithmetic  5.72 us (4%)
  matrix products  4.86 us (4%)
  waiting for transfers between devices  2 us (2%)
    pallas_call x1, Pallas kernels, gather_fold(): pl.pallas_call(partial(gather_fold_kernel, nx, nz, t_dev), out_shape=(jax...  49 us
    pallas_call x1, Pallas kernels, reduce_to_owner(): pl.pallas_call(partial(reduce_kernel, nx, nz, n_tm), out_shape=jax.ShapeD...  43.6 us
    pallas_call x1, Pallas kernels, pool(): pl.pallas_call(partial(pool_kernel, par_dev), out_shape=jax.ShapeDtypeStr...  8.73 us
    ppermute x1, starting transfers between devices, extended_2(): lax.ppermute(head, axis, [((i + 1) % count, i) for i in range(ends)])  4.54 us
    div x1, other arithmetic, local(): coupling = energy * scale * scale * same[None] / NLAG  3.41 us
  transfers between devices with their start and end apart: 2, of which 2 were waited for; matrix products, arithmetic and copies ran while one was open for 2% of the time, Pallas kernels for 0%

profile of v9, /device:TPU:8, one launch (start us, length us, event | category | flops | bytes accessed | tf_op | source)
XLA Modules:
  0.0 133.1 jit_solution(8191058506180820543)
XLA Ops:
  0.0 1.3 fusion.18
  1.3 1.9 %collective-permute-start = (bf16[1280,64]{1,0:T(8,128)(2,1)S(1)}, bf16[1280,64]{1,0:T(8,128)(2,1)}, u32[]{:S(2)}, u32[]{:S(2)}) collective-permute-start(bf16[1280,64]{1,0:T(8,128)(2,1)S(1)} %get-tuple-element.67), channel_id=1, source_target_pairs={{0,1},{1,2},{2,3},{3,4},{4,5},{5,6},{6,7},{7,8},{8,9},{9,10},{10,1... | collective-permute-start | bytes 491528 | tf_op jit(solution)/shard_map/ppermute | solution.py:37
  3.2 4.5 %collective-permute-start.1 = (bf16[1280,64]{1,0:T(8,128)(2,1)S(1)}, bf16[1280,64]{1,0:T(8,128)(2,1)}, u32[]{:S(2)}, u32[]{:S(2)}) collective-permute-start(bf16[1280,64]{1,0:T(8,128)(2,1)S(1)} %get-tuple-element.68), channel_id=1, source_target_pairs={{1,0},{2,1},{3,2},{4,3},{5,4},{6,5},{7,6},{8,7},{9,8},{10,9},{11,1... | collective-permute-start | bytes 491528 | tf_op jit(solution)/shard_map/ppermute | solution.py:39
  7.8 0.1 and_convert_fusion
  8.1 0.8 tile.9
  9.0 0.1 slice.56
  9.2 0.4 tile.21
  9.7 0.1 reshape.177
  10.0 0.6 reshape.172.ids_ref
  10.6 0.4 collective-permute-done
  11.0 1.6 %collective-permute-done.1 = bf16[1280,64]{1,0:T(8,128)(2,1)} collective-permute-done((bf16[1280,64]{1,0:T(8,128)(2,1)S(1)}, bf16[1280,64]{1,0:T(8,128)(2,1)}, u32[]{:S(2)}, u32[]{:S(2)}) %collective-permute-start.1) | collective-permute-done | bytes 163872 | tf_op jit(solution)/shard_map/ppermute | solution.py:39
  12.6 1.5 %pad_maximum_fusion = bf16[1280,256]{1,0:T(8,128)(2,1)S(1)} fusion(bf16[1280,64]{1,0:T(8,128)(2,1)} %collective-permute-done.1, bf16[1280,128]{1,0:T(8,128)(2,1)S(1)} %copy-done, bf16[1280,64]{1,0:T(8,128)(2,1)} %collective-permute-done), kind=kLoop, calls=%fused_computation.16 | loop fusion | flops 1966080 | bytes 1310720 | tf_op jit(solution)/shard_map/concatenate | solution.py:35
  14.1 6.0 %while.10 = (s32[]{:T(128)}, bf16[10,128,2,128]{3,2,1,0:T(2,128)(2,1)S(1)}, bf16[10,128,256]{2,1,0:T(8,128)(2,1)S(1)}, bf16[256,768]{0,1:T(8,128)(2,1)S(1)}, bf16[2,192,128]{2,1,0:T(8,128)(2,1)S(1)}, /*index=5*/s32[]{:T(128)}) while((s32[]{:T(128)}, bf16[10,128,2,128]{3,2,1,0:T(2,128)(2,1)S(1)}, bf16[10,128,256]{2,1,0:T(8,128)(2,1)S(1)}, ...), condition=%wide.region_1.2_spmd, body=%wide.region_0.1_spmd.sunk | while | flops 63143936 | bytes 1540173 | solution.py:347
  14.1 0.3 fusion.32
  14.4 0.2 fusion.33
  14.7 0.2 fusion.32
  15.0 0.2 fusion.33
  15.3 0.3 fusion.32
  15.6 0.2 fusion.33
  15.9 0.2 fusion.32
  16.2 0.2 fusion.33
  16.5 0.3 fusion.32
  16.8 0.2 fusion.33
  17.1 0.2 fusion.32
  17.4 0.2 fusion.33
  17.7 0.2 fusion.32
  18.0 0.2 fusion.33
  18.3 0.3 fusion.32
  18.6 0.2 fusion.33
  18.9 0.2 fusion.32
  19.2 0.2 fusion.33
  19.5 0.3 fusion.32
  19.8 0.2 fusion.33
  20.1 0.9 copy.63
  21.1 8.7 %shard_map.55.x_ref = f32[16,96,256]{2,1,0:T(8,128)} custom-call(s32[3,1,1280]{2,1,0:T(1,128)} %reshape.172.ids_ref, bf16[1280,256]{1,0:T(8,128)(2,1)} %bitcast.65), custom_call_target="tpu_custom_call" | custom-call | flops 1006632960 | bytes 2243584 | tf_op jit(solution)/shard_map/pallas_call | solution.py:305
  29.8 43.6 %shard_map.56 = f32[3,96,256]{2,1,0:T(8,128)} custom-call(f32[16,96,256]{2,1,0:T(8,128)} %shard_map.55.x_ref), custom_call_target="tpu_custom_call" | custom-call | tf_op jit(solution)/shard_map/pallas_call | solution.py:151
  73.4 0.9 slice.49
  74.3 1.1 reshape.179
  75.4 0.2 fusion.19
  75.7 0.2 reduce_sum.18
  75.9 0.2 fusion.11
  76.2 0.2 multiply_reduce_fusion
  76.4 49.0 %shard_map.57 = (f32[2,96,1536]{2,1,0:T(8,128)S(1)}, f32[2,1,1536]{2,1,0:T(1,128)S(1)}) custom-call(bf16[2,96,256]{2,1,0:T(8,128)(2,1)S(1)} %pad.10.own_ref, bf16[2,96,256]{2,1,0:T(8,128)(2,1)S(1)} %pad.11.mid_ref), custom_call_target="tpu_custom_call" | custom-call | flops 19931332608 | bytes 1388544 | tf_op jit(solution)/shard_map/pallas_call | solution.py:263
  125.5 0.5 reshape.180
  126.0 1.3 slice.61
  127.3 2.1 %reshape.184 = f32[1,2,94,1504]{3,2,1,0:T(8,128)S(1)} reshape(f32[2,94,16,94]{3,2,1,0:T(8,128)} %slice.61) | data formatting | bytes 2262016 | tf_op jit(solution)/shard_map/reshape | solution.py:369
  129.6 0.1 copy.40
  129.7 3.4 %fusion.10 = f32[1,2,94,1504]{3,1,2,0:T(2,128)} fusion(f32[1,2,94,1504]{3,2,1,0:T(8,128)S(1)} %reshape.184, f32[94,1504]{1,0:T(8,128)S(1)} %and_convert_fusion, f32[2,1504]{1,0:T(2,128)S(1)} %rsqrt.20, f32[2,94]{0,1:T(8,128)S(1)} %copy.40), kind=kLoop, calls=%fused_computation.14 | loop fusion | flops 1696512 | bytes 2840304 | tf_op jit(solution)/shard_map/div | solution.py:379
  (45 shorter events, 1.8 us)
Async XLA Ops:
  0.0 8.0 %copy-start.4 = (s32[3]{0:T(128)S(1)}, s32[3]{0:T(128)}, u32[]{:S(2)}) copy-start(s32[3]{0:T(128)} %constant.57.clone) | copy-start | bytes 40
  0.0 8.0 %copy-start.1 = (s32[3,1280]{1,0:T(4,128)S(1)}, s32[3,1280]{1,0:T(4,128)}, u32[]{:S(2)}) copy-start(s32[3,1280]{1,0:T(4,128)} %param.10) | copy-start | bytes 46084
  0.0 8.1 %copy-start.2 = (bf16[2,2,65]{2,1,0:T(2,128)(2,1)S(1)}, bf16[2,2,65]{2,1,0:T(2,128)(2,1)}, u32[]{:S(2)}) copy-start(bf16[2,2,65]{2,1,0:T(2,128)(2,1)} %param.8) | copy-start | bytes 1564
  1.3 9.7 %collective-permute-start = (bf16[1280,64]{1,0:T(8,128)(2,1)S(1)}, bf16[1280,64]{1,0:T(8,128)(2,1)}, u32[]{:S(2)}, u32[]{:S(2)}) collective-permute-start(bf16[1280,64]{1,0:T(8,128)(2,1)S(1)} %get-tuple-element.67), channel_id=1, source_target_pairs={{0,1},{1,2},{2,3},{3,4},{4,5},{5,6},{6,7},{7,8},{8,9},{9,10},{10,1... | collective-permute-start | bytes 491528 | tf_op jit(solution)/shard_map/ppermute | solution.py:37
  3.2 9.4 %collective-permute-start.1 = (bf16[1280,64]{1,0:T(8,128)(2,1)S(1)}, bf16[1280,64]{1,0:T(8,128)(2,1)}, u32[]{:S(2)}, u32[]{:S(2)}) collective-permute-start(bf16[1280,64]{1,0:T(8,128)(2,1)S(1)} %get-tuple-element.68), channel_id=1, source_target_pairs={{1,0},{2,1},{3,2},{4,3},{5,4},{6,5},{7,6},{8,7},{9,8},{10,9},{11,1... | collective-permute-start | bytes 491528 | tf_op jit(solution)/shard_map/ppermute | solution.py:39
  8.1 1.1 copy-start.3
  9.0 3.6 %copy-start = (bf16[1280,128]{1,0:T(8,128)(2,1)S(1)}, bf16[1280,128]{1,0:T(8,128)(2,1)}, u32[]{:S(2)}) copy-start(bf16[1280,128]{1,0:T(8,128)(2,1)} %param.7) | copy-start | bytes 983044

commit v10 on v9

--- a/solution.py
+++ b/solution.py
@@ -181,29 +181,31 @@
     )
 
 
-def fold_group(g, group, lhs_ref, gath, out_ref, sums_ref, t_dev):
+def fold_group(g, group, lhs_ref, gath, out_ref, spread_ref, level_ref, t_dev):
     rows = out_ref.shape[1]
     step = LAG_PAD // LAG_CHUNKS
     first = pl.multiple_of(g * group, 128)
+    same = (level_ref[:, 0:1] == level_ref[:, pl.ds(pl.multiple_of(g * group + 128, 128), group)]).astype(jnp.float32)
 
     def one_band(band, carry):
         block = gath[band, pl.ds(first, group), :].astype(jnp.float32)
         rhs_wide = block.T
         rhs = rhs_wide.astype(jnp.bfloat16)
         middle = rhs_wide[LAG : LAG + t_dev, :]
-        sums_ref[band, :, pl.ds(first, group)] = jnp.sum(middle * middle, axis=0, keepdims=True)
+        spread = lax.rsqrt(jnp.sum(middle * middle, axis=0, keepdims=True) / t_dev + EPSILON)
         acc = jnp.zeros((rows, group), jnp.float32)
         for h in range(LAG_CHUNKS):
             lhs = lhs_ref[band, h * step * rows : (h + 1) * step * rows, :]
             r = jnp.dot(lhs, rhs, preferred_element_type=jnp.float32)
             acc = acc + (r * r).reshape(step, rows, group).sum(axis=0)
-        out_ref[band, :, pl.ds(first, group)] = acc
+        scale = spread_ref[band] * spread / t_dev
+        out_ref[band, :, pl.ds(first, group)] = acc * (scale * scale) * same / NLAG
         return carry
 
     lax.fori_loop(0, out_ref.shape[0], one_band, 0)
 
 
-def gather_fold_kernel(nx, nz, t_dev, own_ref, mid_ref, out_ref, sums_ref, gath, lhs_ref,
+def gather_fold_kernel(nx, nz, t_dev, own_ref, mid_ref, spread_ref, level_ref, out_ref, gath, lhs_ref,
                        a_send, a_recv, b_send, b_recv, local_sem):
     me, tm, mx, mz = mesh_peers(nx, nz)
     rows = own_ref.shape[1]
@@ -240,34 +242,31 @@
     near = [ring_copy(mx * group, group, right, 0), ring_copy(mx * group, group, left, 1)]
     for copy in near:
         copy.start()
-    fold_group(mx, group, lhs_ref, gath, out_ref, sums_ref, t_dev)
+    fold_group(mx, group, lhs_ref, gath, out_ref, spread_ref, level_ref, t_dev)
     for copy in near:
         copy.wait_recv()
     far = [ring_copy(left * group, half, right, 2), ring_copy(right * group + half, half, left, 3)]
     for copy in far:
         copy.start()
-    fold_group(left, group, lhs_ref, gath, out_ref, sums_ref, t_dev)
-    fold_group(right, group, lhs_ref, gath, out_ref, sums_ref, t_dev)
+    fold_group(left, group, lhs_ref, gath, out_ref, spread_ref, level_ref, t_dev)
+    fold_group(right, group, lhs_ref, gath, out_ref, spread_ref, level_ref, t_dev)
     for copy in far:
         copy.wait_recv()
-    fold_group(lax.rem(mx + 2, nx), group, lhs_ref, gath, out_ref, sums_ref, t_dev)
+    fold_group(lax.rem(mx + 2, nx), group, lhs_ref, gath, out_ref, spread_ref, level_ref, t_dev)
     for copy in near + far:
         copy.wait_send()
 
 
-def gather_fold(own, mid, nx, nz, t_dev):
+def gather_fold(own, mid, spread, levels, nx, nz, t_dev):
     assert nx == 4
     bands, rows, width = own.shape
     cols = nx * nz * rows
     flops = 2 * bands * LAG_PAD * rows * width * cols
     return pl.pallas_call(
         partial(gather_fold_kernel, nx, nz, t_dev),
-        out_shape=(
-            jax.ShapeDtypeStruct((bands, rows, cols), jnp.float32),
-            jax.ShapeDtypeStruct((bands, 1, cols), jnp.float32),
-        ),
-        in_specs=[pl.BlockSpec(memory_space=pltpu.VMEM)] * 2,
-        out_specs=(pl.BlockSpec(memory_space=pltpu.VMEM),) * 2,
+        out_shape=jax.ShapeDtypeStruct((bands, rows, cols), jnp.float32),
+        in_specs=[pl.BlockSpec(memory_space=pltpu.VMEM)] * 4,
+        out_specs=pl.BlockSpec(memory_space=pltpu.VMEM),
         scratch_shapes=[
             pltpu.VMEM((bands, cols, width), own.dtype),
             pltpu.VMEM((bands, LAG_PAD * rows, width), jnp.bfloat16),
@@ -281,10 +280,10 @@
             collective_id=1, has_side_effects=True, vmem_limit_bytes=48 * 1024 * 1024
         ),
         cost_estimate=pl.CostEstimate(
-            flops=flops, bytes_accessed=2 * (own.size + mid.size) + 4 * bands * (rows + 1) * cols,
+            flops=flops, bytes_accessed=2 * (own.size + mid.size) + 4 * bands * rows * cols,
             transcendentals=0,
         ),
-    )(own, mid)
+    )(own, mid, spread, levels)
 
 
 def pool_kernel(par_dev, ids_ref, env_ref, out_ref):
@@ -364,19 +363,23 @@
     mid = jnp.pad(
         own_middle.transpose(1, 0, 2), ((0, 0), (0, ROW_PAD - par_dev), (0, t_dev))
     )
-    padded_energy, sums = gather_fold(own, mid, nx, VERT_MINOR, t_dev)
-    energy = padded_energy.reshape(BANDS, ROW_PAD, owners, ROW_PAD)[:, :par_dev, :, :par_dev]
-    energy = energy.reshape(BANDS, par_dev, total_par)
-    vis_sums = sums.reshape(BANDS, owners, ROW_PAD)[:, :, :par_dev].reshape(BANDS, total_par)
-    vis_spread = lax.rsqrt(vis_sums / t_dev + EPSILON)
-
-    scale = own_spread.T[:, :, None] * vis_spread[:, None, :] / t_dev
-    own_level = resolution_of(owner_start + lax.iota(jnp.int32, par_dev))
-    all_level = resolution_of(lax.iota(jnp.int32, total_par))
-    same = ((own_level[:, None] == all_level[None, :]) & (own_level[:, None] < 3)).astype(
-        jnp.float32
-    )
-    coupling = energy * scale * scale * same[None] / NLAG
+    spread = jnp.pad(own_spread.T, ((0, 0), (0, ROW_PAD - par_dev)))[:, :, None]
+    r = lax.iota(jnp.int32, ROW_PAD)
+    own_level = jnp.where(
+        r < par_dev, resolution_of(owner_start + r), -2
+    ).astype(jnp.float32)
+    own_level = jnp.where(own_level < 3, own_level, -2.0)
+    col = lax.iota(jnp.int32, owners * ROW_PAD)
+    col_level = jnp.where(
+        col % ROW_PAD < par_dev, resolution_of(col // ROW_PAD * par_dev + col % ROW_PAD), -1
+    ).astype(jnp.float32)
+    levels = jnp.concatenate(
+        [jnp.broadcast_to(own_level[:, None], (ROW_PAD, 128)),
+         jnp.broadcast_to(col_level[None, :], (ROW_PAD, owners * ROW_PAD))], axis=1
+    )
+    padded = gather_fold(own, mid, spread, levels, nx, VERT_MINOR, t_dev)
+    coupling = padded.reshape(BANDS, ROW_PAD, owners, ROW_PAD)[:, :par_dev, :, :par_dev]
+    coupling = coupling.reshape(BANDS, par_dev, total_par)
     return coupling[None]
 
 

time: 133 us -> 129 us (0.970)
  other arithmetic: 5.72 us -> 2.16 us
    div x1 -> x0, other arithmetic: 3.41 us -> none  [local(): coupling = energy * scale * scale * same[None] / NLAG]
    another operation x0 -> x2, local copies, waits for them, and re-layouts: none -> 2.64 us  [local(): return coupling[None]]
    reshape x3 -> x1, local copies, waits for them, and re-layouts: 2.68 us -> 0.53 us  [local(): padded.reshape(BANDS, ROW_PAD, owners, ROW_PAD)[:, :par_dev, :, :par_dev]]
where the time goes in v10:
time: 129 us
  Pallas kernels  102 us (79%)
  local copies, waits for them, and re-layouts  11.4 us (9%)
  starting transfers between devices  6.46 us (5%)
  matrix products  4.86 us (4%)
  other arithmetic  2.16 us (2%)
  waiting for transfers between devices  2.01 us (2%)
    pallas_call x1, Pallas kernels, gather_fold(): pl.pallas_call(partial(gather_fold_kernel, nx, nz, t_dev), out_shape=jax....  49.4 us
    pallas_call x1, Pallas kernels, reduce_to_owner(): pl.pallas_call(partial(reduce_kernel, nx, nz, n_tm), out_shape=jax.ShapeD...  43.6 us
    pallas_call x1, Pallas kernels, pool(): pl.pallas_call(partial(pool_kernel, par_dev), out_shape=jax.ShapeDtypeStr...  8.71 us
    ppermute x1, starting transfers between devices, extended_2(): lax.ppermute(head, axis, [((i + 1) % count, i) for i in range(ends)])  4.54 us
    another operation x2, local copies, waits for them, and re-layouts, local(): return coupling[None]  2.64 us
  transfers between devices with their start and end apart: 2, of which 2 were waited for; matrix products, arithmetic and copies ran while one was open for 2% of the time, Pallas kernels for 0%

profile of v10, /device:TPU:8, one launch (start us, length us, event | category | flops | bytes accessed | tf_op | source)
XLA Modules:
  0.0 129.2 jit_solution(15605688300617559593)
XLA Ops:
  0.0 1.3 fusion.25
  1.3 1.9 %collective-permute-start = (bf16[1280,64]{1,0:T(8,128)(2,1)S(1)}, bf16[1280,64]{1,0:T(8,128)(2,1)}, u32[]{:S(2)}, u32[]{:S(2)}) collective-permute-start(bf16[1280,64]{1,0:T(8,128)(2,1)S(1)} %get-tuple-element.63), channel_id=1, source_target_pairs={{0,1},{1,2},{2,3},{3,4},{4,5},{5,6},{6,7},{7,8},{8,9},{9,10},{10,1... | collective-permute-start | bytes 491528 | tf_op jit(solution)/shard_map/ppermute | solution.py:37
  3.2 4.5 %collective-permute-start.1 = (bf16[1280,64]{1,0:T(8,128)(2,1)S(1)}, bf16[1280,64]{1,0:T(8,128)(2,1)}, u32[]{:S(2)}, u32[]{:S(2)}) collective-permute-start(bf16[1280,64]{1,0:T(8,128)(2,1)S(1)} %get-tuple-element.64), channel_id=1, source_target_pairs={{1,0},{2,1},{3,2},{4,3},{5,4},{6,5},{7,6},{8,7},{9,8},{10,9},{11,1... | collective-permute-start | bytes 491528 | tf_op jit(solution)/shard_map/ppermute | solution.py:39
  8.1 0.8 tile.9
  9.0 0.1 slice.52
  9.2 0.4 tile.21
  9.7 0.1 reshape.107
  9.9 0.1 copy.36
  10.0 0.6 reshape.102.ids_ref
  10.6 0.4 collective-permute-done
  11.0 1.6 %collective-permute-done.1 = bf16[1280,64]{1,0:T(8,128)(2,1)} collective-permute-done((bf16[1280,64]{1,0:T(8,128)(2,1)S(1)}, bf16[1280,64]{1,0:T(8,128)(2,1)}, u32[]{:S(2)}, u32[]{:S(2)}) %collective-permute-start.1) | collective-permute-done | bytes 163872 | tf_op jit(solution)/shard_map/ppermute | solution.py:39
  12.6 1.5 %pad_maximum_fusion = bf16[1280,256]{1,0:T(8,128)(2,1)S(1)} fusion(bf16[1280,64]{1,0:T(8,128)(2,1)} %collective-permute-done.1, bf16[1280,128]{1,0:T(8,128)(2,1)S(1)} %copy-done, bf16[1280,64]{1,0:T(8,128)(2,1)} %collective-permute-done), kind=kLoop, calls=%fused_computation.13 | loop fusion | flops 1966080 | bytes 1310720 | tf_op jit(solution)/shard_map/concatenate | solution.py:35
  14.1 6.0 %while.10 = (s32[]{:T(128)}, bf16[10,128,2,128]{3,2,1,0:T(2,128)(2,1)S(1)}, bf16[10,128,256]{2,1,0:T(8,128)(2,1)S(1)}, bf16[256,768]{0,1:T(8,128)(2,1)S(1)}, bf16[2,192,128]{2,1,0:T(8,128)(2,1)S(1)}, /*index=5*/s32[]{:T(128)}) while((s32[]{:T(128)}, bf16[10,128,2,128]{3,2,1,0:T(2,128)(2,1)S(1)}, bf16[10,128,256]{2,1,0:T(8,128)(2,1)S(1)}, ...), condition=%wide.region_1.2_spmd, body=%wide.region_0.1_spmd.sunk | while | flops 63143936 | bytes 1540173 | solution.py:346
  14.1 0.3 fusion.39
  14.4 0.2 fusion.40
  14.7 0.2 fusion.39
  15.0 0.2 fusion.40
  15.3 0.3 fusion.39
  15.6 0.2 fusion.40
  15.9 0.2 fusion.39
  16.2 0.2 fusion.40
  16.5 0.3 fusion.39
  16.8 0.2 fusion.40
  17.1 0.2 fusion.39
  17.4 0.2 fusion.40
  17.7 0.2 fusion.39
  18.0 0.2 fusion.40
  18.3 0.3 fusion.39
  18.6 0.2 fusion.40
  18.9 0.2 fusion.39
  19.2 0.2 fusion.40
  19.5 0.3 fusion.39
  19.8 0.2 fusion.40
  20.1 0.9 copy.65
  21.1 8.7 %shard_map.55.x_ref = f32[16,96,256]{2,1,0:T(8,128)} custom-call(s32[3,1,1280]{2,1,0:T(1,128)} %reshape.102.ids_ref, bf16[1280,256]{1,0:T(8,128)(2,1)} %bitcast.67), custom_call_target="tpu_custom_call" | custom-call | flops 1006632960 | bytes 2243584 | tf_op jit(solution)/shard_map/pallas_call | solution.py:304
  29.8 43.6 %shard_map.56 = f32[3,96,256]{2,1,0:T(8,128)} custom-call(f32[16,96,256]{2,1,0:T(8,128)} %shard_map.55.x_ref), custom_call_target="tpu_custom_call" | custom-call | tf_op jit(solution)/shard_map/pallas_call | solution.py:151
  73.4 0.9 slice.46
  74.3 1.1 reshape.109
  75.4 0.2 fusion.26
  75.6 0.2 reduce_sum.18
  75.9 0.2 fusion.9
  76.2 0.2 multiply_reduce_fusion
  76.4 0.1 copy.42.spread_ref
  76.6 49.4 %shard_map.57 = f32[2,96,1536]{2,1,0:T(8,128)S(1)} custom-call(bf16[2,96,256]{2,1,0:T(8,128)(2,1)S(1)} %pad.14.own_ref, bf16[2,96,256]{2,1,0:T(8,128)(2,1)S(1)} %pad.15.mid_ref, f32[2,96,1]{2,1,0:T(8,128)S(1)} %copy.42.spread_ref, f32[96,1664]{1,0:T(8,128)S(1)} %pad_maximum_fusion.1.level_ref), custom_call_target="tpu_custom_call" | custom-call | flops 19931332608 | bytes 1376256 | tf_op jit(solution)/shard_map/pallas_call | solution.py:265
  125.9 0.5 reshape.110
  126.5 0.1 slice.57
  126.6 0.7 reshape.112
  127.3 1.9 %copy.45 = f32[1,2,94,1504]{3,1,2,0:T(2,128)} copy(f32[1,2,94,1504]{3,2,1,0:T(8,128)S(1)} %reshape.112) | data formatting | bytes 2262016 | tf_op jit(solution)/shard_map/broadcast_in_dim;reshape | solution.py:383
  (43 shorter events, 1.6 us)
Async XLA Ops:
  0.0 7.9 %copy-start.4 = (s32[3]{0:T(128)S(1)}, s32[3]{0:T(128)}, u32[]{:S(2)}) copy-start(s32[3]{0:T(128)} %constant.79.clone) | copy-start | bytes 40
  0.0 8.0 %copy-start.1 = (s32[3,1280]{1,0:T(4,128)S(1)}, s32[3,1280]{1,0:T(4,128)}, u32[]{:S(2)}) copy-start(s32[3,1280]{1,0:T(4,128)} %param.10) | copy-start | bytes 46084
  0.0 8.0 %copy-start.2 = (bf16[2,2,65]{2,1,0:T(2,128)(2,1)S(1)}, bf16[2,2,65]{2,1,0:T(2,128)(2,1)}, u32[]{:S(2)}) copy-start(bf16[2,2,65]{2,1,0:T(2,128)(2,1)} %param.8) | copy-start | bytes 1564
  1.3 9.7 %collective-permute-start = (bf16[1280,64]{1,0:T(8,128)(2,1)S(1)}, bf16[1280,64]{1,0:T(8,128)(2,1)}, u32[]{:S(2)}, u32[]{:S(2)}) collective-permute-start(bf16[1280,64]{1,0:T(8,128)(2,1)S(1)} %get-tuple-element.63), channel_id=1, source_target_pairs={{0,1},{1,2},{2,3},{3,4},{4,5},{5,6},{6,7},{7,8},{8,9},{9,10},{10,1... | collective-permute-start | bytes 491528 | tf_op jit(solution)/shard_map/ppermute | solution.py:37
  3.2 9.4 %collective-permute-start.1 = (bf16[1280,64]{1,0:T(8,128)(2,1)S(1)}, bf16[1280,64]{1,0:T(8,128)(2,1)}, u32[]{:S(2)}, u32[]{:S(2)}) collective-permute-start(bf16[1280,64]{1,0:T(8,128)(2,1)S(1)} %get-tuple-element.64), channel_id=1, source_target_pairs={{1,0},{2,1},{3,2},{4,3},{5,4},{6,5},{7,6},{8,7},{9,8},{10,9},{11,1... | collective-permute-start | bytes 491528 | tf_op jit(solution)/shard_map/ppermute | solution.py:39
  8.1 1.1 copy-start.3
  9.0 3.7 %copy-start = (bf16[1280,128]{1,0:T(8,128)(2,1)S(1)}, bf16[1280,128]{1,0:T(8,128)(2,1)}, u32[]{:S(2)}) copy-start(bf16[1280,128]{1,0:T(8,128)(2,1)} %param.7) | copy-start | bytes 983044

commit v11 on v10

--- a/solution.py
+++ b/solution.py
@@ -286,30 +286,31 @@
     )(own, mid, spread, levels)
 
 
-def pool_kernel(par_dev, ids_ref, env_ref, out_ref):
-    rows = out_ref.shape[0]
-    vertices = env_ref.shape[0]
-    r = lax.broadcasted_iota(jnp.int32, (rows, vertices), 0)
-    wanted = pl.program_id(0) * par_dev + r
-    hits = jnp.zeros((rows, vertices), jnp.float32)
-    for level in range(ids_ref.shape[0]):
-        hits = hits + (ids_ref[level] == wanted).astype(jnp.float32)
-    hits = jnp.where(r < par_dev, hits, 0.0).astype(jnp.bfloat16)
-    out_ref[...] = jnp.dot(hits, env_ref[...], preferred_element_type=jnp.float32)
+def pool_kernel(par_dev, per_step, ids_ref, env_ref, out_ref):
+    rows = out_ref.shape[1]
+    r = lax.broadcasted_iota(jnp.int32, (rows, 1), 0)
+    env = env_ref[...]
+    for o in range(per_step):
+        wanted = jnp.where(r < par_dev, (pl.program_id(0) * per_step + o) * par_dev + r, -1)
+        hits = (ids_ref[0] == wanted).astype(jnp.float32)
+        for level in range(1, ids_ref.shape[0]):
+            hits = hits + (ids_ref[level] == wanted).astype(jnp.float32)
+        out_ref[o] = jnp.dot(hits.astype(jnp.bfloat16), env, preferred_element_type=jnp.float32)
 
 
 def pool(global_ids, flat_env, owners, par_dev):
     levels, vertices = global_ids.shape
     width = flat_env.shape[1]
+    per_step = 4
     return pl.pallas_call(
-        partial(pool_kernel, par_dev),
+        partial(pool_kernel, par_dev, per_step),
         out_shape=jax.ShapeDtypeStruct((owners, ROW_PAD, width), jnp.float32),
-        grid=(owners,),
+        grid=(owners // per_step,),
         in_specs=[
             pl.BlockSpec((levels, 1, vertices), lambda k: (0, 0, 0)),
             pl.BlockSpec((vertices, width), lambda k: (0, 0)),
         ],
-        out_specs=pl.BlockSpec((None, ROW_PAD, width), lambda k: (k, 0, 0)),
+        out_specs=pl.BlockSpec((per_step, ROW_PAD, width), lambda k: (k, 0, 0)),
         cost_estimate=pl.CostEstimate(
             flops=2 * owners * ROW_PAD * vertices * width,
             bytes_accessed=4 * levels * vertices + 2 * vertices * width + 4 * owners * ROW_PAD * width,

time: 129 us -> 125 us (0.969)
  Pallas kernels: 102 us -> 97.6 us
    pallas_call x1, Pallas kernels: 8.71 us -> 4.68 us  [pool(): pl.pallas_call(partial(pool_kernel, par_dev, per_step), out_shape=jax.Sha...]
where the time goes in v11:
time: 125 us
  Pallas kernels  97.6 us (78%)
  local copies, waits for them, and re-layouts  11.4 us (9%)
  starting transfers between devices  6.46 us (5%)
  matrix products  4.86 us (4%)
  other arithmetic  2.16 us (2%)
  waiting for transfers between devices  2.01 us (2%)
    pallas_call x1, Pallas kernels, gather_fold(): pl.pallas_call(partial(gather_fold_kernel, nx, nz, t_dev), out_shape=jax....  49.3 us
    pallas_call x1, Pallas kernels, reduce_to_owner(): pl.pallas_call(partial(reduce_kernel, nx, nz, n_tm), out_shape=jax.ShapeD...  43.6 us
    pallas_call x1, Pallas kernels, pool(): pl.pallas_call(partial(pool_kernel, par_dev, per_step), out_shape=jax.Sha...  4.68 us
    ppermute x1, starting transfers between devices, extended_2(): lax.ppermute(head, axis, [((i + 1) % count, i) for i in range(ends)])  4.54 us
    another operation x2, local copies, waits for them, and re-layouts, local(): return coupling[None]  2.64 us
    dot_general x10, matrix products, filter_block(): jnp.dot(block, first_mat, preferred_element_type=jnp.float32)  2.53 us
  transfers between devices with their start and end apart: 2, of which 2 were waited for; matrix products, arithmetic and copies ran while one was open for 2% of the time, Pallas kernels for 0%

profile of v11, /device:TPU:8, one launch (start us, length us, event | category | flops | bytes accessed | tf_op | source)
XLA Modules:
  0.0 125.1 jit_solution(14300339030414843452)
XLA Ops:
  0.0 1.3 %fusion.25 = (bf16[1280,64]{1,0:T(8,128)(2,1)S(1)}, bf16[1280,64]{1,0:T(8,128)(2,1)S(1)}) fusion(bf16[1280,128]{1,0:T(8,128)(2,1)} %param.7), kind=kLoop, calls=%fused_computation.51 | loop fusion | bytes 655360 | tf_op jit(solution)/shard_map/slice | solution.py:34
  1.3 1.9 %collective-permute-start = (bf16[1280,64]{1,0:T(8,128)(2,1)S(1)}, bf16[1280,64]{1,0:T(8,128)(2,1)}, u32[]{:S(2)}, u32[]{:S(2)}) collective-permute-start(bf16[1280,64]{1,0:T(8,128)(2,1)S(1)} %get-tuple-element.63), channel_id=1, source_target_pairs={{0,1},{1,2},{2,3},{3,4},{4,5},{5,6},{6,7},{7,8},{8,9},{9,10},{10,1... | collective-permute-start | bytes 491528 | tf_op jit(solution)/shard_map/ppermute | solution.py:37
  3.2 4.5 %collective-permute-start.1 = (bf16[1280,64]{1,0:T(8,128)(2,1)S(1)}, bf16[1280,64]{1,0:T(8,128)(2,1)}, u32[]{:S(2)}, u32[]{:S(2)}) collective-permute-start(bf16[1280,64]{1,0:T(8,128)(2,1)S(1)} %get-tuple-element.64), channel_id=1, source_target_pairs={{1,0},{2,1},{3,2},{4,3},{5,4},{6,5},{7,6},{8,7},{9,8},{10,9},{11,1... | collective-permute-start | bytes 491528 | tf_op jit(solution)/shard_map/ppermute | solution.py:39
  8.1 0.8 tile.9
  9.0 0.1 slice.52
  9.2 0.4 tile.21
  9.7 0.1 reshape.107
  9.9 0.1 copy.36
  10.0 0.6 reshape.102.ids_ref
  10.6 0.4 collective-permute-done
  11.0 1.6 %collective-permute-done.1 = bf16[1280,64]{1,0:T(8,128)(2,1)} collective-permute-done((bf16[1280,64]{1,0:T(8,128)(2,1)S(1)}, bf16[1280,64]{1,0:T(8,128)(2,1)}, u32[]{:S(2)}, u32[]{:S(2)}) %collective-permute-start.1) | collective-permute-done | bytes 163872 | tf_op jit(solution)/shard_map/ppermute | solution.py:39
  12.6 1.5 %pad_maximum_fusion = bf16[1280,256]{1,0:T(8,128)(2,1)S(1)} fusion(bf16[1280,64]{1,0:T(8,128)(2,1)} %collective-permute-done.1, bf16[1280,128]{1,0:T(8,128)(2,1)S(1)} %copy-done, bf16[1280,64]{1,0:T(8,128)(2,1)} %collective-permute-done), kind=kLoop, calls=%fused_computation.13 | loop fusion | flops 1966080 | bytes 1310720 | tf_op jit(solution)/shard_map/concatenate | solution.py:35
  14.1 6.0 %while.10 = (s32[]{:T(128)}, bf16[10,128,2,128]{3,2,1,0:T(2,128)(2,1)S(1)}, bf16[10,128,256]{2,1,0:T(8,128)(2,1)S(1)}, bf16[256,768]{0,1:T(8,128)(2,1)S(1)}, bf16[2,192,128]{2,1,0:T(8,128)(2,1)S(1)}, /*index=5*/s32[]{:T(128)}) while((s32[]{:T(128)}, bf16[10,128,2,128]{3,2,1,0:T(2,128)(2,1)S(1)}, bf16[10,128,256]{2,1,0:T(8,128)(2,1)S(1)}, ...), condition=%wide.region_1.2_spmd, body=%wide.region_0.1_spmd.sunk | while | flops 63143936 | bytes 1540173 | solution.py:347
  14.1 0.3 fusion.39
  14.4 0.2 fusion.40
  14.7 0.2 fusion.39
  15.0 0.2 fusion.40
  15.3 0.3 fusion.39
  15.6 0.2 fusion.40
  15.9 0.2 fusion.39
  16.2 0.2 fusion.40
  16.5 0.3 fusion.39
  16.8 0.2 fusion.40
  17.1 0.2 fusion.39
  17.4 0.2 fusion.40
  17.7 0.2 fusion.39
  18.0 0.2 fusion.40
  18.3 0.3 fusion.39
  18.6 0.2 fusion.40
  18.9 0.2 fusion.39
  19.2 0.2 fusion.40
  19.5 0.3 fusion.39
  19.8 0.2 fusion.40
  20.1 0.9 copy.65
  21.1 4.7 %shard_map.55.x_ref = f32[16,96,256]{2,1,0:T(8,128)} custom-call(s32[3,1,1280]{2,1,0:T(1,128)} %reshape.102.ids_ref, bf16[1280,256]{1,0:T(8,128)(2,1)} %bitcast.67), custom_call_target="tpu_custom_call" | custom-call | flops 1006632960 | bytes 2243584 | tf_op jit(solution)/shard_map/pallas_call | solution.py:305
  25.7 43.6 %shard_map.56 = f32[3,96,256]{2,1,0:T(8,128)} custom-call(f32[16,96,256]{2,1,0:T(8,128)} %shard_map.55.x_ref), custom_call_target="tpu_custom_call" | custom-call | tf_op jit(solution)/shard_map/pallas_call | solution.py:151
  69.3 0.9 slice.46
  70.2 1.1 reshape.109
  71.4 0.2 fusion.26
  71.6 0.2 reduce_sum.18
  71.9 0.2 fusion.9
  72.2 0.2 multiply_reduce_fusion
  72.4 0.1 copy.42.spread_ref
  72.5 49.3 %shard_map.57 = f32[2,96,1536]{2,1,0:T(8,128)S(1)} custom-call(bf16[2,96,256]{2,1,0:T(8,128)(2,1)S(1)} %pad.14.own_ref, bf16[2,96,256]{2,1,0:T(8,128)(2,1)S(1)} %pad.15.mid_ref, f32[2,96,1]{2,1,0:T(8,128)S(1)} %copy.42.spread_ref, f32[96,1664]{1,0:T(8,128)S(1)} %pad_maximum_fusion.1.level_ref), custom_call_target="tpu_custom_call" | custom-call | flops 19931332608 | bytes 1376256 | tf_op jit(solution)/shard_map/pallas_call | solution.py:265
  121.9 0.5 reshape.110
  122.4 0.1 slice.57
  122.5 0.7 reshape.112
  123.2 1.9 %copy.45 = f32[1,2,94,1504]{3,1,2,0:T(2,128)} copy(f32[1,2,94,1504]{3,2,1,0:T(8,128)S(1)} %reshape.112) | data formatting | bytes 2262016 | tf_op jit(solution)/shard_map/broadcast_in_dim;reshape | solution.py:384
  (43 shorter events, 1.6 us)
Async XLA Ops:
  0.0 7.9 %copy-start.4 = (s32[3]{0:T(128)S(1)}, s32[3]{0:T(128)}, u32[]{:S(2)}) copy-start(s32[3]{0:T(128)} %constant.79.clone) | copy-start | bytes 40
  0.0 8.0 %copy-start.1 = (s32[3,1280]{1,0:T(4,128)S(1)}, s32[3,1280]{1,0:T(4,128)}, u32[]{:S(2)}) copy-start(s32[3,1280]{1,0:T(4,128)} %param.10) | copy-start | bytes 46084
  0.0 8.0 %copy-start.2 = (bf16[2,2,65]{2,1,0:T(2,128)(2,1)S(1)}, bf16[2,2,65]{2,1,0:T(2,128)(2,1)}, u32[]{:S(2)}) copy-start(bf16[2,2,65]{2,1,0:T(2,128)(2,1)} %param.8) | copy-start | bytes 1564
  1.3 9.7 %collective-permute-start = (bf16[1280,64]{1,0:T(8,128)(2,1)S(1)}, bf16[1280,64]{1,0:T(8,128)(2,1)}, u32[]{:S(2)}, u32[]{:S(2)}) collective-permute-start(bf16[1280,64]{1,0:T(8,128)(2,1)S(1)} %get-tuple-element.63), channel_id=1, source_target_pairs={{0,1},{1,2},{2,3},{3,4},{4,5},{5,6},{6,7},{7,8},{8,9},{9,10},{10,1... | collective-permute-start | bytes 491528 | tf_op jit(solution)/shard_map/ppermute | solution.py:37
  3.2 9.4 %collective-permute-start.1 = (bf16[1280,64]{1,0:T(8,128)(2,1)S(1)}, bf16[1280,64]{1,0:T(8,128)(2,1)}, u32[]{:S(2)}, u32[]{:S(2)}) collective-permute-start(bf16[1280,64]{1,0:T(8,128)(2,1)S(1)} %get-tuple-element.64), channel_id=1, source_target_pairs={{1,0},{2,1},{3,2},{4,3},{5,4},{6,5},{7,6},{8,7},{9,8},{10,9},{11,1... | collective-permute-start | bytes 491528 | tf_op jit(solution)/shard_map/ppermute | solution.py:39
  8.1 1.1 copy-start.3
  9.0 3.7 %copy-start = (bf16[1280,128]{1,0:T(8,128)(2,1)S(1)}, bf16[1280,128]{1,0:T(8,128)(2,1)}, u32[]{:S(2)}) copy-start(bf16[1280,128]{1,0:T(8,128)(2,1)} %param.7) | copy-start | bytes 983044

commit v12 on v11

--- a/solution.py
+++ b/solution.py
@@ -1,5 +1,4 @@
 from functools import partial
-import math
 
 import jax
 import jax.numpy as jnp
@@ -333,18 +332,13 @@
     second_rows = jax.vmap(partial(toeplitz_band, n_out=t_dev, n_in=n_mid))(smooth_taps)
     second_mat = second_rows.transpose(0, 2, 1)
     widened = extended_2(source, (("tm", 1),), 2 * HALF)
-    block_rows = math.gcd(vert_dev, 128)
-
-    def filter_block(block):
-        wave = jnp.dot(block, first_mat, preferred_element_type=jnp.float32).reshape(
-            block_rows, 2, BANDS, n_mid
-        )
-        power = (wave[:, 0] * wave[:, 0] + wave[:, 1] * wave[:, 1]).astype(jnp.bfloat16)
-        return jnp.einsum(
-            "vbu,but->vbt", power, second_mat, preferred_element_type=jnp.float32
-        ).astype(jnp.bfloat16)
-
-    envelope = lax.map(filter_block, widened.reshape(vert_dev // block_rows, block_rows, n_in))
+    wave = jnp.dot(widened, first_mat, preferred_element_type=jnp.float32).reshape(
+        vert_dev, 2, BANDS, n_mid
+    )
+    power = (wave[:, 0] * wave[:, 0] + wave[:, 1] * wave[:, 1]).astype(jnp.bfloat16)
+    envelope = jnp.einsum(
+        "vbu,but->vbt", power, second_mat, preferred_element_type=jnp.float32
+    ).astype(jnp.bfloat16)
     flat_env = envelope.reshape(vert_dev, BANDS * t_dev)
     offsets = jnp.array([0, P1, P1 + P2], dtype=jnp.int32)
     global_ids = parcel_ids + offsets[:, None]

time: 125 us -> 121 us (0.968); the launches traced: 125 us -> 120 us
  matrix products: 4.86 us -> 1.24 us
  Pallas kernels: 97.6 us -> 95.8 us
  local copies, waits for them, and re-layouts: 11.4 us -> 13.1 us
  other arithmetic: 2.16 us -> 0.7 us
    dot_general x20 -> x2, matrix products: 4.86 us -> 1.24 us  [the longest x1 0.8 us: local(): jnp.dot(widened, first_mat, preferred_element_type=jnp.float32)]
    pallas_call x1, Pallas kernels: 49.3 us -> 47.7 us  [gather_fold(): pl.pallas_call(partial(gather_fold_kernel, nx, nz, t_dev), out_shape=jax....]
    concatenate x1 -> x0, other arithmetic: 1.46 us -> none  [extended_2(): jnp.concatenate([lax.ppermute(tail, axis, [(i, (i + 1) % count) for i in...]
    another operation x2, local copies, waits for them, and re-layouts: 2.64 us -> 3.97 us  [local(): return coupling[None]]
where the time goes in v12:
time: 121 us; the launch traced here: 120 us
  Pallas kernels  95.8 us (79%)
  local copies, waits for them, and re-layouts  13.1 us (11%)
  starting transfers between devices  6.46 us (5%)
  waiting for transfers between devices  2.14 us (2%)
  matrix products  1.24 us (1%)
    pallas_call x1, Pallas kernels, gather_fold(): pl.pallas_call(partial(gather_fold_kernel, nx, nz, t_dev), out_shape=jax....  47.7 us
    pallas_call x1, Pallas kernels, reduce_to_owner(): pl.pallas_call(partial(reduce_kernel, nx, nz, n_tm), out_shape=jax.ShapeD...  43.5 us
    pallas_call x1, Pallas kernels, pool(): pl.pallas_call(partial(pool_kernel, par_dev, per_step), out_shape=jax.Sha...  4.69 us
    ppermute x1, starting transfers between devices, extended_2(): lax.ppermute(head, axis, [((i + 1) % count, i) for i in range(ends)])  4.54 us
    another operation x2, local copies, waits for them, and re-layouts, local(): return coupling[None]  3.97 us
  transfers between devices with their start and end apart: 2, of which 2 were waited for; matrix products, arithmetic and copies ran while one was open for 2% of the time, Pallas kernels for 0%

profile of v12, /device:TPU:8, one launch (start us, length us, event | category | flops | bytes accessed | tf_op | source)
XLA Modules:
  0.0 119.8 jit_solution(774328270065431397)
XLA Ops:
  0.0 0.0 copy-start.4
  0.0 0.0 copy-start.1
  0.0 0.0 copy-start.2
  0.0 1.3 %fusion.26 = (bf16[1280,64]{1,0:T(8,128)(2,1)S(1)}, bf16[1280,64]{1,0:T(8,128)(2,1)S(1)}) fusion(bf16[1280,128]{1,0:T(8,128)(2,1)} %param.5), kind=kLoop, calls=%fused_computation.50 | loop fusion | bytes 655360 | tf_op jit(solution)/shard_map/slice | solution.py:33
  1.3 1.9 %collective-permute-start = (bf16[1280,64]{1,0:T(8,128)(2,1)S(1)}, bf16[1280,64]{1,0:T(8,128)(2,1)S(1)}, u32[]{:S(2)}, u32[]{:S(2)}) collective-permute-start(bf16[1280,64]{1,0:T(8,128)(2,1)S(1)} %get-tuple-element.5), channel_id=1, source_target_pairs={{0,1},{1,2},{2,3},{3,4},{4,5},{5,6},{6,7},{7,8},{8,9},{9,10},{10,1... | collective-permute-start | bytes 491528 | tf_op jit(solution)/shard_map/ppermute | solution.py:36
  3.2 4.5 %collective-permute-start.1 = (bf16[1280,64]{1,0:T(8,128)(2,1)S(1)}, bf16[1280,64]{1,0:T(8,128)(2,1)S(1)}, u32[]{:S(2)}, u32[]{:S(2)}) collective-permute-start(bf16[1280,64]{1,0:T(8,128)(2,1)S(1)} %get-tuple-element.6), channel_id=1, source_target_pairs={{1,0},{2,1},{3,2},{4,3},{5,4},{6,5},{7,6},{8,7},{9,8},{10,9},{11,1... | collective-permute-start | bytes 491528 | tf_op jit(solution)/shard_map/ppermute | solution.py:38
  7.8 0.1 broadcast_in_dim.38
  7.9 0.0 copy-done.4
  8.0 0.0 copy-done.1
  8.0 0.1 broadcast_add_fusion
  8.0 0.0 copy-done.2
  8.0 0.0 copy-start.3
  8.1 0.1 tile.20
  8.1 0.0 copy-start
  8.1 0.8 tile.21
  9.0 0.1 slice.53
  9.2 0.0 copy-done.3
  9.2 0.4 tile.9
  9.6 0.1 slice.52
  9.7 0.1 reshape.100
  9.9 0.6 reshape.99.ids_ref
  10.5 0.4 collective-permute-done
  10.9 1.7 %collective-permute-done.1 = bf16[1280,64]{1,0:T(8,128)(2,1)S(1)} collective-permute-done((bf16[1280,64]{1,0:T(8,128)(2,1)S(1)}, bf16[1280,64]{1,0:T(8,128)(2,1)S(1)}, u32[]{:S(2)}, u32[]{:S(2)}) %collective-permute-start.1) | collective-permute-done | bytes 163872 | tf_op jit(solution)/shard_map/ppermute | solution.py:38
  12.6 0.0 copy-done
  12.6 0.8 fusion.4
  13.4 0.4 convolution_convert_fusion
  13.9 1.1 copy.46.env_ref
  14.9 4.7 %shard_map.55.x_ref = f32[16,96,256]{2,1,0:T(8,128)} custom-call(s32[3,1,1280]{2,1,0:T(1,128)} %reshape.99.ids_ref, bf16[1280,256]{1,0:T(8,128)(2,1)} %copy.46.env_ref), custom_call_target="tpu_custom_call" | custom-call | flops 1006632960 | bytes 2243584 | tf_op jit(solution)/shard_map/pallas_call | solution.py:304
  19.6 43.5 %shard_map.56 = f32[3,96,256]{2,1,0:T(8,128)} custom-call(f32[16,96,256]{2,1,0:T(8,128)} %shard_map.55.x_ref), custom_call_target="tpu_custom_call" | custom-call | tf_op jit(solution)/shard_map/pallas_call | solution.py:150
  63.1 0.9 slice.48
  64.0 1.1 reshape.105
  65.1 0.2 fusion.27
  65.3 0.1 squeeze.2
  65.4 0.2 reduce_sum.18
  65.6 0.1 copy.41
  65.7 0.2 fusion.9
  65.8 0.1 slice_bitcast_fusion
  65.9 0.2 multiply_reduce_fusion
  66.2 0.1 copy.42.spread_ref
  66.3 47.7 %shard_map.57 = f32[2,96,1536]{2,1,0:T(8,128)S(1)} custom-call(bf16[2,96,256]{2,1,0:T(8,128)(2,1)S(1)} %pad.14.own_ref, bf16[2,96,256]{2,1,0:T(8,128)(2,1)S(1)} %pad.15.mid_ref, f32[2,96,1]{2,1,0:T(8,128)S(1)} %copy.42.spread_ref, f32[96,1664]{1,0:T(8,128)S(1)} %pad_maximum_fusion.level_ref), custom_call_target="tpu_custom_call" | custom-call | flops 19931332608 | bytes 1376256 | tf_op jit(solution)/shard_map/pallas_call | solution.py:264
  114.0 0.5 reshape.106
  114.5 1.3 %slice.59 = f32[2,94,16,94]{3,2,1,0:T(8,128)} slice(f32[2,96,16,96]{3,2,1,0:T(8,128)S(1)} %reshape.106), slice={[0:2], [0:94], [0:16], [0:94]} | slice | bytes 2262016 | tf_op jit(solution)/shard_map/slice | solution.py:376
  115.8 2.1 %reshape.108 = f32[1,2,94,1504]{3,2,1,0:T(8,128)S(1)} reshape(f32[2,94,16,94]{3,2,1,0:T(8,128)} %slice.59) | data formatting | bytes 2262016 | tf_op jit(solution)/shard_map/broadcast_in_dim;reshape | solution.py:378
  117.9 1.9 %copy.47 = f32[1,2,94,1504]{3,1,2,0:T(2,128)} copy(f32[1,2,94,1504]{3,2,1,0:T(8,128)S(1)} %reshape.108) | data formatting | bytes 2262016 | tf_op jit(solution)/shard_map/broadcast_in_dim;reshape | solution.py:378
  (15 shorter events, 0.2 us)
Async XLA Ops:
  0.0 7.9 %copy-start.4 = (s32[3]{0:T(128)S(1)}, s32[3]{0:T(128)}, u32[]{:S(2)}) copy-start(s32[3]{0:T(128)} %constant.69.clone) | copy-start | bytes 40
  0.0 8.0 %copy-start.1 = (s32[3,1280]{1,0:T(4,128)S(1)}, s32[3,1280]{1,0:T(4,128)}, u32[]{:S(2)}) copy-start(s32[3,1280]{1,0:T(4,128)} %param.8) | copy-start | bytes 46084
  0.0 8.0 %copy-start.2 = (bf16[2,2,65]{2,1,0:T(2,128)(2,1)S(1)}, bf16[2,2,65]{2,1,0:T(2,128)(2,1)}, u32[]{:S(2)}) copy-start(bf16[2,2,65]{2,1,0:T(2,128)(2,1)} %param.6) | copy-start | bytes 1564
  1.3 9.6 %collective-permute-start = (bf16[1280,64]{1,0:T(8,128)(2,1)S(1)}, bf16[1280,64]{1,0:T(8,128)(2,1)S(1)}, u32[]{:S(2)}, u32[]{:S(2)}) collective-permute-start(bf16[1280,64]{1,0:T(8,128)(2,1)S(1)} %get-tuple-element.5), channel_id=1, source_target_pairs={{0,1},{1,2},{2,3},{3,4},{4,5},{5,6},{6,7},{7,8},{8,9},{9,10},{10,1... | collective-permute-start | bytes 491528 | tf_op jit(solution)/shard_map/ppermute | solution.py:36
  3.2 9.4 %collective-permute-start.1 = (bf16[1280,64]{1,0:T(8,128)(2,1)S(1)}, bf16[1280,64]{1,0:T(8,128)(2,1)S(1)}, u32[]{:S(2)}, u32[]{:S(2)}) collective-permute-start(bf16[1280,64]{1,0:T(8,128)(2,1)S(1)} %get-tuple-element.6), channel_id=1, source_target_pairs={{1,0},{2,1},{3,2},{4,3},{5,4},{6,5},{7,6},{8,7},{9,8},{10,9},{11,1... | collective-permute-start | bytes 491528 | tf_op jit(solution)/shard_map/ppermute | solution.py:38
  8.0 1.1 copy-start.3
  8.1 4.5 %copy-start = (bf16[1280,128]{1,0:T(8,128)(2,1)S(1)}, bf16[1280,128]{1,0:T(8,128)(2,1)}, u32[]{:S(2)}) copy-start(bf16[1280,128]{1,0:T(8,128)(2,1)} %param.5) | copy-start | bytes 983044

commit v13 on v12

--- a/solution.py
+++ b/solution.py
@@ -181,7 +181,8 @@
 
 
 def fold_group(g, group, lhs_ref, gath, out_ref, spread_ref, level_ref, t_dev):
-    rows = out_ref.shape[1]
+    rows = lhs_ref.shape[1] // LAG_PAD
+    kept = out_ref.shape[1]
     step = LAG_PAD // LAG_CHUNKS
     first = pl.multiple_of(g * group, 128)
     same = (level_ref[:, 0:1] == level_ref[:, pl.ds(pl.multiple_of(g * group + 128, 128), group)]).astype(jnp.float32)
@@ -198,7 +199,7 @@
             r = jnp.dot(lhs, rhs, preferred_element_type=jnp.float32)
             acc = acc + (r * r).reshape(step, rows, group).sum(axis=0)
         scale = spread_ref[band] * spread / t_dev
-        out_ref[band, :, pl.ds(first, group)] = acc * (scale * scale) * same / NLAG
+        out_ref[band, :, pl.ds(first, group)] = (acc * (scale * scale) * same / NLAG)[:kept]
         return carry
 
     lax.fori_loop(0, out_ref.shape[0], one_band, 0)
@@ -256,14 +257,14 @@
         copy.wait_send()
 
 
-def gather_fold(own, mid, spread, levels, nx, nz, t_dev):
+def gather_fold(own, mid, spread, levels, nx, nz, t_dev, kept):
     assert nx == 4
     bands, rows, width = own.shape
     cols = nx * nz * rows
     flops = 2 * bands * LAG_PAD * rows * width * cols
     return pl.pallas_call(
         partial(gather_fold_kernel, nx, nz, t_dev),
-        out_shape=jax.ShapeDtypeStruct((bands, rows, cols), jnp.float32),
+        out_shape=jax.ShapeDtypeStruct((bands, kept, cols), jnp.float32),
         in_specs=[pl.BlockSpec(memory_space=pltpu.VMEM)] * 4,
         out_specs=pl.BlockSpec(memory_space=pltpu.VMEM),
         scratch_shapes=[
@@ -372,8 +373,8 @@
         [jnp.broadcast_to(own_level[:, None], (ROW_PAD, 128)),
          jnp.broadcast_to(col_level[None, :], (ROW_PAD, owners * ROW_PAD))], axis=1
     )
-    padded = gather_fold(own, mid, spread, levels, nx, VERT_MINOR, t_dev)
-    coupling = padded.reshape(BANDS, ROW_PAD, owners, ROW_PAD)[:, :par_dev, :, :par_dev]
+    padded = gather_fold(own, mid, spread, levels, nx, VERT_MINOR, t_dev, par_dev)
+    coupling = padded.reshape(BANDS, par_dev, owners, ROW_PAD)[:, :, :, :par_dev]
     coupling = coupling.reshape(BANDS, par_dev, total_par)
     return coupling[None]
 

time: 121 us -> 119 us (0.983)
  local copies, waits for them, and re-layouts: 13.1 us -> 10.5 us
    another operation x2, local copies, waits for them, and re-layouts: 3.97 us -> 2.65 us  [local(): return coupling[None]]
    slice x1 -> x0, local copies, waits for them, and re-layouts: 1.29 us -> none  [local(): padded.reshape(BANDS, ROW_PAD, owners, ROW_PAD)[:, :par_dev, :, :par_dev]]
where the time goes in v13:
time: 119 us; the launch traced here: 117 us
  Pallas kernels  95.8 us (81%)
  local copies, waits for them, and re-layouts  10.5 us (9%)
  starting transfers between devices  6.46 us (5%)
  waiting for transfers between devices  2.14 us (2%)
  matrix products  1.24 us (1%)
    pallas_call x1, Pallas kernels, gather_fold(): pl.pallas_call(partial(gather_fold_kernel, nx, nz, t_dev), out_shape=jax....  47.7 us
    pallas_call x1, Pallas kernels, reduce_to_owner(): pl.pallas_call(partial(reduce_kernel, nx, nz, n_tm), out_shape=jax.ShapeD...  43.5 us
    pallas_call x1, Pallas kernels, pool(): pl.pallas_call(partial(pool_kernel, par_dev, per_step), out_shape=jax.Sha...  4.69 us
    ppermute x1, starting transfers between devices, extended_2(): lax.ppermute(head, axis, [((i + 1) % count, i) for i in range(ends)])  4.54 us
    another operation x2, local copies, waits for them, and re-layouts, local(): return coupling[None]  2.65 us
  transfers between devices with their start and end apart: 2, of which 2 were waited for; matrix products, arithmetic and copies ran while one was open for 2% of the time, Pallas kernels for 0%

profile of v13, /device:TPU:8, one launch (start us, length us, event | category | flops | bytes accessed | tf_op | source)
XLA Modules:
  0.0 117.2 jit_solution(203055385138655280)
XLA Ops:
  0.0 0.0 copy-start.4
  0.0 0.0 copy-start.1
  0.0 0.0 copy-start.2
  0.0 1.3 %fusion.26 = (bf16[1280,64]{1,0:T(8,128)(2,1)S(1)}, bf16[1280,64]{1,0:T(8,128)(2,1)S(1)}) fusion(bf16[1280,128]{1,0:T(8,128)(2,1)} %param.5), kind=kLoop, calls=%fused_computation.50 | loop fusion | bytes 655360 | tf_op jit(solution)/shard_map/slice | solution.py:33
  1.3 1.9 %collective-permute-start = (bf16[1280,64]{1,0:T(8,128)(2,1)S(1)}, bf16[1280,64]{1,0:T(8,128)(2,1)S(1)}, u32[]{:S(2)}, u32[]{:S(2)}) collective-permute-start(bf16[1280,64]{1,0:T(8,128)(2,1)S(1)} %get-tuple-element.5), channel_id=1, source_target_pairs={{0,1},{1,2},{2,3},{3,4},{4,5},{5,6},{6,7},{7,8},{8,9},{9,10},{10,1... | collective-permute-start | bytes 491528 | tf_op jit(solution)/shard_map/ppermute | solution.py:36
  3.2 4.5 %collective-permute-start.1 = (bf16[1280,64]{1,0:T(8,128)(2,1)S(1)}, bf16[1280,64]{1,0:T(8,128)(2,1)S(1)}, u32[]{:S(2)}, u32[]{:S(2)}) collective-permute-start(bf16[1280,64]{1,0:T(8,128)(2,1)S(1)} %get-tuple-element.6), channel_id=1, source_target_pairs={{1,0},{2,1},{3,2},{4,3},{5,4},{6,5},{7,6},{8,7},{9,8},{10,9},{11,1... | collective-permute-start | bytes 491528 | tf_op jit(solution)/shard_map/ppermute | solution.py:38
  7.8 0.1 broadcast_in_dim.38
  7.9 0.0 copy-done.4
  8.0 0.0 copy-done.1
  8.0 0.1 broadcast_add_fusion
  8.0 0.0 copy-done.2
  8.0 0.0 copy-start.3
  8.1 0.1 tile.20
  8.1 0.0 copy-start
  8.1 0.8 tile.21
  9.0 0.1 slice.53
  9.2 0.0 copy-done.3
  9.2 0.4 tile.9
  9.6 0.1 slice.52
  9.7 0.1 reshape.100
  9.9 0.6 reshape.99.ids_ref
  10.5 0.4 collective-permute-done
  10.9 1.7 %collective-permute-done.1 = bf16[1280,64]{1,0:T(8,128)(2,1)S(1)} collective-permute-done((bf16[1280,64]{1,0:T(8,128)(2,1)S(1)}, bf16[1280,64]{1,0:T(8,128)(2,1)S(1)}, u32[]{:S(2)}, u32[]{:S(2)}) %collective-permute-start.1) | collective-permute-done | bytes 163872 | tf_op jit(solution)/shard_map/ppermute | solution.py:38
  12.6 0.0 copy-done
  12.6 0.8 fusion.4
  13.4 0.4 convolution_convert_fusion
  13.9 1.1 copy.53.env_ref
  14.9 4.7 %shard_map.55.x_ref = f32[16,96,256]{2,1,0:T(8,128)} custom-call(s32[3,1,1280]{2,1,0:T(1,128)} %reshape.99.ids_ref, bf16[1280,256]{1,0:T(8,128)(2,1)} %copy.53.env_ref), custom_call_target="tpu_custom_call" | custom-call | flops 1006632960 | bytes 2243584 | tf_op jit(solution)/shard_map/pallas_call | solution.py:305
  19.6 43.5 %shard_map.56 = f32[3,96,256]{2,1,0:T(8,128)} custom-call(f32[16,96,256]{2,1,0:T(8,128)} %shard_map.55.x_ref), custom_call_target="tpu_custom_call" | custom-call | tf_op jit(solution)/shard_map/pallas_call | solution.py:150
  63.1 0.9 slice.48
  64.0 1.1 reshape.105
  65.1 0.2 fusion.27
  65.3 0.1 squeeze.2
  65.4 0.2 reduce_sum.18
  65.6 0.1 copy.48
  65.7 0.2 fusion.9
  65.8 0.1 slice_bitcast_fusion
  65.9 0.2 multiply_reduce_fusion
  66.2 0.1 copy.49.spread_ref
  66.3 47.7 %shard_map.57 = f32[2,94,1536]{2,1,0:T(8,128)S(1)} custom-call(bf16[2,96,256]{2,1,0:T(8,128)(2,1)S(1)} %pad.14.own_ref, bf16[2,96,256]{2,1,0:T(8,128)(2,1)S(1)} %pad.15.mid_ref, f32[2,96,1]{2,1,0:T(8,128)S(1)} %copy.49.spread_ref, f32[96,1664]{1,0:T(8,128)S(1)} %pad_maximum_fusion.level_ref), custom_call_target="tpu_custom_call" | custom-call | flops 19931332608 | bytes 1376256 | tf_op jit(solution)/shard_map/pallas_call | solution.py:265
  114.0 0.5 reshape.106
  114.5 0.7 broadcast_in_dim_reshape.3
  115.2 1.9 %copy.50 = f32[1,2,94,1504]{3,1,2,0:T(2,128)} copy(f32[1,2,94,1504]{3,2,1,0:T(8,128)S(1)} %broadcast_in_dim_reshape.3) | data formatting | bytes 2262016 | tf_op jit(solution)/shard_map/broadcast_in_dim;reshape | solution.py:379
  (15 shorter events, 0.2 us)
Async XLA Ops:
  0.0 7.9 %copy-start.4 = (s32[3]{0:T(128)S(1)}, s32[3]{0:T(128)}, u32[]{:S(2)}) copy-start(s32[3]{0:T(128)} %constant.69.clone) | copy-start | bytes 40
  0.0 8.0 %copy-start.1 = (s32[3,1280]{1,0:T(4,128)S(1)}, s32[3,1280]{1,0:T(4,128)}, u32[]{:S(2)}) copy-start(s32[3,1280]{1,0:T(4,128)} %param.8) | copy-start | bytes 46084
  0.0 8.0 %copy-start.2 = (bf16[2,2,65]{2,1,0:T(2,128)(2,1)S(1)}, bf16[2,2,65]{2,1,0:T(2,128)(2,1)}, u32[]{:S(2)}) copy-start(bf16[2,2,65]{2,1,0:T(2,128)(2,1)} %param.6) | copy-start | bytes 1564
  1.3 9.6 %collective-permute-start = (bf16[1280,64]{1,0:T(8,128)(2,1)S(1)}, bf16[1280,64]{1,0:T(8,128)(2,1)S(1)}, u32[]{:S(2)}, u32[]{:S(2)}) collective-permute-start(bf16[1280,64]{1,0:T(8,128)(2,1)S(1)} %get-tuple-element.5), channel_id=1, source_target_pairs={{0,1},{1,2},{2,3},{3,4},{4,5},{5,6},{6,7},{7,8},{8,9},{9,10},{10,1... | collective-permute-start | bytes 491528 | tf_op jit(solution)/shard_map/ppermute | solution.py:36
  3.2 9.4 %collective-permute-start.1 = (bf16[1280,64]{1,0:T(8,128)(2,1)S(1)}, bf16[1280,64]{1,0:T(8,128)(2,1)S(1)}, u32[]{:S(2)}, u32[]{:S(2)}) collective-permute-start(bf16[1280,64]{1,0:T(8,128)(2,1)S(1)} %get-tuple-element.6), channel_id=1, source_target_pairs={{1,0},{2,1},{3,2},{4,3},{5,4},{6,5},{7,6},{8,7},{9,8},{10,9},{11,1... | collective-permute-start | bytes 491528 | tf_op jit(solution)/shard_map/ppermute | solution.py:38
  8.0 1.1 copy-start.3
  8.1 4.5 %copy-start = (bf16[1280,128]{1,0:T(8,128)(2,1)S(1)}, bf16[1280,128]{1,0:T(8,128)(2,1)}, u32[]{:S(2)}) copy-start(bf16[1280,128]{1,0:T(8,128)(2,1)} %param.5) | copy-start | bytes 983044

commit v14 on v13

--- a/solution.py
+++ b/solution.py
@@ -214,20 +214,31 @@
     mine = gath.at[:, pl.ds(me * rows, rows), :]
     own = pltpu.make_async_copy(own_ref, mine, local_sem)
     own.start()
-    copies = []
-    for k in range(1, nz):
-        copy = pltpu.make_async_remote_copy(
-            src_ref=own_ref, dst_ref=mine,
-            send_sem=a_send.at[k - 1], recv_sem=a_recv.at[k - 1],
-            device_id=(mx * nz + lax.rem(mz + k, nz), tm), device_id_type=pl.DeviceIdType.MESH,
+    below, above = lax.rem(mz + nz - 1, nz), lax.rem(mz + 1, nz)
+
+    def z_copy(src, dst, peer, slot):
+        return pltpu.make_async_remote_copy(
+            src_ref=src, dst_ref=dst, send_sem=a_send.at[slot], recv_sem=a_recv.at[slot],
+            device_id=(mx * nz + peer, tm), device_id_type=pl.DeviceIdType.MESH,
         )
-        copy.start()
-        copies.append(copy)
+
+    near = [z_copy(own_ref, mine, above, 0), z_copy(own_ref, mine, below, 1)]
+    for copy in near:
+        copy.start()
     for band in range(mid_ref.shape[0]):
         fill_lags(mid_ref, lhs_ref, band)
     own.wait()
-    for copy in copies:
-        copy.wait()
+    for copy in near:
+        copy.wait_recv()
+    from_below = gath.at[pl.ds(0, 1), pl.ds((mx * nz + below) * rows, rows), :]
+    from_above = gath.at[pl.ds(1, 1), pl.ds((mx * nz + above) * rows, rows), :]
+    far = [z_copy(from_below, from_below, above, 2), z_copy(from_above, from_above, below, 3)]
+    for copy in far:
+        copy.start()
+    for copy in far:
+        copy.wait_recv()
+    for copy in near + far:
+        copy.wait_send()
     left, right = lax.rem(mx + nx - 1, nx), lax.rem(mx + 1, nx)
     half = group // 2
 
@@ -258,7 +269,7 @@
 
 
 def gather_fold(own, mid, spread, levels, nx, nz, t_dev, kept):
-    assert nx == 4
+    assert nx == 4 and nz == 4 and own.shape[0] == 2
     bands, rows, width = own.shape
     cols = nx * nz * rows
     flops = 2 * bands * LAG_PAD * rows * width * cols
@@ -270,8 +281,8 @@
         scratch_shapes=[
             pltpu.VMEM((bands, cols, width), own.dtype),
             pltpu.VMEM((bands, LAG_PAD * rows, width), jnp.bfloat16),
-            pltpu.SemaphoreType.DMA((nz - 1,)),
-            pltpu.SemaphoreType.DMA((nz - 1,)),
+            pltpu.SemaphoreType.DMA((4,)),
+            pltpu.SemaphoreType.DMA((4,)),
             pltpu.SemaphoreType.DMA((4,)),
             pltpu.SemaphoreType.DMA((4,)),
             pltpu.SemaphoreType.DMA(()),

time: 119 us -> 119 us (level); the launches traced: 117 us -> 119 us
  Pallas kernels: 95.8 us -> 97.2 us
    pallas_call x1, Pallas kernels: 47.7 us -> 49.1 us  [gather_fold(): pl.pallas_call(partial(gather_fold_kernel, nx, nz, t_dev), out_shape=jax....]
where the time goes in v14:
time: 119 us
  Pallas kernels  97.2 us (82%)
  local copies, waits for them, and re-layouts  10.5 us (9%)
  starting transfers between devices  6.46 us (5%)
  waiting for transfers between devices  2.14 us (2%)
  matrix products  1.24 us (1%)
    pallas_call x1, Pallas kernels, gather_fold(): pl.pallas_call(partial(gather_fold_kernel, nx, nz, t_dev), out_shape=jax....  49.1 us
    pallas_call x1, Pallas kernels, reduce_to_owner(): pl.pallas_call(partial(reduce_kernel, nx, nz, n_tm), out_shape=jax.ShapeD...  43.5 us
    pallas_call x1, Pallas kernels, pool(): pl.pallas_call(partial(pool_kernel, par_dev, per_step), out_shape=jax.Sha...  4.69 us
    ppermute x1, starting transfers between devices, extended_2(): lax.ppermute(head, axis, [((i + 1) % count, i) for i in range(ends)])  4.54 us
    another operation x2, local copies, waits for them, and re-layouts, local(): return coupling[None]  2.65 us
  transfers between devices with their start and end apart: 2, of which 2 were waited for; matrix products, arithmetic and copies ran while one was open for 2% of the time, Pallas kernels for 0%

profile of v14, /device:TPU:8, one launch (start us, length us, event | category | flops | bytes accessed | tf_op | source)
XLA Modules:
  0.0 118.6 jit_solution(14677900924187455279)
XLA Ops:
  0.0 0.0 copy-start.4
  0.0 0.0 copy-start.1
  0.0 0.0 copy-start.2
  0.0 1.3 %fusion.26 = (bf16[1280,64]{1,0:T(8,128)(2,1)S(1)}, bf16[1280,64]{1,0:T(8,128)(2,1)S(1)}) fusion(bf16[1280,128]{1,0:T(8,128)(2,1)} %param.5), kind=kLoop, calls=%fused_computation.50 | loop fusion | bytes 655360 | tf_op jit(solution)/shard_map/slice | solution.py:33
  1.3 1.9 %collective-permute-start = (bf16[1280,64]{1,0:T(8,128)(2,1)S(1)}, bf16[1280,64]{1,0:T(8,128)(2,1)S(1)}, u32[]{:S(2)}, u32[]{:S(2)}) collective-permute-start(bf16[1280,64]{1,0:T(8,128)(2,1)S(1)} %get-tuple-element.5), channel_id=1, source_target_pairs={{0,1},{1,2},{2,3},{3,4},{4,5},{5,6},{6,7},{7,8},{8,9},{9,10},{10,1... | collective-permute-start | bytes 491528 | tf_op jit(solution)/shard_map/ppermute | solution.py:36
  3.2 4.5 %collective-permute-start.1 = (bf16[1280,64]{1,0:T(8,128)(2,1)S(1)}, bf16[1280,64]{1,0:T(8,128)(2,1)S(1)}, u32[]{:S(2)}, u32[]{:S(2)}) collective-permute-start(bf16[1280,64]{1,0:T(8,128)(2,1)S(1)} %get-tuple-element.6), channel_id=1, source_target_pairs={{1,0},{2,1},{3,2},{4,3},{5,4},{6,5},{7,6},{8,7},{9,8},{10,9},{11,1... | collective-permute-start | bytes 491528 | tf_op jit(solution)/shard_map/ppermute | solution.py:38
  7.8 0.1 broadcast_in_dim.38
  7.9 0.0 copy-done.4
  8.0 0.0 copy-done.1
  8.0 0.1 broadcast_add_fusion
  8.0 0.0 copy-done.2
  8.0 0.0 copy-start.3
  8.1 0.1 tile.20
  8.1 0.0 copy-start
  8.1 0.8 tile.21
  9.0 0.1 slice.53
  9.2 0.0 copy-done.3
  9.2 0.4 tile.9
  9.6 0.1 slice.52
  9.7 0.1 reshape.100
  9.9 0.6 reshape.99.ids_ref
  10.5 0.4 collective-permute-done
  10.9 1.7 %collective-permute-done.1 = bf16[1280,64]{1,0:T(8,128)(2,1)S(1)} collective-permute-done((bf16[1280,64]{1,0:T(8,128)(2,1)S(1)}, bf16[1280,64]{1,0:T(8,128)(2,1)S(1)}, u32[]{:S(2)}, u32[]{:S(2)}) %collective-permute-start.1) | collective-permute-done | bytes 163872 | tf_op jit(solution)/shard_map/ppermute | solution.py:38
  12.6 0.0 copy-done
  12.6 0.8 fusion.4
  13.4 0.4 convolution_convert_fusion
  13.9 1.1 copy.53.env_ref
  14.9 4.7 %shard_map.55.x_ref = f32[16,96,256]{2,1,0:T(8,128)} custom-call(s32[3,1,1280]{2,1,0:T(1,128)} %reshape.99.ids_ref, bf16[1280,256]{1,0:T(8,128)(2,1)} %copy.53.env_ref), custom_call_target="tpu_custom_call" | custom-call | flops 1006632960 | bytes 2243584 | tf_op jit(solution)/shard_map/pallas_call | solution.py:316
  19.6 43.5 %shard_map.56 = f32[3,96,256]{2,1,0:T(8,128)} custom-call(f32[16,96,256]{2,1,0:T(8,128)} %shard_map.55.x_ref), custom_call_target="tpu_custom_call" | custom-call | tf_op jit(solution)/shard_map/pallas_call | solution.py:150
  63.1 0.9 slice.48
  64.0 1.1 reshape.105
  65.1 0.2 fusion.27
  65.3 0.1 squeeze.2
  65.4 0.2 reduce_sum.18
  65.6 0.1 copy.48
  65.7 0.2 fusion.9
  65.8 0.1 slice_bitcast_fusion
  65.9 0.2 multiply_reduce_fusion
  66.2 0.1 copy.49.spread_ref
  66.3 49.1 %shard_map.57 = f32[2,94,1536]{2,1,0:T(8,128)S(1)} custom-call(bf16[2,96,256]{2,1,0:T(8,128)(2,1)S(1)} %pad.14.own_ref, bf16[2,96,256]{2,1,0:T(8,128)(2,1)S(1)} %pad.15.mid_ref, f32[2,96,1]{2,1,0:T(8,128)S(1)} %copy.49.spread_ref, f32[96,1664]{1,0:T(8,128)S(1)} %pad_maximum_fusion.level_ref), custom_call_target="tpu_custom_call" | custom-call | flops 19931332608 | bytes 1376256 | tf_op jit(solution)/shard_map/pallas_call | solution.py:276
  115.4 0.5 reshape.106
  115.9 0.7 broadcast_in_dim_reshape.3
  116.7 1.9 %copy.50 = f32[1,2,94,1504]{3,1,2,0:T(2,128)} copy(f32[1,2,94,1504]{3,2,1,0:T(8,128)S(1)} %broadcast_in_dim_reshape.3) | data formatting | bytes 2262016 | tf_op jit(solution)/shard_map/broadcast_in_dim;reshape | solution.py:390
  (15 shorter events, 0.2 us)
Async XLA Ops:
  0.0 7.9 %copy-start.4 = (s32[3]{0:T(128)S(1)}, s32[3]{0:T(128)}, u32[]{:S(2)}) copy-start(s32[3]{0:T(128)} %constant.69.clone) | copy-start | bytes 40
  0.0 8.0 %copy-start.1 = (s32[3,1280]{1,0:T(4,128)S(1)}, s32[3,1280]{1,0:T(4,128)}, u32[]{:S(2)}) copy-start(s32[3,1280]{1,0:T(4,128)} %param.8) | copy-start | bytes 46084
  0.0 8.0 %copy-start.2 = (bf16[2,2,65]{2,1,0:T(2,128)(2,1)S(1)}, bf16[2,2,65]{2,1,0:T(2,128)(2,1)}, u32[]{:S(2)}) copy-start(bf16[2,2,65]{2,1,0:T(2,128)(2,1)} %param.6) | copy-start | bytes 1564
  1.3 9.6 %collective-permute-start = (bf16[1280,64]{1,0:T(8,128)(2,1)S(1)}, bf16[1280,64]{1,0:T(8,128)(2,1)S(1)}, u32[]{:S(2)}, u32[]{:S(2)}) collective-permute-start(bf16[1280,64]{1,0:T(8,128)(2,1)S(1)} %get-tuple-element.5), channel_id=1, source_target_pairs={{0,1},{1,2},{2,3},{3,4},{4,5},{5,6},{6,7},{7,8},{8,9},{9,10},{10,1... | collective-permute-start | bytes 491528 | tf_op jit(solution)/shard_map/ppermute | solution.py:36
  3.2 9.4 %collective-permute-start.1 = (bf16[1280,64]{1,0:T(8,128)(2,1)S(1)}, bf16[1280,64]{1,0:T(8,128)(2,1)S(1)}, u32[]{:S(2)}, u32[]{:S(2)}) collective-permute-start(bf16[1280,64]{1,0:T(8,128)(2,1)S(1)} %get-tuple-element.6), channel_id=1, source_target_pairs={{1,0},{2,1},{3,2},{4,3},{5,4},{6,5},{7,6},{8,7},{9,8},{10,9},{11,1... | collective-permute-start | bytes 491528 | tf_op jit(solution)/shard_map/ppermute | solution.py:38
  8.0 1.1 copy-start.3
  8.1 4.5 %copy-start = (bf16[1280,128]{1,0:T(8,128)(2,1)S(1)}, bf16[1280,128]{1,0:T(8,128)(2,1)}, u32[]{:S(2)}) copy-start(bf16[1280,128]{1,0:T(8,128)(2,1)} %param.5) | copy-start | bytes 983044

commit v15 on v13

--- a/solution.py
+++ b/solution.py
@@ -82,11 +82,29 @@
     pl.semaphore_wait(barrier, len(peers))
 
 
-def reduce_kernel(nx, nz, n_tm, x_ref, out_ref, recv_a, send_a, part, recv_b, mine, halo, a_send, a_recv,
-                  b_send, b_recv, t_send, t_recv):
+def reduce_kernel(nx, nz, n_tm, par_dev, ids_ref, env_ref, out_ref, x_ref, recv_a, send_a, part, recv_b, mine,
+                  halo, a_send, a_recv, b_send, b_recv, t_send, t_recv):
     me, tm, mx, mz = mesh_peers(nx, nz)
     greet(mx, mz, tm, nx, nz, n_tm)
     hz = nz // 2
+    rows = x_ref.shape[1]
+    r = lax.broadcasted_iota(jnp.int32, (rows, 1), 0)
+
+    def pool_groups(first_offset, carry):
+        def one(j, c):
+            owner = lax.rem(mx + first_offset + 2 * (j // nz), nx) * nz + j % nz
+            wanted = jnp.where(r < par_dev, owner * par_dev + r, -1)
+            hits = (ids_ref[0] == wanted).astype(jnp.float32)
+            for level in range(1, ids_ref.shape[0]):
+                hits = hits + (ids_ref[level] == wanted).astype(jnp.float32)
+            x_ref[owner] = jnp.dot(
+                hits.astype(jnp.bfloat16), env_ref[...], preferred_element_type=jnp.float32
+            )
+            return c
+
+        return lax.fori_loop(0, 2 * nz, one, carry)
+
+    pool_groups(nx - 1, 0)
     peers = (lax.rem(mx + 1, nx), lax.rem(mx + nx - 1, nx))
 
     def owners_of(g, d):
@@ -108,6 +126,8 @@
             )
             copy.start()
             copies.append(copy)
+        if s == 1:
+            pool_groups(2, 0)
         for copy in copies:
             copy.wait()
     for d in range(2):
@@ -144,21 +164,25 @@
     out_ref[2] = halo[1]
 
 
-def reduce_to_owner(x, nx, nz, n_tm):
-    n, rows, w = x.shape
+def reduce_to_owner(global_ids, flat_env, nx, nz, n_tm, par_dev):
+    levels, vertices = global_ids.shape
+    w = flat_env.shape[1]
+    rows = ROW_PAD
     hz = nz // 2
+    dtype = jnp.float32
     return pl.pallas_call(
-        partial(reduce_kernel, nx, nz, n_tm),
-        out_shape=jax.ShapeDtypeStruct((3, rows, w), x.dtype),
-        in_specs=[pl.BlockSpec(memory_space=pltpu.VMEM)],
+        partial(reduce_kernel, nx, nz, n_tm, par_dev),
+        out_shape=jax.ShapeDtypeStruct((3, rows, w), dtype),
+        in_specs=[pl.BlockSpec(memory_space=pltpu.VMEM)] * 2,
         out_specs=pl.BlockSpec(memory_space=pltpu.VMEM),
         scratch_shapes=[
-            pltpu.VMEM((2, nx - 1, hz, rows, w), x.dtype),
-            pltpu.VMEM((2, nx - 2, hz, rows, w), x.dtype),
-            pltpu.VMEM((nz, rows, w), x.dtype),
-            pltpu.VMEM((nz - 1, rows, w), x.dtype),
-            pltpu.VMEM((rows, w), x.dtype),
-            pltpu.VMEM((2, rows, w), x.dtype),
+            pltpu.VMEM((nx * nz, rows, w), dtype),
+            pltpu.VMEM((2, nx - 1, hz, rows, w), dtype),
+            pltpu.VMEM((2, nx - 2, hz, rows, w), dtype),
+            pltpu.VMEM((nz, rows, w), dtype),
+            pltpu.VMEM((nz - 1, rows, w), dtype),
+            pltpu.VMEM((rows, w), dtype),
+            pltpu.VMEM((2, rows, w), dtype),
             pltpu.SemaphoreType.DMA((2, nx - 1)),
             pltpu.SemaphoreType.DMA((2, nx - 1)),
             pltpu.SemaphoreType.DMA((nz - 1,)),
@@ -167,7 +191,7 @@
             pltpu.SemaphoreType.DMA((2,)),
         ],
         compiler_params=pltpu.CompilerParams(collective_id=0, has_side_effects=True),
-    )(x)
+    )(global_ids.reshape(levels, 1, vertices), flat_env)
 
 
 def fill_lags(mid_ref, lhs_ref, band):
@@ -286,39 +310,6 @@
     )(own, mid, spread, levels)
 
 
-def pool_kernel(par_dev, per_step, ids_ref, env_ref, out_ref):
-    rows = out_ref.shape[1]
-    r = lax.broadcasted_iota(jnp.int32, (rows, 1), 0)
-    env = env_ref[...]
-    for o in range(per_step):
-        wanted = jnp.where(r < par_dev, (pl.program_id(0) * per_step + o) * par_dev + r, -1)
-        hits = (ids_ref[0] == wanted).astype(jnp.float32)
-        for level in range(1, ids_ref.shape[0]):
-            hits = hits + (ids_ref[level] == wanted).astype(jnp.float32)
-        out_ref[o] = jnp.dot(hits.astype(jnp.bfloat16), env, preferred_element_type=jnp.float32)
-
-
-def pool(global_ids, flat_env, owners, par_dev):
-    levels, vertices = global_ids.shape
-    width = flat_env.shape[1]
-    per_step = 4
-    return pl.pallas_call(
-        partial(pool_kernel, par_dev, per_step),
-        out_shape=jax.ShapeDtypeStruct((owners, ROW_PAD, width), jnp.float32),
-        grid=(owners // per_step,),
-        in_specs=[
-            pl.BlockSpec((levels, 1, vertices), lambda k: (0, 0, 0)),
-            pl.BlockSpec((vertices, width), lambda k: (0, 0)),
-        ],
-        out_specs=pl.BlockSpec((per_step, ROW_PAD, width), lambda k: (k, 0, 0)),
-        cost_estimate=pl.CostEstimate(
-            flops=2 * owners * ROW_PAD * vertices * width,
-            bytes_accessed=4 * levels * vertices + 2 * vertices * width + 4 * owners * ROW_PAD * width,
-            transcendentals=0,
-        ),
-    )(global_ids.reshape(levels, 1, vertices), flat_env)
-
-
 def local(source, band_taps, smooth_taps, parcel_ids):
     vert_dev, t_dev = source.shape
     owners = lax.axis_size("vert")
@@ -345,11 +336,10 @@
     global_ids = parcel_ids + offsets[:, None]
     owner_start = lax.axis_index("vert") * par_dev
 
-    pooled = pool(global_ids, flat_env, owners, par_dev)
     nx = owners // VERT_MINOR
     n_tm = lax.axis_size("tm")
     tm = lax.axis_index("tm")
-    sums3 = reduce_to_owner(pooled, nx, VERT_MINOR, n_tm)[:, :par_dev].reshape(3, par_dev, BANDS, t_dev)
+    sums3 = reduce_to_owner(global_ids, flat_env, nx, VERT_MINOR, n_tm, par_dev)[:, :par_dev].reshape(3, par_dev, BANDS, t_dev)
     before = jnp.where(tm > 0, sums3[0, :, :, t_dev - LAG :], 0.0)
     after = jnp.where(tm < n_tm - 1, sums3[2, :, :, :LAG], 0.0)
     own_ext = jnp.concatenate([before, sums3[1], after], axis=2)

time: 119 us -> 116 us (0.975)
  Pallas kernels: 95.8 us -> 93 us
    pallas_call x2 -> x1, Pallas kernels: 48.2 us -> 45.4 us  [reduce_to_owner(): pl.pallas_call(partial(reduce_kernel, nx, nz, n_tm, par_dev), out_shape=j...]
where the time goes in v15:
time: 116 us; the launch traced here: 114 us
  Pallas kernels  93 us (80%)
  local copies, waits for them, and re-layouts  10.5 us (9%)
  starting transfers between devices  6.46 us (6%)
  waiting for transfers between devices  2.14 us (2%)
  matrix products  1.24 us (1%)
    pallas_call x1, Pallas kernels, gather_fold(): pl.pallas_call(partial(gather_fold_kernel, nx, nz, t_dev), out_shape=jax....  47.6 us
    pallas_call x1, Pallas kernels, reduce_to_owner(): pl.pallas_call(partial(reduce_kernel, nx, nz, n_tm, par_dev), out_shape=j...  45.4 us
    ppermute x1, starting transfers between devices, extended_2(): lax.ppermute(head, axis, [((i + 1) % count, i) for i in range(ends)])  4.54 us
    another operation x2, local copies, waits for them, and re-layouts, local(): return coupling[None]  2.65 us
  transfers between devices with their start and end apart: 2, of which 2 were waited for; matrix products, arithmetic and copies ran while one was open for 2% of the time, Pallas kernels for 0%

profile of v15, /device:TPU:8, one launch (start us, length us, event | category | flops | bytes accessed | tf_op | source)
XLA Modules:
  0.0 114.4 jit_solution(14943236394593509624)
XLA Ops:
  0.0 0.0 copy-start.4
  0.0 0.0 copy-start.1
  0.0 0.0 copy-start.2
  0.0 1.3 %fusion.26 = (bf16[1280,64]{1,0:T(8,128)(2,1)S(1)}, bf16[1280,64]{1,0:T(8,128)(2,1)S(1)}) fusion(bf16[1280,128]{1,0:T(8,128)(2,1)} %param.5), kind=kLoop, calls=%fused_computation.50 | loop fusion | bytes 655360 | tf_op jit(solution)/shard_map/slice | solution.py:33
  1.3 1.9 %collective-permute-start = (bf16[1280,64]{1,0:T(8,128)(2,1)S(1)}, bf16[1280,64]{1,0:T(8,128)(2,1)S(1)}, u32[]{:S(2)}, u32[]{:S(2)}) collective-permute-start(bf16[1280,64]{1,0:T(8,128)(2,1)S(1)} %get-tuple-element.5), channel_id=1, source_target_pairs={{0,1},{1,2},{2,3},{3,4},{4,5},{5,6},{6,7},{7,8},{8,9},{9,10},{10,1... | collective-permute-start | bytes 491528 | tf_op jit(solution)/shard_map/ppermute | solution.py:36
  3.2 4.5 %collective-permute-start.1 = (bf16[1280,64]{1,0:T(8,128)(2,1)S(1)}, bf16[1280,64]{1,0:T(8,128)(2,1)S(1)}, u32[]{:S(2)}, u32[]{:S(2)}) collective-permute-start(bf16[1280,64]{1,0:T(8,128)(2,1)S(1)} %get-tuple-element.6), channel_id=1, source_target_pairs={{1,0},{2,1},{3,2},{4,3},{5,4},{6,5},{7,6},{8,7},{9,8},{10,9},{11,1... | collective-permute-start | bytes 491528 | tf_op jit(solution)/shard_map/ppermute | solution.py:38
  7.8 0.1 broadcast_in_dim.38
  7.9 0.0 copy-done.4
  8.0 0.0 copy-done.1
  8.0 0.1 broadcast_add_fusion
  8.0 0.0 copy-done.2
  8.0 0.0 copy-start.3
  8.1 0.1 tile.20
  8.1 0.0 copy-start
  8.1 0.8 tile.21
  9.0 0.1 slice.53
  9.2 0.0 copy-done.3
  9.2 0.4 tile.9
  9.6 0.1 slice.52
  9.7 0.1 reshape.100
  9.9 0.6 reshape.99.ids_ref
  10.5 0.4 collective-permute-done
  10.9 1.7 %collective-permute-done.1 = bf16[1280,64]{1,0:T(8,128)(2,1)S(1)} collective-permute-done((bf16[1280,64]{1,0:T(8,128)(2,1)S(1)}, bf16[1280,64]{1,0:T(8,128)(2,1)S(1)}, u32[]{:S(2)}, u32[]{:S(2)}) %collective-permute-start.1) | collective-permute-done | bytes 163872 | tf_op jit(solution)/shard_map/ppermute | solution.py:38
  12.6 0.0 copy-done
  12.6 0.8 fusion.4
  13.4 0.4 convolution_convert_fusion
  13.9 1.1 copy.53.env_ref
  14.9 45.4 %shard_map.55 = f32[3,96,256]{2,1,0:T(8,128)} custom-call(s32[3,1,1280]{2,1,0:T(1,128)} %reshape.99.ids_ref, bf16[1280,256]{1,0:T(8,128)(2,1)} %copy.53.env_ref), custom_call_target="tpu_custom_call" | custom-call | tf_op jit(solution)/shard_map/pallas_call | solution.py:173
  60.4 0.9 slice.48
  61.3 1.1 reshape.105
  62.4 0.2 fusion.27
  62.6 0.1 squeeze.2
  62.6 0.2 reduce_sum.18
  62.8 0.1 copy.48
  62.9 0.2 fusion.9
  63.1 0.1 slice_bitcast_fusion
  63.2 0.2 multiply_reduce_fusion
  63.4 0.1 copy.49.spread_ref
  63.6 47.6 %shard_map.56 = f32[2,94,1536]{2,1,0:T(8,128)S(1)} custom-call(bf16[2,96,256]{2,1,0:T(8,128)(2,1)S(1)} %pad.14.own_ref, bf16[2,96,256]{2,1,0:T(8,128)(2,1)S(1)} %pad.15.mid_ref, f32[2,96,1]{2,1,0:T(8,128)S(1)} %copy.49.spread_ref, f32[96,1664]{1,0:T(8,128)S(1)} %pad_maximum_fusion.level_ref), custom_call_target="tpu_custom_call" | custom-call | flops 19931332608 | bytes 1376256 | tf_op jit(solution)/shard_map/pallas_call | solution.py:289
  111.2 0.5 reshape.106
  111.7 0.7 broadcast_in_dim_reshape.3
  112.5 1.9 %copy.50 = f32[1,2,94,1504]{3,1,2,0:T(2,128)} copy(f32[1,2,94,1504]{3,2,1,0:T(8,128)S(1)} %broadcast_in_dim_reshape.3) | data formatting | bytes 2262016 | tf_op jit(solution)/shard_map/broadcast_in_dim;reshape | solution.py:369
  (15 shorter events, 0.2 us)
Async XLA Ops:
  0.0 7.9 %copy-start.4 = (s32[3]{0:T(128)S(1)}, s32[3]{0:T(128)}, u32[]{:S(2)}) copy-start(s32[3]{0:T(128)} %constant.69.clone) | copy-start | bytes 40
  0.0 8.0 %copy-start.1 = (s32[3,1280]{1,0:T(4,128)S(1)}, s32[3,1280]{1,0:T(4,128)}, u32[]{:S(2)}) copy-start(s32[3,1280]{1,0:T(4,128)} %param.8) | copy-start | bytes 46084
  0.0 8.0 %copy-start.2 = (bf16[2,2,65]{2,1,0:T(2,128)(2,1)S(1)}, bf16[2,2,65]{2,1,0:T(2,128)(2,1)}, u32[]{:S(2)}) copy-start(bf16[2,2,65]{2,1,0:T(2,128)(2,1)} %param.6) | copy-start | bytes 1564
  1.3 9.6 %collective-permute-start = (bf16[1280,64]{1,0:T(8,128)(2,1)S(1)}, bf16[1280,64]{1,0:T(8,128)(2,1)S(1)}, u32[]{:S(2)}, u32[]{:S(2)}) collective-permute-start(bf16[1280,64]{1,0:T(8,128)(2,1)S(1)} %get-tuple-element.5), channel_id=1, source_target_pairs={{0,1},{1,2},{2,3},{3,4},{4,5},{5,6},{6,7},{7,8},{8,9},{9,10},{10,1... | collective-permute-start | bytes 491528 | tf_op jit(solution)/shard_map/ppermute | solution.py:36
  3.2 9.4 %collective-permute-start.1 = (bf16[1280,64]{1,0:T(8,128)(2,1)S(1)}, bf16[1280,64]{1,0:T(8,128)(2,1)S(1)}, u32[]{:S(2)}, u32[]{:S(2)}) collective-permute-start(bf16[1280,64]{1,0:T(8,128)(2,1)S(1)} %get-tuple-element.6), channel_id=1, source_target_pairs={{1,0},{2,1},{3,2},{4,3},{5,4},{6,5},{7,6},{8,7},{9,8},{10,9},{11,1... | collective-permute-start | bytes 491528 | tf_op jit(solution)/shard_map/ppermute | solution.py:38
  8.0 1.1 copy-start.3
  8.1 4.5 %copy-start = (bf16[1280,128]{1,0:T(8,128)(2,1)S(1)}, bf16[1280,128]{1,0:T(8,128)(2,1)}, u32[]{:S(2)}) copy-start(bf16[1280,128]{1,0:T(8,128)(2,1)} %param.5) | copy-start | bytes 983044

commit v16 on v15

--- a/solution.py
+++ b/solution.py
@@ -323,10 +323,16 @@
     first_mat = first_rows.transpose(2, 0, 1).reshape(n_in, 2 * BANDS * n_mid)
     second_rows = jax.vmap(partial(toeplitz_band, n_out=t_dev, n_in=n_mid))(smooth_taps)
     second_mat = second_rows.transpose(0, 2, 1)
-    widened = extended_2(source, (("tm", 1),), 2 * HALF)
-    wave = jnp.dot(widened, first_mat, preferred_element_type=jnp.float32).reshape(
-        vert_dev, 2, BANDS, n_mid
-    )
+    count = lax.axis_size("tm")
+    width = 2 * HALF
+    before = lax.ppermute(
+        source[:, t_dev - width :], "tm", [(i, i + 1) for i in range(count - 1)]
+    )
+    after = lax.ppermute(source[:, :width], "tm", [(i + 1, i) for i in range(count - 1)])
+    wave = jnp.dot(source, first_mat[width : width + t_dev], preferred_element_type=jnp.float32)
+    wave = wave + jnp.dot(before, first_mat[:width], preferred_element_type=jnp.float32)
+    wave = wave + jnp.dot(after, first_mat[width + t_dev :], preferred_element_type=jnp.float32)
+    wave = wave.reshape(vert_dev, 2, BANDS, n_mid)
     power = (wave[:, 0] * wave[:, 0] + wave[:, 1] * wave[:, 1]).astype(jnp.bfloat16)
     envelope = jnp.einsum(
         "vbu,but->vbt", power, second_mat, preferred_element_type=jnp.float32

time: 116 us -> 117 us (level)
  the two profiles are of different devices: /device:TPU:8 before, /device:TPU:10 now
where the time goes in v16:
time: 117 us; the launch traced here: 116 us
  Pallas kernels  91 us (78%)
  local copies, waits for them, and re-layouts  11.4 us (10%)
  matrix products  6.48 us (6%)
  starting transfers between devices  6.46 us (6%)
    pallas_call x1, Pallas kernels, gather_fold(): pl.pallas_call(partial(gather_fold_kernel, nx, nz, t_dev), out_shape=jax....  51 us
    pallas_call x1, Pallas kernels, reduce_to_owner(): pl.pallas_call(partial(reduce_kernel, nx, nz, n_tm, par_dev), out_shape=j...  40 us
    ppermute x1, starting transfers between devices, local(): lax.ppermute(source[:, :width], 'tm', [(i + 1, i) for i in range(count -...  4.54 us
    dot_general x1, matrix products, local(): jnp.dot(before, first_mat[:width], preferred_element_type=jnp.float32)  2.79 us
    another operation x2, local copies, waits for them, and re-layouts, local(): return coupling[None]  2.65 us
    dot_general x1, matrix products, local(): jnp.dot(source, first_mat[width:width + t_dev], preferred_element_type=jn...  2.53 us
  transfers between devices with their start and end apart: 2, of which 0 were waited for; matrix products, arithmetic and copies ran while one was open for 8% of the time, Pallas kernels for 0%

profile of v16, /device:TPU:10, one launch (start us, length us, event | category | flops | bytes accessed | tf_op | source)
XLA Modules:
  0.0 116.3 jit_solution(9483365611961387302)
XLA Ops:
  0.0 0.0 copy-start
  0.0 1.3 %fusion.21 = (bf16[1280,64]{1,0:T(8,128)(2,1)S(1)}, bf16[1280,64]{1,0:T(8,128)(2,1)S(1)}) fusion(bf16[1280,128]{1,0:T(8,128)(2,1)} %param.5), kind=kLoop, calls=%fused_computation.46 | loop fusion | bytes 655360 | tf_op jit(solution)/shard_map/slice | solution.py:331
  1.3 1.9 %collective-permute-start = (bf16[1280,64]{1,0:T(8,128)(2,1)S(1)}, bf16[1280,64]{1,0:T(8,128)(2,1)S(1)}, u32[]{:S(2)}, u32[]{:S(2)}) collective-permute-start(bf16[1280,64]{1,0:T(8,128)(2,1)S(1)} %get-tuple-element.8), channel_id=1, source_target_pairs={{0,1},{1,2},{2,3},{3,4},{4,5},{5,6},{6,7},{7,8},{8,9},{9,10},{10,1... | collective-permute-start | bytes 491528 | tf_op jit(solution)/shard_map/ppermute | solution.py:328
  3.2 4.5 %collective-permute-start.1 = (bf16[1280,64]{1,0:T(8,128)(2,1)S(1)}, bf16[1280,64]{1,0:T(8,128)(2,1)S(1)}, u32[]{:S(2)}, u32[]{:S(2)}) collective-permute-start(bf16[1280,64]{1,0:T(8,128)(2,1)S(1)} %get-tuple-element.7), channel_id=1, source_target_pairs={{1,0},{2,1},{3,2},{4,3},{5,4},{6,5},{7,6},{8,7},{9,8},{10,9},{11,1... | collective-permute-start | bytes 491528 | tf_op jit(solution)/shard_map/ppermute | solution.py:331
  7.8 0.7 concatenate.13
  8.5 0.0 copy-start.2
  8.5 0.1 tile.20
  8.5 0.0 copy-start.1
  8.6 0.0 copy-start.3
  8.6 0.8 tile.21
  9.4 0.1 slice.77
  9.6 0.1 slice.78
  9.7 0.0 copy-done
  9.7 2.5 %fusion.23 = f32[768,1280]{1,0:T(8,128)} fusion(bf16[128,768]{0,1:T(8,128)(2,1)S(1)} %bitcast.49, bf16[1280,128]{1,0:T(8,128)(2,1)S(1)} %copy-done), kind=kOutput, calls=%fused_computation.48 | convolution fusion | flops 251658240 | bytes 4456448 | tf_op jit(solution)/shard_map/dot_general | solution.py:332
  12.3 0.0 copy-done.2
  12.3 0.4 tile.9
  12.7 0.1 slice.76
  12.8 0.1 reshape.102
  13.0 0.0 copy-done.1
  13.0 0.0 copy-done.3
  13.0 0.1 broadcast_add_fusion
  13.0 0.6 reshape.101.ids_ref
  13.7 0.1 broadcast_in_dim.38
  13.8 0.1 fusion.20
  13.9 0.0 collective-permute-done
  13.9 2.8 %convolution_add_fusion.1 = f32[768,1280]{1,0:T(8,128)S(1)} fusion(f32[768,1280]{1,0:T(8,128)} %fusion.23, bf16[64,768]{0,1:T(8,128)(2,1)S(1)} %bitcast.51, bf16[1280,64]{1,0:T(8,128)(2,1)S(1)} %collective-permute-done), kind=kOutput, calls=%fused_computation.1 | convolution fusion | flops 126812160 | bytes 8126464 | tf_op jit(solution)/shard_map/dot_general | solution.py:333
  16.7 0.0 collective-permute-done.1
  16.8 0.7 convolution_add_fusion
  17.5 0.5 convolution_convert_fusion
  17.9 1.1 copy.52.env_ref
  19.0 40.0 %shard_map.55 = f32[3,96,256]{2,1,0:T(8,128)} custom-call(s32[3,1,1280]{2,1,0:T(1,128)} %reshape.101.ids_ref, bf16[1280,256]{1,0:T(8,128)(2,1)} %copy.52.env_ref), custom_call_target="tpu_custom_call" | custom-call | tf_op jit(solution)/shard_map/pallas_call | solution.py:173
  59.0 0.9 slice.72
  59.9 1.1 reshape.107
  61.0 0.2 fusion.22
  61.2 0.1 squeeze.2
  61.3 0.2 reduce_sum.18
  61.5 0.1 copy.48
  61.6 0.2 fusion.4
  61.7 0.1 slice_bitcast_fusion
  61.8 0.2 multiply_reduce_fusion
  62.1 0.1 copy.49.spread_ref
  62.2 51.0 %shard_map.56 = f32[2,94,1536]{2,1,0:T(8,128)S(1)} custom-call(bf16[2,96,256]{2,1,0:T(8,128)(2,1)S(1)} %pad.14.own_ref, bf16[2,96,256]{2,1,0:T(8,128)(2,1)S(1)} %pad.15.mid_ref, f32[2,96,1]{2,1,0:T(8,128)S(1)} %copy.49.spread_ref, f32[96,1664]{1,0:T(8,128)S(1)} %pad_maximum_fusion.level_ref), custom_call_target="tpu_custom_call" | custom-call | flops 19931332608 | bytes 1376256 | tf_op jit(solution)/shard_map/pallas_call | solution.py:289
  113.2 0.5 reshape.108
  113.7 0.7 broadcast_in_dim_reshape.3
  114.4 1.9 %copy.50 = f32[1,2,94,1504]{3,1,2,0:T(2,128)} copy(f32[1,2,94,1504]{3,2,1,0:T(8,128)S(1)} %broadcast_in_dim_reshape.3) | data formatting | bytes 2262016 | tf_op jit(solution)/shard_map/broadcast_in_dim;reshape | solution.py:375
  (14 shorter events, 0.2 us)
Async XLA Ops:
  0.0 9.7 %copy-start = (bf16[1280,128]{1,0:T(8,128)(2,1)S(1)}, bf16[1280,128]{1,0:T(8,128)(2,1)}, u32[]{:S(2)}) copy-start(bf16[1280,128]{1,0:T(8,128)(2,1)} %param.5) | copy-start | bytes 983044
  1.3 12.6 %collective-permute-start = (bf16[1280,64]{1,0:T(8,128)(2,1)S(1)}, bf16[1280,64]{1,0:T(8,128)(2,1)S(1)}, u32[]{:S(2)}, u32[]{:S(2)}) collective-permute-start(bf16[1280,64]{1,0:T(8,128)(2,1)S(1)} %get-tuple-element.8), channel_id=1, source_target_pairs={{0,1},{1,2},{2,3},{3,4},{4,5},{5,6},{6,7},{7,8},{8,9},{9,10},{10,1... | collective-permute-start | bytes 491528 | tf_op jit(solution)/shard_map/ppermute | solution.py:328
  3.2 13.5 %collective-permute-start.1 = (bf16[1280,64]{1,0:T(8,128)(2,1)S(1)}, bf16[1280,64]{1,0:T(8,128)(2,1)S(1)}, u32[]{:S(2)}, u32[]{:S(2)}) collective-permute-start(bf16[1280,64]{1,0:T(8,128)(2,1)S(1)} %get-tuple-element.7), channel_id=1, source_target_pairs={{1,0},{2,1},{3,2},{4,3},{5,4},{6,5},{7,6},{8,7},{9,8},{10,9},{11,1... | collective-permute-start | bytes 491528 | tf_op jit(solution)/shard_map/ppermute | solution.py:331
  8.5 3.8 %copy-start.2 = (bf16[2,65]{1,0:T(2,128)(2,1)S(1)}, bf16[2,65]{1,0:T(2,128)(2,1)}, u32[]{:S(2)}) copy-start(bf16[2,65]{1,0:T(2,128)(2,1)} %param.7) | copy-start | bytes 784
  8.5 4.4 %copy-start.1 = (s32[3,1280]{1,0:T(4,128)S(1)}, s32[3,1280]{1,0:T(4,128)}, u32[]{:S(2)}) copy-start(s32[3,1280]{1,0:T(4,128)} %param.8) | copy-start | bytes 46084
  8.6 4.4 %copy-start.3 = (s32[3]{0:T(128)S(1)}, s32[3]{0:T(128)}, u32[]{:S(2)}) copy-start(s32[3]{0:T(128)} %constant.69.clone) | copy-start | bytes 40

commit v17 on v15

--- a/solution.py
+++ b/solution.py
@@ -90,9 +90,13 @@
     rows = x_ref.shape[1]
     r = lax.broadcasted_iota(jnp.int32, (rows, 1), 0)
 
-    def pool_groups(first_offset, carry):
+    def pool_groups(first_offset, carry, count=2 * nz, part_of=None):
         def one(j, c):
-            owner = lax.rem(mx + first_offset + 2 * (j // nz), nx) * nz + j % nz
+            if part_of is None:
+                owner = lax.rem(mx + first_offset + 2 * (j // nz), nx) * nz + j % nz
+            else:
+                side = j // hz
+                owner = lax.rem(mx + first_offset + 2 * side, nx) * nz + (part_of + side - 2 * part_of * side) * hz + j % hz
             wanted = jnp.where(r < par_dev, owner * par_dev + r, -1)
             hits = (ids_ref[0] == wanted).astype(jnp.float32)
             for level in range(1, ids_ref.shape[0]):
@@ -102,9 +106,9 @@
             )
             return c
 
-        return lax.fori_loop(0, 2 * nz, one, carry)
-
-    pool_groups(nx - 1, 0)
+        return lax.fori_loop(0, count, one, carry)
+
+    pool_groups(nx - 1, 0, nz, 0)
     peers = (lax.rem(mx + 1, nx), lax.rem(mx + nx - 1, nx))
 
     def owners_of(g, d):
@@ -127,6 +131,7 @@
             copy.start()
             copies.append(copy)
         if s == 1:
+            pool_groups(nx - 1, 0, nz, 1)
             pool_groups(2, 0)
         for copy in copies:
             copy.wait()

time: 116 us -> 115 us (level)
  no operation moved by 1% of the time
where the time goes in v17:
time: 115 us; the launch traced here: 113 us
  Pallas kernels  91.9 us (80%)
  local copies, waits for them, and re-layouts  10.5 us (9%)
  starting transfers between devices  6.46 us (6%)
  waiting for transfers between devices  2.14 us (2%)
  matrix products  1.24 us (1%)
    pallas_call x1, Pallas kernels, gather_fold(): pl.pallas_call(partial(gather_fold_kernel, nx, nz, t_dev), out_shape=jax....  47.6 us
    pallas_call x1, Pallas kernels, reduce_to_owner(): pl.pallas_call(partial(reduce_kernel, nx, nz, n_tm, par_dev), out_shape=j...  44.3 us
    ppermute x1, starting transfers between devices, extended_2(): lax.ppermute(head, axis, [((i + 1) % count, i) for i in range(ends)])  4.54 us
    another operation x2, local copies, waits for them, and re-layouts, local(): return coupling[None]  2.65 us
  transfers between devices with their start and end apart: 2, of which 2 were waited for; matrix products, arithmetic and copies ran while one was open for 2% of the time, Pallas kernels for 0%

profile of v17, /device:TPU:8, one launch (start us, length us, event | category | flops | bytes accessed | tf_op | source)
XLA Modules:
  0.0 113.3 jit_solution(54728240209042853)
XLA Ops:
  0.0 0.0 copy-start.4
  0.0 0.0 copy-start.1
  0.0 0.0 copy-start.2
  0.0 1.3 %fusion.26 = (bf16[1280,64]{1,0:T(8,128)(2,1)S(1)}, bf16[1280,64]{1,0:T(8,128)(2,1)S(1)}) fusion(bf16[1280,128]{1,0:T(8,128)(2,1)} %param.5), kind=kLoop, calls=%fused_computation.50 | loop fusion | bytes 655360 | tf_op jit(solution)/shard_map/slice | solution.py:33
  1.3 1.9 %collective-permute-start = (bf16[1280,64]{1,0:T(8,128)(2,1)S(1)}, bf16[1280,64]{1,0:T(8,128)(2,1)S(1)}, u32[]{:S(2)}, u32[]{:S(2)}) collective-permute-start(bf16[1280,64]{1,0:T(8,128)(2,1)S(1)} %get-tuple-element.5), channel_id=1, source_target_pairs={{0,1},{1,2},{2,3},{3,4},{4,5},{5,6},{6,7},{7,8},{8,9},{9,10},{10,1... | collective-permute-start | bytes 491528 | tf_op jit(solution)/shard_map/ppermute | solution.py:36
  3.2 4.5 %collective-permute-start.1 = (bf16[1280,64]{1,0:T(8,128)(2,1)S(1)}, bf16[1280,64]{1,0:T(8,128)(2,1)S(1)}, u32[]{:S(2)}, u32[]{:S(2)}) collective-permute-start(bf16[1280,64]{1,0:T(8,128)(2,1)S(1)} %get-tuple-element.6), channel_id=1, source_target_pairs={{1,0},{2,1},{3,2},{4,3},{5,4},{6,5},{7,6},{8,7},{9,8},{10,9},{11,1... | collective-permute-start | bytes 491528 | tf_op jit(solution)/shard_map/ppermute | solution.py:38
  7.8 0.1 broadcast_in_dim.38
  7.9 0.0 copy-done.4
  8.0 0.0 copy-done.1
  8.0 0.1 broadcast_add_fusion
  8.0 0.0 copy-done.2
  8.0 0.0 copy-start.3
  8.1 0.1 tile.20
  8.1 0.0 copy-start
  8.1 0.8 tile.21
  9.0 0.1 slice.53
  9.2 0.0 copy-done.3
  9.2 0.4 tile.9
  9.6 0.1 slice.52
  9.7 0.1 reshape.100
  9.9 0.6 reshape.99.ids_ref
  10.5 0.4 collective-permute-done
  10.9 1.7 %collective-permute-done.1 = bf16[1280,64]{1,0:T(8,128)(2,1)S(1)} collective-permute-done((bf16[1280,64]{1,0:T(8,128)(2,1)S(1)}, bf16[1280,64]{1,0:T(8,128)(2,1)S(1)}, u32[]{:S(2)}, u32[]{:S(2)}) %collective-permute-start.1) | collective-permute-done | bytes 163872 | tf_op jit(solution)/shard_map/ppermute | solution.py:38
  12.6 0.0 copy-done
  12.6 0.8 fusion.4
  13.4 0.4 convolution_convert_fusion
  13.9 1.1 copy.53.env_ref
  14.9 44.3 %shard_map.55 = f32[3,96,256]{2,1,0:T(8,128)} custom-call(s32[3,1,1280]{2,1,0:T(1,128)} %reshape.99.ids_ref, bf16[1280,256]{1,0:T(8,128)(2,1)} %copy.53.env_ref), custom_call_target="tpu_custom_call" | custom-call | tf_op jit(solution)/shard_map/pallas_call | solution.py:178
  59.3 0.9 slice.48
  60.2 1.1 reshape.105
  61.3 0.2 fusion.27
  61.4 0.1 squeeze.2
  61.5 0.2 reduce_sum.18
  61.7 0.1 copy.48
  61.8 0.2 fusion.9
  62.0 0.1 slice_bitcast_fusion
  62.1 0.2 multiply_reduce_fusion
  62.3 0.1 copy.49.spread_ref
  62.4 47.6 %shard_map.56 = f32[2,94,1536]{2,1,0:T(8,128)S(1)} custom-call(bf16[2,96,256]{2,1,0:T(8,128)(2,1)S(1)} %pad.14.own_ref, bf16[2,96,256]{2,1,0:T(8,128)(2,1)S(1)} %pad.15.mid_ref, f32[2,96,1]{2,1,0:T(8,128)S(1)} %copy.49.spread_ref, f32[96,1664]{1,0:T(8,128)S(1)} %pad_maximum_fusion.level_ref), custom_call_target="tpu_custom_call" | custom-call | flops 19931332608 | bytes 1376256 | tf_op jit(solution)/shard_map/pallas_call | solution.py:294
  110.1 0.5 reshape.106
  110.6 0.7 broadcast_in_dim_reshape.3
  111.3 1.9 %copy.50 = f32[1,2,94,1504]{3,1,2,0:T(2,128)} copy(f32[1,2,94,1504]{3,2,1,0:T(8,128)S(1)} %broadcast_in_dim_reshape.3) | data formatting | bytes 2262016 | tf_op jit(solution)/shard_map/broadcast_in_dim;reshape | solution.py:374
  (15 shorter events, 0.2 us)
Async XLA Ops:
  0.0 7.9 %copy-start.4 = (s32[3]{0:T(128)S(1)}, s32[3]{0:T(128)}, u32[]{:S(2)}) copy-start(s32[3]{0:T(128)} %constant.69.clone) | copy-start | bytes 40
  0.0 8.0 %copy-start.1 = (s32[3,1280]{1,0:T(4,128)S(1)}, s32[3,1280]{1,0:T(4,128)}, u32[]{:S(2)}) copy-start(s32[3,1280]{1,0:T(4,128)} %param.8) | copy-start | bytes 46084
  0.0 8.0 %copy-start.2 = (bf16[2,2,65]{2,1,0:T(2,128)(2,1)S(1)}, bf16[2,2,65]{2,1,0:T(2,128)(2,1)}, u32[]{:S(2)}) copy-start(bf16[2,2,65]{2,1,0:T(2,128)(2,1)} %param.6) | copy-start | bytes 1564
  1.3 9.6 %collective-permute-start = (bf16[1280,64]{1,0:T(8,128)(2,1)S(1)}, bf16[1280,64]{1,0:T(8,128)(2,1)S(1)}, u32[]{:S(2)}, u32[]{:S(2)}) collective-permute-start(bf16[1280,64]{1,0:T(8,128)(2,1)S(1)} %get-tuple-element.5), channel_id=1, source_target_pairs={{0,1},{1,2},{2,3},{3,4},{4,5},{5,6},{6,7},{7,8},{8,9},{9,10},{10,1... | collective-permute-start | bytes 491528 | tf_op jit(solution)/shard_map/ppermute | solution.py:36
  3.2 9.4 %collective-permute-start.1 = (bf16[1280,64]{1,0:T(8,128)(2,1)S(1)}, bf16[1280,64]{1,0:T(8,128)(2,1)S(1)}, u32[]{:S(2)}, u32[]{:S(2)}) collective-permute-start(bf16[1280,64]{1,0:T(8,128)(2,1)S(1)} %get-tuple-element.6), channel_id=1, source_target_pairs={{1,0},{2,1},{3,2},{4,3},{5,4},{6,5},{7,6},{8,7},{9,8},{10,9},{11,1... | collective-permute-start | bytes 491528 | tf_op jit(solution)/shard_map/ppermute | solution.py:38
  8.0 1.1 copy-start.3
  8.1 4.5 %copy-start = (bf16[1280,128]{1,0:T(8,128)(2,1)S(1)}, bf16[1280,128]{1,0:T(8,128)(2,1)}, u32[]{:S(2)}) copy-start(bf16[1280,128]{1,0:T(8,128)(2,1)} %param.5) | copy-start | bytes 983044

commit v18 on v17

--- a/solution.py
+++ b/solution.py
@@ -20,7 +20,7 @@
 EPSILON = 1e-05
 
 ROW_PAD = 96
-LAG_CHUNKS = 11
+LAG_CHUNKS = 12
 LAG_PAD = 132
 VERT_MINOR = 4
 

time: 115 us -> 115 us (level)
  no operation moved by 1% of the time
where the time goes in v18:
time: 115 us; the launch traced here: 113 us
  Pallas kernels  91.9 us (80%)
  local copies, waits for them, and re-layouts  10.5 us (9%)
  starting transfers between devices  6.46 us (6%)
  waiting for transfers between devices  2.14 us (2%)
  matrix products  1.24 us (1%)
    pallas_call x1, Pallas kernels, gather_fold(): pl.pallas_call(partial(gather_fold_kernel, nx, nz, t_dev), out_shape=jax....  47.6 us
    pallas_call x1, Pallas kernels, reduce_to_owner(): pl.pallas_call(partial(reduce_kernel, nx, nz, n_tm, par_dev), out_shape=j...  44.3 us
    ppermute x1, starting transfers between devices, extended_2(): lax.ppermute(head, axis, [((i + 1) % count, i) for i in range(ends)])  4.54 us
    another operation x2, local copies, waits for them, and re-layouts, local(): return coupling[None]  2.65 us
  transfers between devices with their start and end apart: 2, of which 2 were waited for; matrix products, arithmetic and copies ran while one was open for 2% of the time, Pallas kernels for 0%

profile of v18, /device:TPU:8, one launch (start us, length us, event | category | flops | bytes accessed | tf_op | source)
XLA Modules:
  0.0 113.3 jit_solution(14771379535443162578)
XLA Ops:
  0.0 0.0 copy-start.4
  0.0 0.0 copy-start.1
  0.0 0.0 copy-start.2
  0.0 1.3 %fusion.26 = (bf16[1280,64]{1,0:T(8,128)(2,1)S(1)}, bf16[1280,64]{1,0:T(8,128)(2,1)S(1)}) fusion(bf16[1280,128]{1,0:T(8,128)(2,1)} %param.5), kind=kLoop, calls=%fused_computation.50 | loop fusion | bytes 655360 | tf_op jit(solution)/shard_map/slice | solution.py:33
  1.3 1.9 %collective-permute-start = (bf16[1280,64]{1,0:T(8,128)(2,1)S(1)}, bf16[1280,64]{1,0:T(8,128)(2,1)S(1)}, u32[]{:S(2)}, u32[]{:S(2)}) collective-permute-start(bf16[1280,64]{1,0:T(8,128)(2,1)S(1)} %get-tuple-element.5), channel_id=1, source_target_pairs={{0,1},{1,2},{2,3},{3,4},{4,5},{5,6},{6,7},{7,8},{8,9},{9,10},{10,1... | collective-permute-start | bytes 491528 | tf_op jit(solution)/shard_map/ppermute | solution.py:36
  3.2 4.5 %collective-permute-start.1 = (bf16[1280,64]{1,0:T(8,128)(2,1)S(1)}, bf16[1280,64]{1,0:T(8,128)(2,1)S(1)}, u32[]{:S(2)}, u32[]{:S(2)}) collective-permute-start(bf16[1280,64]{1,0:T(8,128)(2,1)S(1)} %get-tuple-element.6), channel_id=1, source_target_pairs={{1,0},{2,1},{3,2},{4,3},{5,4},{6,5},{7,6},{8,7},{9,8},{10,9},{11,1... | collective-permute-start | bytes 491528 | tf_op jit(solution)/shard_map/ppermute | solution.py:38
  7.8 0.1 broadcast_in_dim.38
  7.9 0.0 copy-done.4
  8.0 0.0 copy-done.1
  8.0 0.1 broadcast_add_fusion
  8.0 0.0 copy-done.2
  8.0 0.0 copy-start.3
  8.1 0.1 tile.20
  8.1 0.0 copy-start
  8.1 0.8 tile.21
  9.0 0.1 slice.53
  9.2 0.0 copy-done.3
  9.2 0.4 tile.9
  9.6 0.1 slice.52
  9.7 0.1 reshape.100
  9.9 0.6 reshape.99.ids_ref
  10.5 0.4 collective-permute-done
  10.9 1.7 %collective-permute-done.1 = bf16[1280,64]{1,0:T(8,128)(2,1)S(1)} collective-permute-done((bf16[1280,64]{1,0:T(8,128)(2,1)S(1)}, bf16[1280,64]{1,0:T(8,128)(2,1)S(1)}, u32[]{:S(2)}, u32[]{:S(2)}) %collective-permute-start.1) | collective-permute-done | bytes 163872 | tf_op jit(solution)/shard_map/ppermute | solution.py:38
  12.6 0.0 copy-done
  12.6 0.8 fusion.4
  13.4 0.4 convolution_convert_fusion
  13.9 1.1 copy.53.env_ref
  14.9 44.3 %shard_map.55 = f32[3,96,256]{2,1,0:T(8,128)} custom-call(s32[3,1,1280]{2,1,0:T(1,128)} %reshape.99.ids_ref, bf16[1280,256]{1,0:T(8,128)(2,1)} %copy.53.env_ref), custom_call_target="tpu_custom_call" | custom-call | tf_op jit(solution)/shard_map/pallas_call | solution.py:178
  59.3 0.9 slice.48
  60.2 1.1 reshape.105
  61.3 0.2 fusion.27
  61.4 0.1 squeeze.2
  61.5 0.2 reduce_sum.18
  61.7 0.1 copy.48
  61.8 0.2 fusion.9
  62.0 0.1 slice_bitcast_fusion
  62.1 0.2 multiply_reduce_fusion
  62.3 0.1 copy.49.spread_ref
  62.4 47.6 %shard_map.56 = f32[2,94,1536]{2,1,0:T(8,128)S(1)} custom-call(bf16[2,96,256]{2,1,0:T(8,128)(2,1)S(1)} %pad.14.own_ref, bf16[2,96,256]{2,1,0:T(8,128)(2,1)S(1)} %pad.15.mid_ref, f32[2,96,1]{2,1,0:T(8,128)S(1)} %copy.49.spread_ref, f32[96,1664]{1,0:T(8,128)S(1)} %pad_maximum_fusion.level_ref), custom_call_target="tpu_custom_call" | custom-call | flops 19931332608 | bytes 1376256 | tf_op jit(solution)/shard_map/pallas_call | solution.py:294
  110.1 0.5 reshape.106
  110.6 0.7 broadcast_in_dim_reshape.3
  111.3 1.9 %copy.50 = f32[1,2,94,1504]{3,1,2,0:T(2,128)} copy(f32[1,2,94,1504]{3,2,1,0:T(8,128)S(1)} %broadcast_in_dim_reshape.3) | data formatting | bytes 2262016 | tf_op jit(solution)/shard_map/broadcast_in_dim;reshape | solution.py:374
  (15 shorter events, 0.2 us)
Async XLA Ops:
  0.0 7.9 %copy-start.4 = (s32[3]{0:T(128)S(1)}, s32[3]{0:T(128)}, u32[]{:S(2)}) copy-start(s32[3]{0:T(128)} %constant.69.clone) | copy-start | bytes 40
  0.0 8.0 %copy-start.1 = (s32[3,1280]{1,0:T(4,128)S(1)}, s32[3,1280]{1,0:T(4,128)}, u32[]{:S(2)}) copy-start(s32[3,1280]{1,0:T(4,128)} %param.8) | copy-start | bytes 46084
  0.0 8.0 %copy-start.2 = (bf16[2,2,65]{2,1,0:T(2,128)(2,1)S(1)}, bf16[2,2,65]{2,1,0:T(2,128)(2,1)}, u32[]{:S(2)}) copy-start(bf16[2,2,65]{2,1,0:T(2,128)(2,1)} %param.6) | copy-start | bytes 1564
  1.3 9.6 %collective-permute-start = (bf16[1280,64]{1,0:T(8,128)(2,1)S(1)}, bf16[1280,64]{1,0:T(8,128)(2,1)S(1)}, u32[]{:S(2)}, u32[]{:S(2)}) collective-permute-start(bf16[1280,64]{1,0:T(8,128)(2,1)S(1)} %get-tuple-element.5), channel_id=1, source_target_pairs={{0,1},{1,2},{2,3},{3,4},{4,5},{5,6},{6,7},{7,8},{8,9},{9,10},{10,1... | collective-permute-start | bytes 491528 | tf_op jit(solution)/shard_map/ppermute | solution.py:36
  3.2 9.4 %collective-permute-start.1 = (bf16[1280,64]{1,0:T(8,128)(2,1)S(1)}, bf16[1280,64]{1,0:T(8,128)(2,1)S(1)}, u32[]{:S(2)}, u32[]{:S(2)}) collective-permute-start(bf16[1280,64]{1,0:T(8,128)(2,1)S(1)} %get-tuple-element.6), channel_id=1, source_target_pairs={{1,0},{2,1},{3,2},{4,3},{5,4},{6,5},{7,6},{8,7},{9,8},{10,9},{11,1... | collective-permute-start | bytes 491528 | tf_op jit(solution)/shard_map/ppermute | solution.py:38
  8.0 1.1 copy-start.3
  8.1 4.5 %copy-start = (bf16[1280,128]{1,0:T(8,128)(2,1)S(1)}, bf16[1280,128]{1,0:T(8,128)(2,1)}, u32[]{:S(2)}) copy-start(bf16[1280,128]{1,0:T(8,128)(2,1)} %param.5) | copy-start | bytes 983044

commit v19 on v18

--- a/solution.py
+++ b/solution.py
@@ -20,7 +20,7 @@
 EPSILON = 1e-05
 
 ROW_PAD = 96
-LAG_CHUNKS = 12
+LAG_CHUNKS = 22
 LAG_PAD = 132
 VERT_MINOR = 4
 

time: 115 us -> 115 us (level)
  no operation moved by 1% of the time
where the time goes in v19:
time: 115 us; the launch traced here: 113 us
  Pallas kernels  91.9 us (80%)
  local copies, waits for them, and re-layouts  10.5 us (9%)
  starting transfers between devices  6.46 us (6%)
  waiting for transfers between devices  2.14 us (2%)
  matrix products  1.24 us (1%)
    pallas_call x1, Pallas kernels, gather_fold(): pl.pallas_call(partial(gather_fold_kernel, nx, nz, t_dev), out_shape=jax....  47.6 us
    pallas_call x1, Pallas kernels, reduce_to_owner(): pl.pallas_call(partial(reduce_kernel, nx, nz, n_tm, par_dev), out_shape=j...  44.3 us
    ppermute x1, starting transfers between devices, extended_2(): lax.ppermute(head, axis, [((i + 1) % count, i) for i in range(ends)])  4.54 us
    another operation x2, local copies, waits for them, and re-layouts, local(): return coupling[None]  2.65 us
  transfers between devices with their start and end apart: 2, of which 2 were waited for; matrix products, arithmetic and copies ran while one was open for 2% of the time, Pallas kernels for 0%

profile of v19, /device:TPU:8, one launch (start us, length us, event | category | flops | bytes accessed | tf_op | source)
XLA Modules:
  0.0 113.3 jit_solution(17347491754432320819)
XLA Ops:
  0.0 0.0 copy-start.4
  0.0 0.0 copy-start.1
  0.0 0.0 copy-start.2
  0.0 1.3 %fusion.26 = (bf16[1280,64]{1,0:T(8,128)(2,1)S(1)}, bf16[1280,64]{1,0:T(8,128)(2,1)S(1)}) fusion(bf16[1280,128]{1,0:T(8,128)(2,1)} %param.5), kind=kLoop, calls=%fused_computation.50 | loop fusion | bytes 655360 | tf_op jit(solution)/shard_map/slice | solution.py:33
  1.3 1.9 %collective-permute-start = (bf16[1280,64]{1,0:T(8,128)(2,1)S(1)}, bf16[1280,64]{1,0:T(8,128)(2,1)S(1)}, u32[]{:S(2)}, u32[]{:S(2)}) collective-permute-start(bf16[1280,64]{1,0:T(8,128)(2,1)S(1)} %get-tuple-element.5), channel_id=1, source_target_pairs={{0,1},{1,2},{2,3},{3,4},{4,5},{5,6},{6,7},{7,8},{8,9},{9,10},{10,1... | collective-permute-start | bytes 491528 | tf_op jit(solution)/shard_map/ppermute | solution.py:36
  3.2 4.5 %collective-permute-start.1 = (bf16[1280,64]{1,0:T(8,128)(2,1)S(1)}, bf16[1280,64]{1,0:T(8,128)(2,1)S(1)}, u32[]{:S(2)}, u32[]{:S(2)}) collective-permute-start(bf16[1280,64]{1,0:T(8,128)(2,1)S(1)} %get-tuple-element.6), channel_id=1, source_target_pairs={{1,0},{2,1},{3,2},{4,3},{5,4},{6,5},{7,6},{8,7},{9,8},{10,9},{11,1... | collective-permute-start | bytes 491528 | tf_op jit(solution)/shard_map/ppermute | solution.py:38
  7.8 0.1 broadcast_in_dim.38
  7.9 0.0 copy-done.4
  8.0 0.0 copy-done.1
  8.0 0.1 broadcast_add_fusion
  8.0 0.0 copy-done.2
  8.0 0.0 copy-start.3
  8.1 0.1 tile.20
  8.1 0.0 copy-start
  8.1 0.8 tile.21
  9.0 0.1 slice.53
  9.2 0.0 copy-done.3
  9.2 0.4 tile.9
  9.6 0.1 slice.52
  9.7 0.1 reshape.100
  9.9 0.6 reshape.99.ids_ref
  10.5 0.4 collective-permute-done
  10.9 1.7 %collective-permute-done.1 = bf16[1280,64]{1,0:T(8,128)(2,1)S(1)} collective-permute-done((bf16[1280,64]{1,0:T(8,128)(2,1)S(1)}, bf16[1280,64]{1,0:T(8,128)(2,1)S(1)}, u32[]{:S(2)}, u32[]{:S(2)}) %collective-permute-start.1) | collective-permute-done | bytes 163872 | tf_op jit(solution)/shard_map/ppermute | solution.py:38
  12.6 0.0 copy-done
  12.6 0.8 fusion.4
  13.4 0.4 convolution_convert_fusion
  13.9 1.1 copy.53.env_ref
  14.9 44.3 %shard_map.55 = f32[3,96,256]{2,1,0:T(8,128)} custom-call(s32[3,1,1280]{2,1,0:T(1,128)} %reshape.99.ids_ref, bf16[1280,256]{1,0:T(8,128)(2,1)} %copy.53.env_ref), custom_call_target="tpu_custom_call" | custom-call | tf_op jit(solution)/shard_map/pallas_call | solution.py:178
  59.3 0.9 slice.48
  60.2 1.1 reshape.105
  61.3 0.2 fusion.27
  61.4 0.1 squeeze.2
  61.5 0.2 reduce_sum.18
  61.7 0.1 copy.48
  61.8 0.2 fusion.9
  62.0 0.1 slice_bitcast_fusion
  62.1 0.2 multiply_reduce_fusion
  62.3 0.1 copy.49.spread_ref
  62.4 47.6 %shard_map.56 = f32[2,94,1536]{2,1,0:T(8,128)S(1)} custom-call(bf16[2,96,256]{2,1,0:T(8,128)(2,1)S(1)} %pad.14.own_ref, bf16[2,96,256]{2,1,0:T(8,128)(2,1)S(1)} %pad.15.mid_ref, f32[2,96,1]{2,1,0:T(8,128)S(1)} %copy.49.spread_ref, f32[96,1664]{1,0:T(8,128)S(1)} %pad_maximum_fusion.level_ref), custom_call_target="tpu_custom_call" | custom-call | flops 19931332608 | bytes 1376256 | tf_op jit(solution)/shard_map/pallas_call | solution.py:294
  110.1 0.5 reshape.106
  110.6 0.7 broadcast_in_dim_reshape.3
  111.3 1.9 %copy.50 = f32[1,2,94,1504]{3,1,2,0:T(2,128)} copy(f32[1,2,94,1504]{3,2,1,0:T(8,128)S(1)} %broadcast_in_dim_reshape.3) | data formatting | bytes 2262016 | tf_op jit(solution)/shard_map/broadcast_in_dim;reshape | solution.py:374
  (15 shorter events, 0.2 us)
Async XLA Ops:
  0.0 7.9 %copy-start.4 = (s32[3]{0:T(128)S(1)}, s32[3]{0:T(128)}, u32[]{:S(2)}) copy-start(s32[3]{0:T(128)} %constant.69.clone) | copy-start | bytes 40
  0.0 8.0 %copy-start.1 = (s32[3,1280]{1,0:T(4,128)S(1)}, s32[3,1280]{1,0:T(4,128)}, u32[]{:S(2)}) copy-start(s32[3,1280]{1,0:T(4,128)} %param.8) | copy-start | bytes 46084
  0.0 8.0 %copy-start.2 = (bf16[2,2,65]{2,1,0:T(2,128)(2,1)S(1)}, bf16[2,2,65]{2,1,0:T(2,128)(2,1)}, u32[]{:S(2)}) copy-start(bf16[2,2,65]{2,1,0:T(2,128)(2,1)} %param.6) | copy-start | bytes 1564
  1.3 9.6 %collective-permute-start = (bf16[1280,64]{1,0:T(8,128)(2,1)S(1)}, bf16[1280,64]{1,0:T(8,128)(2,1)S(1)}, u32[]{:S(2)}, u32[]{:S(2)}) collective-permute-start(bf16[1280,64]{1,0:T(8,128)(2,1)S(1)} %get-tuple-element.5), channel_id=1, source_target_pairs={{0,1},{1,2},{2,3},{3,4},{4,5},{5,6},{6,7},{7,8},{8,9},{9,10},{10,1... | collective-permute-start | bytes 491528 | tf_op jit(solution)/shard_map/ppermute | solution.py:36
  3.2 9.4 %collective-permute-start.1 = (bf16[1280,64]{1,0:T(8,128)(2,1)S(1)}, bf16[1280,64]{1,0:T(8,128)(2,1)S(1)}, u32[]{:S(2)}, u32[]{:S(2)}) collective-permute-start(bf16[1280,64]{1,0:T(8,128)(2,1)S(1)} %get-tuple-element.6), channel_id=1, source_target_pairs={{1,0},{2,1},{3,2},{4,3},{5,4},{6,5},{7,6},{8,7},{9,8},{10,9},{11,1... | collective-permute-start | bytes 491528 | tf_op jit(solution)/shard_map/ppermute | solution.py:38
  8.0 1.1 copy-start.3
  8.1 4.5 %copy-start = (bf16[1280,128]{1,0:T(8,128)(2,1)S(1)}, bf16[1280,128]{1,0:T(8,128)(2,1)}, u32[]{:S(2)}) copy-start(bf16[1280,128]{1,0:T(8,128)(2,1)} %param.5) | copy-start | bytes 983044
